TPU v7x, 256 devices: a whole 4x4x8 slice. The times are simulated.
256 devices in a mesh: sector: 4 (over x_lo, core), tile: 64 (over x_hi, z, y).
Axes of the slice: x: 4 (x_hi: 2, x_lo: 2; x = x_hi * 2 + x_lo), y: 4, z: 8, core: 2. Of those that a mesh axis runs over, the one named last changes fastest.
Arguments:
- snapshots: bfloat16 [4, 245760, 384], P(None, ('sector', 'tile')), may hold values from -6 to 6
- density: float32 [245760], P(('sector', 'tile')), may hold values from 0.5 to 2
- sound_speed: float32 [245760], P(('sector', 'tile')), may hold values from 0.5 to 2
- offsets: int32 [245760], P(('sector', 'tile')), may hold values from -32 to 32
- rotation: bfloat16 [384, 128], P('tile'), may hold values from -0.3125 to 0.3125
Outputs:
- projection: float32 [4, 384, 128], replicated
All inputs are finite; a program needn't handle non-finite values.
Results may differ from a plain program's by a relative error of at most 0.0003.
Values may be sent and summed in bfloat16 or wider, within the bound.
No kernel may reach another device: no remote copies, remote signals or barrier semaphores. Data moves between devices by JAX's collectives and lax.ppermute only.
A program may use at most 64 MiB of HBM per device.

v0:
```python
import math

import jax
import jax.numpy as jnp
from jax import lax
from jax.sharding import PartitionSpec as P

HALO = 32


def padded_2(block, sides, width):
    for axis, dim in sides:
        count = lax.axis_size(axis)
        forward = [(i, i + 1) for i in range(count - 1)]
        forward.append((count - 1, 0))
        backward = [(target, source) for source, target in forward]
        low = lax.ppermute(
            lax.slice_in_dim(block, block.shape[dim] - width, None, axis=dim), axis, forward
        )
        high = lax.ppermute(lax.slice_in_dim(block, 0, width, axis=dim), axis, backward)
        block = jnp.concatenate([low, block, high], axis=dim)
    return block


def weighting(local_cells, near_press, near_sum, density, sound_speed):
    local_wide = local_cells.astype(jnp.float32)
    inverse = 1.0 / (density * sound_speed * sound_speed)
    vel_local = local_wide[1] + local_wide[2] + local_wide[3]
    potential = local_wide[0] * inverse + 0.5 * (near_sum - vel_local) / sound_speed
    kinetic = (
        density[None] * local_wide[1:]
        + 0.5 * (near_press - local_wide[0])[None] / sound_speed[None]
    )
    return jnp.concatenate([potential[None], kinetic], axis=0).astype(jnp.bfloat16)


def with_rims(field, extended):
    return jnp.concatenate(
        [extended[:, :HALO], field, extended[:, extended.shape[1] - HALO :]], axis=1
    )


def edge_rows(field, cell_count):
    return jnp.concatenate([field[:, :HALO], field[:, cell_count - HALO :]], axis=1)


def on_device(snapshots, density, sound_speed, offsets, rotation):
    cell_count = snapshots.shape[1]
    width_snap = snapshots.shape[2]
    neighbor_rows = jnp.arange(cell_count, dtype=jnp.int32) + offsets + HALO
    edges = edge_rows(snapshots, cell_count)
    extended = padded_2(edges, ((("sector", "tile"), 1),), HALO)
    padded = with_rims(snapshots, extended)
    neighbors = jnp.take(padded, neighbor_rows, axis=1).astype(jnp.float32)
    near_press = neighbors[0]
    near_sum = neighbors[1] + neighbors[2] + neighbors[3]
    weighted = weighting(snapshots, near_press, near_sum, density[:, None], sound_speed[:, None])
    full_rotation = lax.all_gather(rotation, "tile", axis=0, tiled=True)
    mode_count = full_rotation.shape[1]
    mode_fields = jnp.dot(
        snapshots.reshape(4 * cell_count, width_snap),
        full_rotation,
        preferred_element_type=jnp.float32,
    )
    mode_fields = mode_fields.astype(jnp.bfloat16).reshape(4, cell_count, mode_count)
    parts = [
        jnp.dot(weighted[component].T, mode_fields[component], preferred_element_type=jnp.float32)
        for component in range(4)
    ]
    partial_sum = jnp.stack(parts, axis=0)
    summed = lax.psum(partial_sum, ("sector", "tile"))
    cell_total = cell_count * lax.axis_size("sector") * lax.axis_size("tile")
    return summed / math.sqrt(cell_total)


def solution(mesh):
    return jax.shard_map(
        on_device,
        mesh=mesh,
        in_specs=(
            P(None, ("sector", "tile"), None),
            P(("sector", "tile")),
            P(("sector", "tile")),
            P(("sector", "tile")),
            P("tile", None),
        ),
        out_specs=P(),
        check_vma=False,
    )
```

profile of v0, /device:TPU:1, one launch (start us, length us, event | category | flops | bytes accessed | tf_op | source)
XLA Modules:
  0.0 502.8 jit_solution(18045077108584224494)
XLA Ops:
  6.5 0.0 copy-start.6
  6.5 0.0 copy-start.7
  6.5 0.0 copy-start.5
  6.5 0.0 copy-start.4
  6.5 0.0 all-reduce.2.cloned.1.call-start
  6.6 0.0 copy-start
  6.6 7.5 %fusion.21 = (bf16[4,960,384]{2,0,1:T(4,128)(2,1)S(1)}, f32[4,960,384]{2,0,1:T(4,128)}) fusion(bf16[4,960,384]{2,1,0:T(8,128)(2,1)} %param.5), kind=kLoop, calls=%fused_computation.44 | loop fusion | flops 1474560 | bytes 11796480 | tf_op args[0]
  14.1 0.0 copy-start.1
  14.1 1.6 copy-done.1
  15.8 0.1 fusion.20
  15.9 2.2 collective-permute-start
  18.1 9.8 %collective-permute-start.1 = (bf16[4,32,384]{2,0,1:T(4,128)(2,1)S(1)}, bf16[4,32,384]{2,0,1:T(4,128)(2,1)}, u32[]{:S(2)}, u32[]{:S(2)}) collective-permute-start(bf16[4,32,384]{2,0,1:T(4,128)(2,1)S(1)} %get-tuple-element.11), channel_id=1, source_target_pairs={{1,0},{2,1},{3,2},{4,3},{5,4},{6,5},{7,6},{8,7},{9,8},{10,9},{11,1... | collective-permute-start | bytes 294920 | tf_op jit(solution)/shard_map/ppermute | solution.py:20
  27.9 0.0 copy-done.6
  27.9 0.0 copy-done.7
  27.9 148.4 %all-gather = bf16[64,6,128]{2,1,0:T(8,128)(2,1)S(1)} all-gather(bf16[1,6,128]{2,1,0:T(8,128)(2,1)S(1)} %bitcast.33), channel_id=1, replica_groups=mesh['sector'=4,'tile'=64] {'tile'}, dimensions={0}, use_global_device_ids=true | all-gather | bytes 99840 | tf_op jit(solution)/shard_map/all_gather | solution.py:58
  176.4 0.0 copy-done.5
  176.4 0.0 copy-done.4
  176.4 0.0 copy-done
  176.4 0.0 copy-start.2
  176.5 1.9 convolution_convert_fusion
  178.4 0.0 collective-permute-done
  178.4 0.0 collective-permute-done.1
  178.4 0.0 copy-done.2
  178.4 4.4 pad_maximum_fusion
  182.8 0.0 slice-start
  182.8 11.9 %gather_fusion = bf16[960,4,384]{2,1,0:T(4,128)(2,1)} fusion(bf16[4,1024,384]{2,0,1:T(4,128)(2,1)} %pad_maximum_fusion, s32[1024]{0:T(1024)S(1)} %pad_clamp_fusion), kind=kCustom, calls=%fused_computation | custom fusion | bytes 5902080 | tf_op jit(solution)/shard_map/jit(_take)/gather | solution.py:54
  194.7 0.0 slice-start.1
  194.8 5.0 convert_bitcast_fusion
  199.7 0.0 slice-done
  199.7 0.0 slice-done.1
  199.8 12.0 %fusion.5 = (bf16[1,960,384]{2,0,1:T(2,128)(2,1)S(1)}, f32[1,960,384]{2,0,1:T(1,128)S(1)}) fusion(f32[4,960,384]{2,0,1:T(4,128)S(1)} %bitcast.30, f32[4,960,384]{2,0,1:T(4,128)S(1)} %convert_bitcast_fusion, f32[960]{0:T(1024)S(1)} %fusion.18, f32[960]{0:T(1024)S(1)} %copy-done.4), kind=kLoop, calls=%fused_computation.17 | loop fusion | flops 4792320 | bytes 14016000 | tf_op jit(solution)/shard_map/slice | solution.py:67
  211.7 0.1 copy.42
  211.9 3.5 fusion.1
  215.4 0.0 copy-start.3
  215.4 3.2 fusion.19
  218.6 0.0 copy-done.3
  218.6 0.4 convolution_bitcast_fusion
  219.0 0.4 convolution_bitcast_fusion.1
  219.4 0.4 convolution_bitcast_fusion.2
  219.9 0.4 convolution_bitcast_fusion.3
  220.3 0.9 pad_maximum_fusion.1
  221.2 0.0 all-reduce.2.cloned.1.call-update
  221.2 272.6 %all-reduce.2.cloned.1.call-done = f32[4,384,128]{2,1,0:T(8,128)} async-done(((f32[4,384,128]{2,1,0:T(8,128)}), f32[4,384,128]{2,1,0:T(8,128)}) %all-reduce.2.cloned.1.call-update) | async-done | bytes 786448 | tf_op jit(solution)/shard_map/psum | solution.py:71
  493.9 2.1 broadcast_multiply_fusion
  (6 shorter events, 0.1 us)
Async XLA Ops:
  6.5 21.4 %copy-start.6 = (s32[960]{0:T(1024)S(1)}, s32[960]{0:T(1024)}, u32[]{:S(2)}) copy-start(s32[960]{0:T(1024)} %param.8) | copy-start | bytes 11524
  6.5 21.4 %copy-start.7 = (bf16[6,128]{1,0:T(8,128)(2,1)S(1)}, bf16[6,128]{1,0:T(8,128)(2,1)}, u32[]{:S(2)}) copy-start(bf16[6,128]{1,0:T(8,128)(2,1)} %param.9) | copy-start | bytes 4612
  6.5 169.9 %copy-start.5 = (f32[960]{0:T(1024)S(1)}, f32[960]{0:T(1024)}, u32[]{:S(2)}) copy-start(f32[960]{0:T(1024)} %param.6) | copy-start | bytes 11524
  6.5 169.9 %copy-start.4 = (f32[960]{0:T(1024)S(1)}, f32[960]{0:T(1024)}, u32[]{:S(2)}) copy-start(f32[960]{0:T(1024)} %param.7) | copy-start | bytes 11524
  6.5 487.3 %all-reduce.2.cloned.1.call-start = ((), (), s32[]{:S(2)}) async-start(), calls=%async_computation | async-start | bytes 1572864 | tf_op jit(solution)/shard_map/psum | solution.py:71
  6.6 169.9 %copy-start = (bf16[4,960,384]{2,1,0:T(8,128)(2,1)S(1)}, bf16[4,960,384]{2,1,0:T(8,128)(2,1)}, u32[]{:S(2)}) copy-start(bf16[4,960,384]{2,1,0:T(8,128)(2,1)} %param.5) | copy-start | bytes 8847364
  14.1 1.6 copy-start.1
  15.9 162.5 %collective-permute-start = (bf16[4,32,384]{2,0,1:T(4,128)(2,1)S(1)}, bf16[4,32,384]{2,0,1:T(4,128)(2,1)S(1)}, u32[]{:S(2)}, u32[]{:S(2)}) collective-permute-start(bf16[4,32,384]{2,0,1:T(4,128)(2,1)S(1)} %get-tuple-element.10), channel_id=1, source_target_pairs={{0,1},{1,2},{2,3},{3,4},{4,5},{5,6},{6,7},{7,8},{8,9},{9,10},{10,1... | collective-permute-start | bytes 294920 | tf_op jit(solution)/shard_map/ppermute | solution.py:17
  18.1 160.3 %collective-permute-start.1 = (bf16[4,32,384]{2,0,1:T(4,128)(2,1)S(1)}, bf16[4,32,384]{2,0,1:T(4,128)(2,1)}, u32[]{:S(2)}, u32[]{:S(2)}) collective-permute-start(bf16[4,32,384]{2,0,1:T(4,128)(2,1)S(1)} %get-tuple-element.11), channel_id=1, source_target_pairs={{1,0},{2,1},{3,2},{4,3},{5,4},{6,5},{7,6},{8,7},{9,8},{10,9},{11,1... | collective-permute-start | bytes 294920 | tf_op jit(solution)/shard_map/ppermute | solution.py:20
  176.4 2.0 copy-start.2
  182.8 16.9 %slice-start = ((s8[5898240]{0:T(1024)(128)(4,1)}), s8[1703936]{0:T(1024)(128)(4,1)S(1)}, s32[]{:S(2)}) async-start(s8[5898240]{0:T(1024)(128)(4,1)} %bitcast.29), calls=%async_computation.1 | async-start | bytes 3407872
  194.7 5.0 slice-start.1
  215.4 3.2 copy-start.3
Sparse Core Ops, SparseCore 0:
  221.4 272.4 all-reduce.1
where the time goes:
time: 504 us; the launch traced here: 503 us
  waiting for transfers between devices  273 us (54%)
  blocking collectives  148 us (29%)
  other arithmetic  35.5 us (7%)
  local copies, waits for them, and re-layouts  17 us (3%)
  between operations  13.6 us (3%)
  starting transfers between devices  12.1 us (2%)
    psum x1, waiting for transfers between devices, on_device(): summed = lax.psum(partial_sum, ('sector', 'tile'))  273 us
    all_gather x1, blocking collectives, on_device(): full_rotation = lax.all_gather(rotation, 'tile', axis=0, tiled=True)  148 us
    slice x1, other arithmetic, on_device(): weighted[component]  12 us
    gather x1, local copies, waits for them, and re-layouts, on_device(): neighbors = jnp.take(padded, neighbor_rows, axis=1).astype(jnp.float32)  11.9 us
  transfers between devices with their start and end apart: 3, of which 1 were waited for; matrix products, arithmetic and copies ran while one was open for 0% of the time, Pallas kernels for 0%

commit v1 on v0

v1 whole, which is shorter than its diff:
```python
import math

import jax
import jax.numpy as jnp
from jax import lax
from jax.experimental import pallas as pl
from jax.experimental.pallas import tpu as pltpu
from jax.sharding import Mesh, PartitionSpec as P

HALO = 32
COMPONENTS = 4
BLOCK = 192
TILE_AXES = ("x_hi", "z", "y")
PLANE_AXES = ("x_lo", "core", "x_hi", "y")
CELL_AXES = ("x_lo", "core", "x_hi", "z", "y")


def project_kernel(snap, low, high, dens, speed, offs, rot, out, rows_ref, weighted):
    cells = snap.shape[1]
    density = dens[...]
    sound = speed[...]
    rows_ref[...] = jnp.zeros_like(rows_ref)
    rows_ref[0:1, 0:cells] = density
    rows_ref[1:2, 0:cells] = 1.0 / (density * sound * sound)
    rows_ref[2:3, 0:cells] = 0.5 / sound
    rows_ref[3:4, 0:cells] = offs[...].astype(jnp.float32)
    columns = rows_ref[...].T
    rotation_t = rot[...].T
    window = BLOCK + 2 * HALO
    row_at = lax.broadcasted_iota(jnp.int32, (BLOCK, window), 0) + HALO
    col_at = lax.broadcasted_iota(jnp.int32, (BLOCK, window), 1)
    here = (col_at == row_at).astype(jnp.float32)
    modes = [[] for _ in range(COMPONENTS)]
    for start in range(0, cells, BLOCK):
        stop = start + BLOCK
        scale = columns[start:stop]
        rho, inverse, half = scale[:, 0:1], scale[:, 1:2], scale[:, 2:3]
        shift = scale[:, 3:4].astype(jnp.int32)
        there = (col_at == row_at + shift).astype(jnp.float32)
        stencil = (there - here).astype(jnp.bfloat16)

        def around(component):
            parts = []
            if start == 0:
                parts.append(low[component])
            parts.append(snap[component, max(start - HALO, 0) : min(stop + HALO, cells)])
            if stop == cells:
                parts.append(high[component])
            return parts[0] if len(parts) == 1 else jnp.concatenate(parts, axis=0)

        def difference(component):
            return jnp.dot(stencil, around(component), preferred_element_type=jnp.float32)

        press_part = half * difference(0)
        sum_part = half * ((difference(1) + difference(2)) + difference(3))
        for component in range(COMPONENTS):
            block = snap[component, start:stop]
            wide = block.astype(jnp.float32)
            if component == 0:
                value = wide * inverse + sum_part
            else:
                value = rho * wide + press_part
            weighted[component, start:stop] = value.astype(jnp.bfloat16)
            mode = lax.dot_general(
                rotation_t, block, (((1,), (1,)), ((), ())), preferred_element_type=jnp.float32
            )
            modes[component].append(mode.astype(jnp.bfloat16))
    for component in range(COMPONENTS):
        mode_t = jnp.concatenate(modes[component], axis=1)
        total = jnp.dot(mode_t, weighted[component], preferred_element_type=jnp.float32)
        out[component] = total.T


def local_projection(snapshots, low, high, density, sound_speed, offsets, rotation):
    components, cells, width = snapshots.shape
    modes = rotation.shape[1]
    return pl.pallas_call(
        project_kernel,
        out_shape=jax.ShapeDtypeStruct((components, width, modes), jnp.float32),
        in_specs=[pl.BlockSpec(memory_space=pltpu.VMEM)] * 7,
        out_specs=pl.BlockSpec(memory_space=pltpu.VMEM),
        scratch_shapes=[
            pltpu.VMEM((8, 1024), jnp.float32),
            pltpu.VMEM((components, cells, width), jnp.bfloat16),
        ],
        compiler_params=pltpu.CompilerParams(vmem_limit_bytes=40 << 20),
        cost_estimate=pl.CostEstimate(flops=2_000_000_000, bytes_accessed=6_000_000, transcendentals=0),
    )(
        snapshots,
        low,
        high,
        density.reshape(1, cells),
        sound_speed.reshape(1, cells),
        offsets.reshape(1, cells),
        rotation,
    )


def spread(block, axes):
    count = lax.axis_size(axes)
    return lax.all_to_all(jnp.broadcast_to(block[None], (count,) + block.shape), axes, 0, 0)


def on_device(snapshots, density, sound_speed, offsets, rotation):
    components, cells, width = snapshots.shape
    count = lax.axis_size(CELL_AXES)
    forward = [(i, (i + 1) % count) for i in range(count)]
    backward = [(i, (i - 1) % count) for i in range(count)]
    with jax.named_scope("halo"):
        low = lax.ppermute(snapshots[:, cells - HALO :], CELL_AXES, forward)
        high = lax.ppermute(snapshots[:, :HALO], CELL_AXES, backward)
    with jax.named_scope("rotation_rows"):
        full_rotation = spread(rotation, TILE_AXES).reshape(width, rotation.shape[1])
    with jax.named_scope("local_projection"):
        partial = local_projection(
            snapshots, low, high, density, sound_speed, offsets, full_rotation
        )
    modes = partial.shape[2]
    members = lax.axis_size(PLANE_AXES)
    with jax.named_scope("sum_plane"):
        pieces = partial.reshape(members, components * width // members, modes)
        piece = jnp.sum(lax.all_to_all(pieces, PLANE_AXES, 0, 0), axis=0)
    with jax.named_scope("sum_z"):
        piece = jnp.sum(spread(piece, ("z",)), axis=0)
        piece = piece * (1.0 / math.sqrt(cells * count))
    with jax.named_scope("share_plane"):
        whole = spread(piece, PLANE_AXES)
    return whole.reshape(components, width, modes)


def solution(mesh):
    fine = Mesh(mesh.devices.reshape(2, 2, 2, 8, 4), CELL_AXES)
    return jax.shard_map(
        on_device,
        mesh=fine,
        in_specs=(
            P(None, CELL_AXES, None),
            P(CELL_AXES),
            P(CELL_AXES),
            P(CELL_AXES),
            P(TILE_AXES, None),
        ),
        out_specs=P(),
        check_vma=False,
    )
```

time: 504 us -> 91.4 us (0.18)
  waiting for transfers between devices: 273 us -> 9.71 us
  blocking collectives: 148 us -> 46.7 us
  other arithmetic: 35.5 us -> 0.08 us
  between operations: 13.6 us -> 0.06 us
  starting transfers between devices: 12.1 us -> 23.4 us
  local copies, waits for them, and re-layouts: 17 us -> 7.2 us
    psum x1 -> x0, waiting for transfers between devices: 273 us -> none  [on_device(): summed = lax.psum(partial_sum, ('sector', 'tile'))]
    all_gather x1 -> x0, blocking collectives: 148 us -> none  [on_device(): full_rotation = lax.all_gather(rotation, 'tile', axis=0, tiled=True)]
    all_to_all x0 -> x3, blocking collectives: none -> 46.7 us  [the longest x2 31.1 us: spread(): lax.all_to_all(jnp.broadcast_to(block[None], (count,) + block.shape), axe...]
    all_to_all x0 -> x1, starting transfers between devices: none -> 15.1 us  [spread(): lax.all_to_all(jnp.broadcast_to(block[None], (count,) + block.shape), axe...]
    slice x1 -> x0, other arithmetic: 12 us -> none  [on_device(): weighted[component]]
    gather x1 -> x0, local copies, waits for them, and re-layouts: 11.9 us -> none  [on_device(): neighbors = jnp.take(padded, neighbor_rows, axis=1).astype(jnp.float32)]
    unnamed x2 -> x0, other arithmetic: 7.55 us -> none
    ppermute x2, waiting for transfers between devices: 0.01 us -> 7.41 us  [the longest x1 7.41 us: on_device(): low = lax.ppermute(snapshots[:, cells - HALO:], CELL_AXES, forward)]
  transfers between devices with their start and end apart: 3 -> 3, of which waited for: 1 -> 2; matrix products, arithmetic and copies ran while one was open for 0% -> 1% of each run, Pallas kernels for 0% -> 0%
where the time goes in v1:
time: 91.4 us; the launch traced here: 91 us
  blocking collectives  46.7 us (51%)
  starting transfers between devices  23.4 us (26%)
  waiting for transfers between devices  9.71 us (11%)
  local copies, waits for them, and re-layouts  7.2 us (8%)
  Pallas kernels  3.89 us (4%)
    all_to_all x2, blocking collectives, spread(): lax.all_to_all(jnp.broadcast_to(block[None], (count,) + block.shape), axe...  31.1 us
    all_to_all x1, blocking collectives, on_device(): piece = jnp.sum(lax.all_to_all(pieces, PLANE_AXES, 0, 0), axis=0)  15.6 us
    all_to_all x1, starting transfers between devices, spread(): lax.all_to_all(jnp.broadcast_to(block[None], (count,) + block.shape), axe...  15.1 us
    ppermute x1, starting transfers between devices, on_device(): high = lax.ppermute(snapshots[:, :HALO], CELL_AXES, backward)  8.24 us
    ppermute x1, waiting for transfers between devices, on_device(): low = lax.ppermute(snapshots[:, cells - HALO:], CELL_AXES, forward)  7.41 us
    unnamed x9, local copies, waits for them, and re-layouts  4.77 us
    pallas_call x1, Pallas kernels, local_projection(): pl.pallas_call(project_kernel, out_shape=jax.ShapeDtypeStruct((components...  3.89 us
    all_to_all x1, waiting for transfers between devices, spread(): lax.all_to_all(jnp.broadcast_to(block[None], (count,) + block.shape), axe...  2.3 us
  transfers between devices with their start and end apart: 3, of which 2 were waited for; matrix products, arithmetic and copies ran while one was open for 1% of the time, Pallas kernels for 0%

profile of v1, /device:TPU:1, one launch (start us, length us, event | category | flops | bytes accessed | tf_op | source)
XLA Modules:
  0.0 91.0 jit_solution(4259538297596254524)
XLA Ops:
  0.0 1.4 %broadcast_in_dim.6 = bf16[64,6,128]{2,1,0:T(8,128)(2,1)} broadcast(bf16[6,128]{1,0:T(8,128)(2,1)} %param.9), dimensions={1,2} | broadcast | bytes 99840 | tf_op jit(solution)/shard_map/rotation_rows/broadcast_in_dim | solution.py:101
  1.4 15.1 %all-to-all-start = ((bf16[64,6,128]{2,1,0:T(8,128)(2,1)}), bf16[64,6,128]{2,1,0:T(8,128)(2,1)S(1)}, u32[]{:S(2)}, u32[]{:S(2)}) async-start(bf16[64,6,128]{2,1,0:T(8,128)(2,1)} %broadcast_in_dim.6), calls=%async_computation | async-start | bytes 262144 | tf_op jit(solution)/shard_map/rotation_rows/all_to_all | solution.py:101
  16.5 1.0 %fusion = (bf16[4,32,384]{2,1,0:T(8,128)(2,1)S(1)}, bf16[4,32,384]{2,1,0:T(8,128)(2,1)S(1)}) fusion(bf16[4,960,384]{2,1,0:T(8,128)(2,1)} %snap.1), kind=kLoop, calls=%fused_computation.1 | loop fusion | bytes 393216 | tf_op jit(solution)/shard_map/halo/slice | solution.py:111
  17.4 8.2 %collective-permute-start.1 = (bf16[4,32,384]{2,1,0:T(8,128)(2,1)S(1)}, bf16[4,32,384]{2,1,0:T(8,128)(2,1)S(1)}, u32[]{:S(2)}, u32[]{:S(2)}) collective-permute-start(bf16[4,32,384]{2,1,0:T(8,128)(2,1)S(1)} %get-tuple-element.5), channel_id=1, source_target_pairs={{0,255},{1,0},{2,1},{3,2},{4,3},{5,4},{6,5},{7,6},{8,7},{9,8},{10,... | collective-permute-start | bytes 294920 | tf_op jit(solution)/shard_map/halo/ppermute | solution.py:111
  25.7 0.0 collective-permute-start
  25.7 2.3 %all-to-all-done = bf16[64,6,128]{2,1,0:T(8,128)(2,1)S(1)} async-done(((bf16[64,6,128]{2,1,0:T(8,128)(2,1)}), bf16[64,6,128]{2,1,0:T(8,128)(2,1)S(1)}, u32[]{:S(2)}, u32[]{:S(2)}) %all-to-all-start) | async-done | bytes 98336 | tf_op jit(solution)/shard_map/rotation_rows/all_to_all | solution.py:101
  28.0 0.0 collective-permute-done.1.high
  28.0 7.4 %collective-permute-done.low = bf16[4,32,384]{2,1,0:T(8,128)(2,1)S(1)} collective-permute-done((bf16[4,32,384]{2,1,0:T(8,128)(2,1)S(1)}, bf16[4,32,384]{2,1,0:T(8,128)(2,1)S(1)}, u32[]{:S(2)}, u32[]{:S(2)}) %collective-permute-start) | collective-permute-done | bytes 98336 | tf_op jit(solution)/shard_map/halo/ppermute | solution.py:110
  35.5 0.0 copy-start
  35.5 1.8 %copy-done = bf16[4,960,384]{2,1,0:T(8,128)(2,1)S(1)} copy-done((bf16[4,960,384]{2,1,0:T(8,128)(2,1)S(1)}, bf16[4,960,384]{2,1,0:T(8,128)(2,1)}, u32[]{:S(2)}) %copy-start) | copy-done | bytes 2949144
  37.3 0.0 copy-start.1
  37.3 0.7 copy-done.1
  38.0 0.0 copy-start.2
  38.0 0.7 copy-done.2
  38.7 0.0 copy-start.3
  38.7 0.7 copy-done.3
  39.4 3.9 %local_projection.1 = f32[4,384,128]{2,1,0:T(8,128)S(1)} custom-call(bf16[4,960,384]{2,1,0:T(8,128)(2,1)S(1)} %copy-done, bf16[4,32,384]{2,1,0:T(8,128)(2,1)S(1)} %collective-permute-done.low, bf16[4,32,384]{2,1,0:T(8,128)(2,1)S(1)} %collective-permute-done.1.high, f32[1,960]{1,0:T(1,128)S(1)} %bitcast.6, f32[1,960]{1,0:T(1,128)S(1)} %bitcast.7, ...), custom_call_target="tpu_custom_call" | custom-call | flops 2000000000 | bytes 6000000 | tf_op jit(solution)/shard_map/local_projection/pallas_call | solution.py:77
  43.2 15.6 %all_to_all.20 = f32[32,48,128]{2,1,0:T(8,128)S(1)} all-to-all(f32[32,48,128]{2,1,0:T(8,128)S(1)} %bitcast.5), channel_id=1, replica_groups=mesh['x_lo'=2,'core'=2,'x_hi'=2,'z'=8,'y'=4] {'x_lo','core','x_hi','y'}, dimensions={0} | all-to-all | bytes 1572864 | tf_op jit(solution)/shard_map/sum_plane/all_to_all | solution.py:122
  58.8 0.1 reduce_sum.18
  58.9 11.1 %all_to_all.21 = f32[8,48,128]{2,1,0:T(8,128)S(1)} all-to-all(f32[8,48,128]{2,1,0:T(8,128)S(1)} %broadcast_in_dim.7), channel_id=1, replica_groups=mesh['x_lo'=2,'core'=2,'x_hi'=2,'z'=8,'y'=4] {'z'}, dimensions={0} | all-to-all | bytes 393216 | tf_op jit(solution)/shard_map/sum_z/all_to_all | solution.py:101
  70.1 0.1 broadcast_in_dim.8
  70.1 19.9 %all_to_all.22 = f32[32,48,128]{2,1,0:T(8,128)S(1)} all-to-all(f32[32,48,128]{2,1,0:T(8,128)S(1)} %broadcast_in_dim.8), channel_id=1, replica_groups=mesh['x_lo'=2,'core'=2,'x_hi'=2,'z'=8,'y'=4] {'x_lo','core','x_hi','y'}, dimensions={0} | all-to-all | bytes 1572864 | tf_op jit(solution)/shard_map/share_plane/all_to_all | solution.py:101
  90.1 0.9 copy.7
  (4 shorter events, 0.1 us)
Async XLA Ops:
  1.4 26.6 %all-to-all-start = ((bf16[64,6,128]{2,1,0:T(8,128)(2,1)}), bf16[64,6,128]{2,1,0:T(8,128)(2,1)S(1)}, u32[]{:S(2)}, u32[]{:S(2)}) async-start(bf16[64,6,128]{2,1,0:T(8,128)(2,1)} %broadcast_in_dim.6), calls=%async_computation | async-start | bytes 262144 | tf_op jit(solution)/shard_map/rotation_rows/all_to_all | solution.py:101
  17.4 10.6 %collective-permute-start.1 = (bf16[4,32,384]{2,1,0:T(8,128)(2,1)S(1)}, bf16[4,32,384]{2,1,0:T(8,128)(2,1)S(1)}, u32[]{:S(2)}, u32[]{:S(2)}) collective-permute-start(bf16[4,32,384]{2,1,0:T(8,128)(2,1)S(1)} %get-tuple-element.5), channel_id=1, source_target_pairs={{0,255},{1,0},{2,1},{3,2},{4,3},{5,4},{6,5},{7,6},{8,7},{9,8},{10,... | collective-permute-start | bytes 294920 | tf_op jit(solution)/shard_map/halo/ppermute | solution.py:111
  25.7 9.8 %collective-permute-start = (bf16[4,32,384]{2,1,0:T(8,128)(2,1)S(1)}, bf16[4,32,384]{2,1,0:T(8,128)(2,1)S(1)}, u32[]{:S(2)}, u32[]{:S(2)}) collective-permute-start(bf16[4,32,384]{2,1,0:T(8,128)(2,1)S(1)} %get-tuple-element.6), channel_id=1, source_target_pairs={{0,1},{1,2},{2,3},{3,4},{4,5},{5,6},{6,7},{7,8},{8,9},{9,10},{10,1... | collective-permute-start | bytes 294920 | tf_op jit(solution)/shard_map/halo/ppermute | solution.py:110
  35.5 1.8 %copy-start = (bf16[4,960,384]{2,1,0:T(8,128)(2,1)S(1)}, bf16[4,960,384]{2,1,0:T(8,128)(2,1)}, u32[]{:S(2)}) copy-start(bf16[4,960,384]{2,1,0:T(8,128)(2,1)} %snap.1) | copy-start | bytes 8847364
  37.3 0.7 copy-start.1
  38.0 0.7 copy-start.2
  38.7 0.7 copy-start.3

commit v2 on v1

v2 whole, which is shorter than its diff:
```python
import math

import jax
import jax.numpy as jnp
from jax import lax
from jax.experimental import pallas as pl
from jax.experimental.pallas import tpu as pltpu
from jax.sharding import Mesh, PartitionSpec as P

HALO = 32
COMPONENTS = 4
BLOCK = 192
TILE_AXES = ("x_hi", "z", "y")
PLANE_AXES = ("x_lo", "x_hi", "y")
CELL_AXES = ("x_lo", "core", "x_hi", "z", "y")
VMEM = pl.BlockSpec(memory_space=pltpu.VMEM)
HBM = pl.BlockSpec(memory_space=pltpu.HBM)
PARAMS = pltpu.CompilerParams(vmem_limit_bytes=12 << 20)


def in_hbm(array):
    return pltpu.with_memory_space_constraint(array, pltpu.HBM)


def weighting_kernel(
    snap_hbm, low, high, dens_hbm, speed_hbm, offs_hbm, weighted, snap, dens, speed, offs, rows_ref, sems
):
    cells = snap.shape[1]
    vectors = ((dens_hbm, dens), (speed_hbm, speed), (offs_hbm, offs))
    small = [
        pltpu.make_async_copy(source, target, sems.at[COMPONENTS + i])
        for i, (source, target) in enumerate(vectors)
    ]
    copies = [
        pltpu.make_async_copy(snap_hbm.at[component], snap.at[component], sems.at[component])
        for component in range(COMPONENTS)
    ]
    for copy in small + copies:
        copy.start()
    for copy in small:
        copy.wait()
    density = dens[...]
    sound = speed[...]
    rows_ref[...] = jnp.zeros_like(rows_ref)
    rows_ref[0:1, 0:cells] = density
    rows_ref[1:2, 0:cells] = 1.0 / (density * sound * sound)
    rows_ref[2:3, 0:cells] = 0.5 / sound
    rows_ref[3:4, 0:cells] = offs[...].astype(jnp.float32)
    columns = rows_ref[...].T
    window = BLOCK + 2 * HALO
    row_at = lax.broadcasted_iota(jnp.int32, (BLOCK, window), 0) + HALO
    col_at = lax.broadcasted_iota(jnp.int32, (BLOCK, window), 1)
    here = (col_at == row_at).astype(jnp.float32)
    for copy in copies:
        copy.wait()
    for start in range(0, cells, BLOCK):
        stop = start + BLOCK
        scale = columns[start:stop]
        rho, inverse, half = scale[:, 0:1], scale[:, 1:2], scale[:, 2:3]
        shift = scale[:, 3:4].astype(jnp.int32)
        there = (col_at == row_at + shift).astype(jnp.float32)
        stencil = (there - here).astype(jnp.bfloat16)

        def around(component):
            parts = []
            if start == 0:
                parts.append(low[component])
            parts.append(snap[component, max(start - HALO, 0) : min(stop + HALO, cells)])
            if stop == cells:
                parts.append(high[component])
            return parts[0] if len(parts) == 1 else jnp.concatenate(parts, axis=0)

        def difference(component):
            return jnp.dot(stencil, around(component), preferred_element_type=jnp.float32)

        press_part = half * difference(0)
        sum_part = half * ((difference(1) + difference(2)) + difference(3))
        for component in range(COMPONENTS):
            wide = snap[component, start:stop].astype(jnp.float32)
            if component == 0:
                value = wide * inverse + sum_part
            else:
                value = rho * wide + press_part
            weighted[component, start:stop] = value.astype(jnp.bfloat16)


def weigh(snapshots, low, high, density, sound_speed, offsets):
    components, cells, width = snapshots.shape
    return pl.pallas_call(
        weighting_kernel,
        out_shape=jax.ShapeDtypeStruct(snapshots.shape, jnp.bfloat16),
        in_specs=[HBM, VMEM, VMEM, HBM, HBM, HBM],
        out_specs=VMEM,
        scratch_shapes=[
            pltpu.VMEM(snapshots.shape, jnp.bfloat16),
            pltpu.VMEM((1, cells), jnp.float32),
            pltpu.VMEM((1, cells), jnp.float32),
            pltpu.VMEM((1, cells), jnp.int32),
            pltpu.VMEM((8, 1024), jnp.float32),
            pltpu.SemaphoreType.DMA((components + 3,)),
        ],
        compiler_params=PARAMS,
        cost_estimate=pl.CostEstimate(flops=800_000_000, bytes_accessed=6_000_000, transcendentals=0),
    )(
        snapshots,
        low,
        high,
        in_hbm(density.reshape(1, cells)),
        in_hbm(sound_speed.reshape(1, cells)),
        in_hbm(offsets.reshape(1, cells)),
    )


def projection_kernel(snap_hbm, weighted, rot, keep, send, snap, sems):
    copies = [
        pltpu.make_async_copy(snap_hbm.at[component], snap.at[component], sems.at[component])
        for component in range(COMPONENTS)
    ]
    for copy in copies:
        copy.start()
    rotation_t = rot[...].T
    core = lax.axis_index("core")
    for component in range(COMPONENTS):
        copies[component].wait()
        mode = lax.dot_general(
            rotation_t,
            snap[component],
            (((1,), (1,)), ((), ())),
            preferred_element_type=jnp.float32,
        ).astype(jnp.bfloat16)
        total = jnp.dot(mode, weighted[component], preferred_element_type=jnp.float32).T
        owner, place = divmod(component, 2)

        @pl.when(core == owner)
        def _():
            keep[place] = total

        @pl.when(core != owner)
        def _():
            send[place] = total


def project(snapshots, weighted, rotation):
    components, cells, width = snapshots.shape
    modes = rotation.shape[1]
    half = jax.ShapeDtypeStruct((components // 2, width, modes), jnp.float32)
    return pl.pallas_call(
        projection_kernel,
        out_shape=(half, half),
        in_specs=[HBM, VMEM, VMEM],
        out_specs=(VMEM, VMEM),
        scratch_shapes=[
            pltpu.VMEM(snapshots.shape, jnp.bfloat16),
            pltpu.SemaphoreType.DMA((components,)),
        ],
        compiler_params=PARAMS,
        cost_estimate=pl.CostEstimate(flops=800_000_000, bytes_accessed=6_000_000, transcendentals=0),
    )(snapshots, weighted, rotation)


def place_kernel(mine, other, out, sems):
    core = lax.axis_index("core")
    half = mine.shape[0]
    copies = [
        pltpu.make_async_copy(mine, out.at[pl.ds(core * half, half)], sems.at[0]),
        pltpu.make_async_copy(other, out.at[pl.ds((1 - core) * half, half)], sems.at[1]),
    ]
    for copy in copies:
        copy.start()
    for copy in copies:
        copy.wait()


def place(mine, other):
    half, width, modes = mine.shape
    return pl.pallas_call(
        place_kernel,
        out_shape=jax.ShapeDtypeStruct((2 * half, width, modes), mine.dtype),
        in_specs=[VMEM, VMEM],
        out_specs=HBM,
        scratch_shapes=[pltpu.SemaphoreType.DMA((2,))],
        compiler_params=PARAMS,
    )(mine, other)


def spread(block, axes):
    count = lax.axis_size(axes)
    return lax.all_to_all(jnp.broadcast_to(block[None], (count,) + block.shape), axes, 0, 0)


def on_device(snapshots, density, sound_speed, offsets, rotation):
    components, cells, width = snapshots.shape
    count = lax.axis_size(CELL_AXES)
    resident = in_hbm(snapshots)
    forward = [(i, (i + 1) % count) for i in range(count)]
    backward = [(i, (i - 1) % count) for i in range(count)]
    swap = [(0, 1), (1, 0)]
    with jax.named_scope("halo"):
        ends = snapshots[:, cells - HALO :], snapshots[:, :HALO]
        last, first, rotation = lax.optimization_barrier((*ends, rotation))
        low = lax.ppermute(last, CELL_AXES, forward)
        high = lax.ppermute(first, CELL_AXES, backward)
    with jax.named_scope("rotation_rows"):
        full_rotation = spread(rotation, TILE_AXES).reshape(width, rotation.shape[1])
    with jax.named_scope("weighting"):
        weighted = weigh(resident, low, high, density, sound_speed, offsets)
    with jax.named_scope("projections"):
        keep, send = project(resident, weighted, full_rotation)
    modes = keep.shape[2]
    members = lax.axis_size(PLANE_AXES)
    with jax.named_scope("sum_core"):
        mine = keep + lax.ppermute(send, "core", swap)
    with jax.named_scope("sum_plane"):
        pieces = mine.reshape(members, components * width // (2 * members), modes)
        piece = jnp.sum(lax.all_to_all(pieces, PLANE_AXES, 0, 0), axis=0)
    with jax.named_scope("sum_z"):
        piece = jnp.sum(spread(piece, ("z",)), axis=0)
        piece = piece * (1.0 / math.sqrt(cells * count))
    with jax.named_scope("share_plane"):
        mine = spread(piece, PLANE_AXES).reshape(components // 2, width, modes)
    with jax.named_scope("share_core"):
        return place(mine, lax.ppermute(mine, "core", swap))


def solution(mesh):
    fine = Mesh(mesh.devices.reshape(2, 2, 2, 8, 4), CELL_AXES)
    return jax.shard_map(
        on_device,
        mesh=fine,
        in_specs=(
            P(None, CELL_AXES, None),
            P(CELL_AXES),
            P(CELL_AXES),
            P(CELL_AXES),
            P(TILE_AXES, None),
        ),
        out_specs=P(),
        check_vma=False,
    )
```

time: 91.4 us -> 84 us (0.919)
  blocking collectives: 46.7 us -> 37.3 us
  starting transfers between devices: 23.4 us -> 28.3 us
  local copies, waits for them, and re-layouts: 7.2 us -> 2.4 us
  Pallas kernels: 3.89 us -> 8.05 us
  waiting for transfers between devices: 9.71 us -> 7.47 us
    all_to_all x2, blocking collectives: 31.1 us -> 25.6 us  [spread(): lax.all_to_all(jnp.broadcast_to(block[None], (count,) + block.shape), axe...]
    ppermute x2 -> x4, starting transfers between devices: 8.25 us -> 13.2 us  [the longest x1 7.24 us: on_device(): high = lax.ppermute(first, CELL_AXES, backward)]
    unnamed x9 -> x0, local copies, waits for them, and re-layouts: 4.77 us -> none
    pallas_call x1 -> x3, Pallas kernels: 3.89 us -> 8.05 us  [the longest x1 3.73 us: project(): pl.pallas_call(projection_kernel, out_shape=(half, half), in_specs=[HBM,...]
    all_to_all x1, blocking collectives: 15.6 us -> 11.7 us  [on_device(): piece = jnp.sum(lax.all_to_all(pieces, PLANE_AXES, 0, 0), axis=0)]
    all_to_all x1, waiting for transfers between devices: 2.3 us -> 0.01 us  [spread(): lax.all_to_all(jnp.broadcast_to(block[None], (count,) + block.shape), axe...]
    ppermute x2 -> x4, waiting for transfers between devices: 7.41 us -> 7.47 us  [the longest x1 4.49 us: on_device(): low = lax.ppermute(last, CELL_AXES, forward)]
  transfers between devices with their start and end apart: 3 -> 5, of which waited for: 2 -> 3; matrix products, arithmetic and copies ran while one was open for 1% -> 0% of each run, Pallas kernels for 0% -> 4%
where the time goes in v2:
time: 84 us; the launch traced here: 83.7 us
  blocking collectives  37.3 us (44%)
  starting transfers between devices  28.3 us (34%)
  Pallas kernels  8.05 us (10%)
  waiting for transfers between devices  7.47 us (9%)
  local copies, waits for them, and re-layouts  2.4 us (3%)
    all_to_all x2, blocking collectives, spread(): lax.all_to_all(jnp.broadcast_to(block[None], (count,) + block.shape), axe...  25.6 us
    all_to_all x1, starting transfers between devices, spread(): lax.all_to_all(jnp.broadcast_to(block[None], (count,) + block.shape), axe...  15.1 us
    all_to_all x1, blocking collectives, on_device(): piece = jnp.sum(lax.all_to_all(pieces, PLANE_AXES, 0, 0), axis=0)  11.7 us
    ppermute x1, starting transfers between devices, on_device(): high = lax.ppermute(first, CELL_AXES, backward)  7.24 us
    ppermute x1, starting transfers between devices, on_device(): return place(mine, lax.ppermute(mine, 'core', swap))  4.68 us
    ppermute x1, waiting for transfers between devices, on_device(): low = lax.ppermute(last, CELL_AXES, forward)  4.49 us
    pallas_call x1, Pallas kernels, project(): pl.pallas_call(projection_kernel, out_shape=(half, half), in_specs=[HBM,...  3.73 us
    pallas_call x1, Pallas kernels, weigh(): pl.pallas_call(weighting_kernel, out_shape=jax.ShapeDtypeStruct(snapshots...  3.43 us
  transfers between devices with their start and end apart: 5, of which 3 were waited for; matrix products, arithmetic and copies ran while one was open for 0% of the time, Pallas kernels for 4%

profile of v2, /device:TPU:1, one launch (start us, length us, event | category | flops | bytes accessed | tf_op | source)
XLA Modules:
  0.0 83.7 jit_solution(7979793328443613695)
XLA Ops:
  0.0 1.0 %fusion = (bf16[4,32,384]{2,1,0:T(8,128)(2,1)S(1)}, bf16[4,32,384]{2,1,0:T(8,128)(2,1)S(1)}) fusion(bf16[4,960,384]{2,1,0:T(8,128)(2,1)} %snap_hbm.3), kind=kLoop, calls=%fused_computation.1 | loop fusion | bytes 393216 | tf_op jit(solution)/shard_map/halo/slice | solution.py:199
  1.0 1.4 %broadcast_in_dim.6 = bf16[64,6,128]{2,1,0:T(8,128)(2,1)} broadcast(bf16[6,128]{1,0:T(8,128)(2,1)} %param.9), dimensions={1,2} | broadcast | bytes 99840 | tf_op jit(solution)/shard_map/rotation_rows/broadcast_in_dim | solution.py:188
  2.3 15.1 %all-to-all-start = ((bf16[64,6,128]{2,1,0:T(8,128)(2,1)}), bf16[64,6,128]{2,1,0:T(8,128)(2,1)S(1)}, u32[]{:S(2)}, u32[]{:S(2)}) async-start(bf16[64,6,128]{2,1,0:T(8,128)(2,1)} %broadcast_in_dim.6), calls=%async_computation | async-start | bytes 262144 | tf_op jit(solution)/shard_map/rotation_rows/all_to_all | solution.py:188
  17.4 1.1 %collective-permute-start = (bf16[4,32,384]{2,1,0:T(8,128)(2,1)S(1)}, bf16[4,32,384]{2,1,0:T(8,128)(2,1)S(1)}, u32[]{:S(2)}, u32[]{:S(2)}) collective-permute-start(bf16[4,32,384]{2,1,0:T(8,128)(2,1)S(1)} %get-tuple-element.10), channel_id=1, source_target_pairs={{0,1},{1,2},{2,3},{3,4},{4,5},{5,6},{6,7},{7,8},{8,9},{9,10},{10,1... | collective-permute-start | bytes 294920 | tf_op jit(solution)/shard_map/halo/ppermute | solution.py:201
  18.5 7.2 %collective-permute-start.1 = (bf16[4,32,384]{2,1,0:T(8,128)(2,1)S(1)}, bf16[4,32,384]{2,1,0:T(8,128)(2,1)S(1)}, u32[]{:S(2)}, u32[]{:S(2)}) collective-permute-start(bf16[4,32,384]{2,1,0:T(8,128)(2,1)S(1)} %get-tuple-element.11), channel_id=1, source_target_pairs={{0,255},{1,0},{2,1},{3,2},{4,3},{5,4},{6,5},{7,6},{8,7},{9,8},{10,... | collective-permute-start | bytes 294920 | tf_op jit(solution)/shard_map/halo/ppermute | solution.py:202
  25.8 4.5 %collective-permute-done.low = bf16[4,32,384]{2,1,0:T(8,128)(2,1)S(1)} collective-permute-done((bf16[4,32,384]{2,1,0:T(8,128)(2,1)S(1)}, bf16[4,32,384]{2,1,0:T(8,128)(2,1)S(1)}, u32[]{:S(2)}, u32[]{:S(2)}) %collective-permute-start) | collective-permute-done | bytes 98336 | tf_op jit(solution)/shard_map/halo/ppermute | solution.py:201
  30.3 0.0 collective-permute-done.1.high
  30.3 3.4 %weighting.1.weighted = bf16[4,960,384]{2,1,0:T(8,128)(2,1)S(1)} custom-call(bf16[4,960,384]{2,1,0:T(8,128)(2,1)} %snap_hbm.3, bf16[4,32,384]{2,1,0:T(8,128)(2,1)S(1)} %collective-permute-done.low, bf16[4,32,384]{2,1,0:T(8,128)(2,1)S(1)} %collective-permute-done.1.high, f32[1,960]{1,0:T(1,128)} %bitcast.8, f32[1,960]{1,0:T(1,128)} %bitcast.9, s32[1,960]{1,0:T(1,128)} %bitcast.10), custom_call_target="tpu_custom_call" | custom-call | flops 800000000 | bytes 6000000 | tf_op jit(solution)/shard_map/weighting/pallas_call | solution.py:89
  33.7 0.0 all-to-all-done
  33.8 3.7 %projections.1 = (f32[2,384,128]{2,1,0:T(8,128)S(1)}, f32[2,384,128]{2,1,0:T(8,128)S(1)}) custom-call(bf16[4,960,384]{2,1,0:T(8,128)(2,1)} %snap_hbm.3, bf16[4,960,384]{2,1,0:T(8,128)(2,1)S(1)} %weighting.1.weighted, bf16[384,128]{1,0:T(8,128)(2,1)S(1)} %reshape.26.rot), custom_call_target="tpu_custom_call" | custom-call | flops 800000000 | bytes 6000000 | tf_op jit(solution)/shard_map/projections/pallas_call | solution.py:147
  37.5 0.2 collective-permute-start.2
  37.7 1.6 %collective-permute-done.2 = f32[2,384,128]{2,1,0:T(8,128)S(1)} collective-permute-done((f32[2,384,128]{2,1,0:T(8,128)S(1)}, f32[2,384,128]{2,1,0:T(8,128)S(1)}, u32[]{:S(2)}, u32[]{:S(2)}) %collective-permute-start.2) | collective-permute-done | bytes 393248 | tf_op jit(solution)/shard_map/sum_core/ppermute | solution.py:212
  39.3 0.1 add.3
  39.4 11.7 %all_to_all.20 = f32[16,48,128]{2,1,0:T(8,128)S(1)} all-to-all(f32[16,48,128]{2,1,0:T(8,128)S(1)} %bitcast.7), channel_id=1, replica_groups=mesh['x_lo'=2,'core'=2,'x_hi'=2,'z'=8,'y'=4] {'x_lo','x_hi','y'}, dimensions={0} | all-to-all | bytes 786432 | tf_op jit(solution)/shard_map/sum_plane/all_to_all | solution.py:215
  51.1 14.8 %all_to_all.21 = f32[8,48,128]{2,1,0:T(8,128)S(1)} all-to-all(f32[8,48,128]{2,1,0:T(8,128)S(1)} %broadcast_in_dim.7), channel_id=1, replica_groups=mesh['x_lo'=2,'core'=2,'x_hi'=2,'z'=8,'y'=4] {'z'}, dimensions={0} | all-to-all | bytes 393216 | tf_op jit(solution)/shard_map/sum_z/all_to_all | solution.py:188
  66.0 10.8 %all_to_all.22 = f32[16,48,128]{2,1,0:T(8,128)S(1)} all-to-all(f32[16,48,128]{2,1,0:T(8,128)S(1)} %broadcast_in_dim.8), channel_id=1, replica_groups=mesh['x_lo'=2,'core'=2,'x_hi'=2,'z'=8,'y'=4] {'x_lo','x_hi','y'}, dimensions={0} | all-to-all | bytes 786432 | tf_op jit(solution)/shard_map/share_plane/all_to_all | solution.py:188
  76.8 4.7 %collective-permute-start.3 = (f32[2,384,128]{2,1,0:T(8,128)S(1)}, f32[2,384,128]{2,1,0:T(8,128)S(1)}, u32[]{:S(2)}, u32[]{:S(2)}) collective-permute-start(f32[2,384,128]{2,1,0:T(8,128)S(1)} %bitcast.5), channel_id=1, source_target_pairs={{0,64},{64,0},{1,65},{65,1},{2,66},{66,2},{3,67},{67,3},{4,68},{68... | collective-permute-start | bytes 1179656 | tf_op jit(solution)/shard_map/share_core/ppermute | solution.py:222
  81.4 1.3 %collective-permute-done.3.other = f32[2,384,128]{2,1,0:T(8,128)S(1)} collective-permute-done((f32[2,384,128]{2,1,0:T(8,128)S(1)}, f32[2,384,128]{2,1,0:T(8,128)S(1)}, u32[]{:S(2)}, u32[]{:S(2)}) %collective-permute-start.3) | collective-permute-done | bytes 393248 | tf_op jit(solution)/shard_map/share_core/ppermute | solution.py:222
  82.8 0.9 %share_core.1 = f32[4,384,128]{2,1,0:T(8,128)} custom-call(f32[2,384,128]{2,1,0:T(8,128)S(1)} %bitcast.6, f32[2,384,128]{2,1,0:T(8,128)S(1)} %collective-permute-done.3.other), custom_call_target="tpu_custom_call" | custom-call | tf_op jit(solution)/shard_map/share_core/pallas_call | solution.py:176
  (6 shorter events, 0.1 us)
Async XLA Ops:
  2.3 31.4 %all-to-all-start = ((bf16[64,6,128]{2,1,0:T(8,128)(2,1)}), bf16[64,6,128]{2,1,0:T(8,128)(2,1)S(1)}, u32[]{:S(2)}, u32[]{:S(2)}) async-start(bf16[64,6,128]{2,1,0:T(8,128)(2,1)} %broadcast_in_dim.6), calls=%async_computation | async-start | bytes 262144 | tf_op jit(solution)/shard_map/rotation_rows/all_to_all | solution.py:188
  17.4 12.8 %collective-permute-start = (bf16[4,32,384]{2,1,0:T(8,128)(2,1)S(1)}, bf16[4,32,384]{2,1,0:T(8,128)(2,1)S(1)}, u32[]{:S(2)}, u32[]{:S(2)}) collective-permute-start(bf16[4,32,384]{2,1,0:T(8,128)(2,1)S(1)} %get-tuple-element.10), channel_id=1, source_target_pairs={{0,1},{1,2},{2,3},{3,4},{4,5},{5,6},{6,7},{7,8},{8,9},{9,10},{10,1... | collective-permute-start | bytes 294920 | tf_op jit(solution)/shard_map/halo/ppermute | solution.py:201
  18.5 11.7 %collective-permute-start.1 = (bf16[4,32,384]{2,1,0:T(8,128)(2,1)S(1)}, bf16[4,32,384]{2,1,0:T(8,128)(2,1)S(1)}, u32[]{:S(2)}, u32[]{:S(2)}) collective-permute-start(bf16[4,32,384]{2,1,0:T(8,128)(2,1)S(1)} %get-tuple-element.11), channel_id=1, source_target_pairs={{0,255},{1,0},{2,1},{3,2},{4,3},{5,4},{6,5},{7,6},{8,7},{9,8},{10,... | collective-permute-start | bytes 294920 | tf_op jit(solution)/shard_map/halo/ppermute | solution.py:202
  37.5 1.8 %collective-permute-start.2 = (f32[2,384,128]{2,1,0:T(8,128)S(1)}, f32[2,384,128]{2,1,0:T(8,128)S(1)}, u32[]{:S(2)}, u32[]{:S(2)}) collective-permute-start(f32[2,384,128]{2,1,0:T(8,128)S(1)} %get-tuple-element.14), channel_id=1, source_target_pairs={{0,64},{64,0},{1,65},{65,1},{2,66},{66,2},{3,67},{67,3},{4,68},{68... | collective-permute-start | bytes 1179656 | tf_op jit(solution)/shard_map/sum_core/ppermute | solution.py:212
  76.8 6.0 %collective-permute-start.3 = (f32[2,384,128]{2,1,0:T(8,128)S(1)}, f32[2,384,128]{2,1,0:T(8,128)S(1)}, u32[]{:S(2)}, u32[]{:S(2)}) collective-permute-start(f32[2,384,128]{2,1,0:T(8,128)S(1)} %bitcast.5), channel_id=1, source_target_pairs={{0,64},{64,0},{1,65},{65,1},{2,66},{66,2},{3,67},{67,3},{4,68},{68... | collective-permute-start | bytes 1179656 | tf_op jit(solution)/shard_map/share_core/ppermute | solution.py:222

commit v3 on v2

v3 whole, which is shorter than its diff:
```python
import math

import jax
import jax.numpy as jnp
from jax import lax
from jax.experimental import pallas as pl
from jax.experimental.pallas import tpu as pltpu
from jax.sharding import Mesh, PartitionSpec as P

HALO = 32
COMPONENTS = 4
BLOCK = 192
PADDED = 8
WEIGHT_FLOPS = 1_000_000_000
EDGE_FLOPS = 10_000_000_000
TILE_AXES = ("x_hi", "z", "y")
PLANE_AXES = ("x_lo", "x_hi", "y")
CELL_AXES = ("x_lo", "core", "x_hi", "z", "y")
VMEM = pl.BlockSpec(memory_space=pltpu.VMEM)
HBM = pl.BlockSpec(memory_space=pltpu.HBM)
PARAMS = pltpu.CompilerParams(vmem_limit_bytes=12 << 20)


def in_hbm(array):
    return pltpu.with_memory_space_constraint(array, pltpu.HBM)


def start_kernel(snap, rot_hbm, first, last, spread_rot, rot, sems):
    cells = snap.shape[1]
    copies = [
        pltpu.make_async_copy(rot_hbm, rot, sems.at[0]),
        pltpu.make_async_copy(snap.at[:, pl.ds(0, HALO)], first, sems.at[1]),
        pltpu.make_async_copy(snap.at[:, pl.ds(cells - HALO, HALO)], last, sems.at[2]),
    ]
    for copy in copies:
        copy.start()
    copies[0].wait()
    rows = rot.shape[0]
    padding = jnp.zeros((PADDED - rows, rot.shape[1]), jnp.float32)
    block = jnp.concatenate([rot[...].astype(jnp.float32), padding], axis=0).astype(jnp.bfloat16)
    for tile in range(spread_rot.shape[0]):
        spread_rot[tile] = block
    for copy in copies[1:]:
        copy.wait()


def start(snapshots, rotation, tiles):
    components, _, width = snapshots.shape
    rows, modes = rotation.shape
    edge = jax.ShapeDtypeStruct((components, HALO, width), jnp.bfloat16)
    return pl.pallas_call(
        start_kernel,
        out_shape=(edge, edge, jax.ShapeDtypeStruct((tiles, PADDED, modes), jnp.bfloat16)),
        in_specs=[HBM, HBM],
        out_specs=(VMEM, VMEM, VMEM),
        scratch_shapes=[pltpu.VMEM((rows, modes), jnp.bfloat16), pltpu.SemaphoreType.DMA((3,))],
        compiler_params=PARAMS,
    )(snapshots, in_hbm(rotation))


def stencil_of(shift, window, offset):
    shape = (shift.shape[0], window)
    row_at = lax.broadcasted_iota(jnp.int32, shape, 0) + offset
    col_at = lax.broadcasted_iota(jnp.int32, shape, 1)
    here = (col_at == row_at).astype(jnp.float32)
    there = (col_at == row_at + shift).astype(jnp.float32)
    return (there - here).astype(jnp.bfloat16)


def weigh_rows(scale, offset, around, block):
    rho, inverse, half = scale[:, 0:1], scale[:, 1:2], scale[:, 2:3]
    stencil = stencil_of(scale[:, 3:4].astype(jnp.int32), around(0).shape[0], offset)

    def difference(component):
        return jnp.dot(stencil, around(component), preferred_element_type=jnp.float32)

    press_part = half * difference(0)
    sum_part = half * ((difference(1) + difference(2)) + difference(3))
    values = []
    for component in range(COMPONENTS):
        wide = block(component).astype(jnp.float32)
        value = wide * inverse + sum_part if component == 0 else rho * wide + press_part
        values.append(value.astype(jnp.bfloat16))
    return values


def weighting_kernel(
    snap_hbm, dens_hbm, speed_hbm, offs_hbm, weighted, edge_scale, snap, dens, speed, offs, rows_ref, sems
):
    cells = snap.shape[1]
    vectors = ((dens_hbm, dens), (speed_hbm, speed), (offs_hbm, offs))
    small = [
        pltpu.make_async_copy(source, target, sems.at[COMPONENTS + i])
        for i, (source, target) in enumerate(vectors)
    ]
    copies = [
        pltpu.make_async_copy(snap_hbm.at[component], snap.at[component], sems.at[component])
        for component in range(COMPONENTS)
    ]
    for copy in small + copies:
        copy.start()
    for copy in small:
        copy.wait()
    density = dens[...]
    sound = speed[...]
    rows_ref[...] = jnp.zeros_like(rows_ref)
    rows_ref[0:1, 0:cells] = density
    rows_ref[1:2, 0:cells] = 1.0 / (density * sound * sound)
    rows_ref[2:3, 0:cells] = 0.5 / sound
    rows_ref[3:4, 0:cells] = offs[...].astype(jnp.float32)
    columns = rows_ref[...].T
    edge_scale[0:HALO] = columns[0:HALO]
    edge_scale[HALO:] = columns[cells - HALO : cells]
    for copy in copies:
        copy.wait()
    for begin in range(0, cells, BLOCK):
        stop = begin + BLOCK
        low, high = max(begin - HALO, 0), min(stop + HALO, cells)
        values = weigh_rows(
            columns[begin:stop],
            begin - low,
            lambda component: snap[component, low:high],
            lambda component: snap[component, begin:stop],
        )
        for component in range(COMPONENTS):
            weighted[component, begin:stop] = values[component]


def weigh(snapshots, density, sound_speed, offsets):
    components, cells, width = snapshots.shape
    field = jax.ShapeDtypeStruct(snapshots.shape, jnp.bfloat16)
    return pl.pallas_call(
        weighting_kernel,
        out_shape=(field, jax.ShapeDtypeStruct((2 * HALO, 8), jnp.float32)),
        in_specs=[HBM] * 4,
        out_specs=(VMEM, VMEM),
        scratch_shapes=[
            pltpu.VMEM(snapshots.shape, jnp.bfloat16),
            pltpu.VMEM((1, cells), jnp.float32),
            pltpu.VMEM((1, cells), jnp.float32),
            pltpu.VMEM((1, cells), jnp.int32),
            pltpu.VMEM((8, 1024), jnp.float32),
            pltpu.SemaphoreType.DMA((components + 3,)),
        ],
        compiler_params=PARAMS,
        cost_estimate=pl.CostEstimate(
            flops=WEIGHT_FLOPS, bytes_accessed=6_000_000, transcendentals=0
        ),
    )(
        snapshots,
        in_hbm(density.reshape(1, cells)),
        in_hbm(sound_speed.reshape(1, cells)),
        in_hbm(offsets.reshape(1, cells)),
    )


def edge_kernel(snap_hbm, edge_scale, low, high, edges, begin, end, sems):
    cells = snap_hbm.shape[1]
    copies = [
        pltpu.make_async_copy(snap_hbm.at[:, pl.ds(0, 2 * HALO)], begin, sems.at[0]),
        pltpu.make_async_copy(snap_hbm.at[:, pl.ds(cells - 2 * HALO, 2 * HALO)], end, sems.at[1]),
    ]
    for copy in copies:
        copy.start()
    for copy in copies:
        copy.wait()
    first = weigh_rows(
        edge_scale[0:HALO],
        HALO,
        lambda component: jnp.concatenate([low[component], begin[component]], axis=0),
        lambda component: begin[component, 0:HALO],
    )
    last = weigh_rows(
        edge_scale[HALO:],
        HALO,
        lambda component: jnp.concatenate([end[component], high[component]], axis=0),
        lambda component: end[component, HALO:],
    )
    for component in range(COMPONENTS):
        edges[component, 0:HALO] = first[component]
        edges[component, HALO:] = last[component]


def weigh_edges(snapshots, edge_scale, low, high):
    components, _, width = snapshots.shape
    rim = (components, 2 * HALO, width)
    return pl.pallas_call(
        edge_kernel,
        out_shape=jax.ShapeDtypeStruct(rim, jnp.bfloat16),
        in_specs=[HBM, VMEM, VMEM, VMEM],
        out_specs=VMEM,
        scratch_shapes=[
            pltpu.VMEM(rim, jnp.bfloat16),
            pltpu.VMEM(rim, jnp.bfloat16),
            pltpu.SemaphoreType.DMA((2,)),
        ],
        compiler_params=PARAMS,
        cost_estimate=pl.CostEstimate(flops=EDGE_FLOPS, bytes_accessed=600_000, transcendentals=0),
    )(snapshots, edge_scale, low, high)


def projection_kernel(snap_hbm, weighted, edges, rot, keep, send, snap, sems):
    cells, width = snap.shape[1:]
    copies = [
        pltpu.make_async_copy(snap_hbm.at[component], snap.at[component], sems.at[component])
        for component in range(COMPONENTS)
    ]
    for copy in copies[:2]:
        copy.start()
    tiles, padded, modes = rot.shape
    rows = width // tiles
    shape = (width, tiles * padded)
    target = lax.broadcasted_iota(jnp.int32, shape, 0)
    source = lax.broadcasted_iota(jnp.int32, shape, 1)
    within = source & (padded - 1)
    tile = (source - within) // padded
    chosen = jnp.logical_and(target == tile * rows + within, within < rows)
    compact = jnp.dot(
        chosen.astype(jnp.float32).astype(jnp.bfloat16),
        rot[...].reshape(tiles * padded, modes),
        preferred_element_type=jnp.float32,
    )
    rotation_t = compact.T.astype(jnp.bfloat16)
    core = lax.axis_index("core")
    for component in range(COMPONENTS):
        copies[component].wait()
        if component + 2 < COMPONENTS:
            copies[component + 2].start()
        mode = lax.dot_general(
            rotation_t,
            snap[component],
            (((1,), (1,)), ((), ())),
            preferred_element_type=jnp.float32,
        ).astype(jnp.bfloat16)
        parts = [
            edges[component, 0:HALO],
            weighted[component, HALO : cells - HALO],
            edges[component, HALO:],
        ]
        total = jnp.dot(mode, jnp.concatenate(parts, axis=0), preferred_element_type=jnp.float32).T
        owner, place = divmod(component, 2)

        @pl.when(core == owner)
        def _():
            keep[place] = total

        @pl.when(core != owner)
        def _():
            send[place] = total


def project(snapshots, weighted, edges, rotation):
    components, _, width = snapshots.shape
    half = jax.ShapeDtypeStruct((components // 2, width, rotation.shape[2]), jnp.float32)
    return pl.pallas_call(
        projection_kernel,
        out_shape=(half, half),
        in_specs=[HBM] + [VMEM] * 3,
        out_specs=(VMEM, VMEM),
        scratch_shapes=[
            pltpu.VMEM(snapshots.shape, jnp.bfloat16),
            pltpu.SemaphoreType.DMA((components,)),
        ],
        compiler_params=PARAMS,
        cost_estimate=pl.CostEstimate(flops=800_000_000, bytes_accessed=6_000_000, transcendentals=0),
    )(snapshots, weighted, edges, rotation)


def place_kernel(mine, other, out, sems):
    core = lax.axis_index("core")
    half = mine.shape[0]
    copies = [
        pltpu.make_async_copy(mine, out.at[pl.ds(core * half, half)], sems.at[0]),
        pltpu.make_async_copy(other, out.at[pl.ds((1 - core) * half, half)], sems.at[1]),
    ]
    for copy in copies:
        copy.start()
    for copy in copies:
        copy.wait()


def place(mine, other):
    half, width, modes = mine.shape
    return pl.pallas_call(
        place_kernel,
        out_shape=jax.ShapeDtypeStruct((2 * half, width, modes), mine.dtype),
        in_specs=[VMEM, VMEM],
        out_specs=HBM,
        scratch_shapes=[pltpu.SemaphoreType.DMA((2,))],
        compiler_params=PARAMS,
    )(mine, other)


def spread(block, axes):
    count = lax.axis_size(axes)
    return lax.all_to_all(jnp.broadcast_to(block[None], (count,) + block.shape), axes, 0, 0)


def on_device(snapshots, density, sound_speed, offsets, rotation):
    components, cells, width = snapshots.shape
    count = lax.axis_size(CELL_AXES)
    resident = in_hbm(snapshots)
    forward = [(i, (i + 1) % count) for i in range(count)]
    backward = [(i, (i - 1) % count) for i in range(count)]
    swap = [(0, 1), (1, 0)]
    with jax.named_scope("start"):
        first, last, rows = start(resident, rotation, lax.axis_size(TILE_AXES))
    with jax.named_scope("halo"):
        low = lax.ppermute(last, CELL_AXES, forward)
        high = lax.ppermute(first, CELL_AXES, backward)
    with jax.named_scope("rotation_rows"):
        full_rotation = lax.all_to_all(rows, TILE_AXES, 0, 0)
    with jax.named_scope("weighting"):
        weighted, edge_scale = weigh(resident, density, sound_speed, offsets)
        edges = weigh_edges(resident, edge_scale, low, high)
    with jax.named_scope("projections"):
        keep, send = project(resident, weighted, edges, full_rotation)
    modes = keep.shape[2]
    members = lax.axis_size(PLANE_AXES)
    with jax.named_scope("sum_core"):
        mine = keep + lax.ppermute(send, "core", swap)
    with jax.named_scope("sum_plane"):
        pieces = mine.reshape(members, components * width // (2 * members), modes)
        piece = jnp.sum(lax.all_to_all(pieces, PLANE_AXES, 0, 0), axis=0)
    with jax.named_scope("sum_z"):
        piece = jnp.sum(spread(piece, ("z",)), axis=0)
        piece = piece * (1.0 / math.sqrt(cells * count))
    with jax.named_scope("share_plane"):
        mine = spread(piece, PLANE_AXES).reshape(components // 2, width, modes)
    with jax.named_scope("share_core"):
        return place(mine, lax.ppermute(mine, "core", swap))


def solution(mesh):
    fine = Mesh(mesh.devices.reshape(2, 2, 2, 8, 4), CELL_AXES)
    return jax.shard_map(
        on_device,
        mesh=fine,
        in_specs=(
            P(None, CELL_AXES, None),
            P(CELL_AXES),
            P(CELL_AXES),
            P(CELL_AXES),
            P(TILE_AXES, None),
        ),
        out_specs=P(),
        check_vma=False,
    )
```

time: 84 us -> 79.3 us (0.944)
  starting transfers between devices: 28.3 us -> 24.1 us
  blocking collectives: 37.3 us -> 34.1 us
  Pallas kernels: 8.05 us -> 11.1 us
  local copies, waits for them, and re-layouts: 2.4 us -> 0.04 us
  waiting for transfers between devices: 7.47 us -> 9.38 us
    all_to_all x1, starting transfers between devices: 15.1 us -> 5.3 us  [on_device(): full_rotation = lax.all_to_all(rows, TILE_AXES, 0, 0)]
    all_to_all x1, waiting for transfers between devices: 0.01 us -> 6.68 us  [on_device(): full_rotation = lax.all_to_all(rows, TILE_AXES, 0, 0)]
    ppermute x1, waiting for transfers between devices: 4.49 us -> 0.01 us  [on_device(): low = lax.ppermute(last, CELL_AXES, forward)]
    all_to_all x2, blocking collectives: 25.6 us -> 22.5 us  [spread(): lax.all_to_all(jnp.broadcast_to(block[None], (count,) + block.shape), axe...]
    pallas_call x2 -> x4, Pallas kernels: 7.16 us -> 10.2 us  [the longest x1 3.83 us: project(): pl.pallas_call(projection_kernel, out_shape=(half, half), in_specs=[HBM]...]
    ppermute x1, starting transfers between devices: 0.19 us -> 2.8 us  [on_device(): mine = keep + lax.ppermute(send, 'core', swap)]
    ppermute x1, starting transfers between devices: 7.24 us -> 9.84 us  [on_device(): high = lax.ppermute(first, CELL_AXES, backward)]
    broadcast_in_dim x3 -> x2, local copies, waits for them, and re-layouts: 1.4 us -> 0.04 us  [spread(): jnp.broadcast_to(block[None], (count,) + block.shape)]
  transfers between devices with their start and end apart: 5 -> 5, of which waited for: 3 -> 3; matrix products, arithmetic and copies ran while one was open for 0% -> 0% of each run, Pallas kernels for 4% -> 6%
where the time goes in v3:
time: 79.3 us; the launch traced here: 78.9 us
  blocking collectives  34.1 us (43%)
  starting transfers between devices  24.1 us (30%)
  Pallas kernels  11.1 us (14%)
  waiting for transfers between devices  9.38 us (12%)
    all_to_all x2, blocking collectives, spread(): lax.all_to_all(jnp.broadcast_to(block[None], (count,) + block.shape), axe...  22.5 us
    all_to_all x1, blocking collectives, on_device(): piece = jnp.sum(lax.all_to_all(pieces, PLANE_AXES, 0, 0), axis=0)  11.6 us
    ppermute x1, starting transfers between devices, on_device(): high = lax.ppermute(first, CELL_AXES, backward)  9.84 us
    all_to_all x1, waiting for transfers between devices, on_device(): full_rotation = lax.all_to_all(rows, TILE_AXES, 0, 0)  6.68 us
    all_to_all x1, starting transfers between devices, on_device(): full_rotation = lax.all_to_all(rows, TILE_AXES, 0, 0)  5.3 us
    ppermute x1, starting transfers between devices, on_device(): return place(mine, lax.ppermute(mine, 'core', swap))  3.96 us
    pallas_call x1, Pallas kernels, project(): pl.pallas_call(projection_kernel, out_shape=(half, half), in_specs=[HBM]...  3.83 us
    pallas_call x1, Pallas kernels, weigh(): pl.pallas_call(weighting_kernel, out_shape=(field, jax.ShapeDtypeStruct((...  3.42 us
  transfers between devices with their start and end apart: 5, of which 3 were waited for; matrix products, arithmetic and copies ran while one was open for 0% of the time, Pallas kernels for 6%

profile of v3, /device:TPU:1, one launch (start us, length us, event | category | flops | bytes accessed | tf_op | source)
XLA Modules:
  0.0 78.9 jit_solution(2775298550619252782)
XLA Ops:
  0.0 1.6 %start.1 = (bf16[4,32,384]{2,1,0:T(8,128)(2,1)S(1)}, bf16[4,32,384]{2,1,0:T(8,128)(2,1)S(1)}, bf16[64,8,128]{2,1,0:T(8,128)(2,1)}) custom-call(bf16[4,960,384]{2,1,0:T(8,128)(2,1)} %snap_hbm.5, bf16[6,128]{1,0:T(8,128)(2,1)} %rot_hbm.1), custom_call_target="tpu_custom_call" | custom-call | tf_op jit(solution)/shard_map/start/pallas_call | solution.py:51
  1.6 2.2 %collective-permute-start = (bf16[4,32,384]{2,1,0:T(8,128)(2,1)S(1)}, bf16[4,32,384]{2,1,0:T(8,128)(2,1)S(1)}, u32[]{:S(2)}, u32[]{:S(2)}) collective-permute-start(bf16[4,32,384]{2,1,0:T(8,128)(2,1)S(1)} %get-tuple-element.14), channel_id=1, source_target_pairs={{0,1},{1,2},{2,3},{3,4},{4,5},{5,6},{6,7},{7,8},{8,9},{9,10},{10,1... | collective-permute-start | bytes 294920 | tf_op jit(solution)/shard_map/halo/ppermute | solution.py:309
  3.9 9.8 %collective-permute-start.1 = (bf16[4,32,384]{2,1,0:T(8,128)(2,1)S(1)}, bf16[4,32,384]{2,1,0:T(8,128)(2,1)S(1)}, u32[]{:S(2)}, u32[]{:S(2)}) collective-permute-start(bf16[4,32,384]{2,1,0:T(8,128)(2,1)S(1)} %get-tuple-element.15), channel_id=1, source_target_pairs={{0,255},{1,0},{2,1},{3,2},{4,3},{5,4},{6,5},{7,6},{8,7},{9,8},{10,... | collective-permute-start | bytes 294920 | tf_op jit(solution)/shard_map/halo/ppermute | solution.py:310
  13.7 5.3 %all-to-all-start = ((bf16[64,8,128]{2,1,0:T(8,128)(2,1)}), bf16[64,8,128]{2,1,0:T(8,128)(2,1)S(1)}, u32[]{:S(2)}, u32[]{:S(2)}) async-start(bf16[64,8,128]{2,1,0:T(8,128)(2,1)} %get-tuple-element.16), calls=%async_computation | async-start | bytes 262144 | tf_op jit(solution)/shard_map/rotation_rows/all_to_all | solution.py:312
  19.0 3.4 %weighting.2 = (bf16[4,960,384]{2,1,0:T(8,128)(2,1)S(1)}, f32[64,8]{1,0:T(8,128)S(1)}) custom-call(bf16[4,960,384]{2,1,0:T(8,128)(2,1)} %snap_hbm.5, f32[1,960]{1,0:T(1,128)} %bitcast.8, f32[1,960]{1,0:T(1,128)} %bitcast.9, s32[1,960]{1,0:T(1,128)} %bitcast.10), custom_call_target="tpu_custom_call" | custom-call | flops 1000000000 | bytes 6000000 | tf_op jit(solution)/shard_map/weighting/pallas_call | solution.py:132
  22.4 0.0 collective-permute-done.low
  22.4 0.0 collective-permute-done.1.high
  22.4 1.3 %weighting.3.edges = bf16[4,64,384]{2,1,0:T(8,128)(2,1)S(1)} custom-call(bf16[4,960,384]{2,1,0:T(8,128)(2,1)} %snap_hbm.5, f32[64,8]{1,0:T(8,128)S(1)} %get-tuple-element.13.edge_scale, bf16[4,32,384]{2,1,0:T(8,128)(2,1)S(1)} %collective-permute-done.low, bf16[4,32,384]{2,1,0:T(8,128)(2,1)S(1)} %collective-permute-done.1.high), custom_call_target="tpu_custom_call" | custom-call | flops 10000000000 | bytes 600000 | tf_op jit(solution)/shard_map/weighting/pallas_call | solution.py:187
  23.8 6.7 %all-to-all-done.rot = bf16[64,8,128]{2,1,0:T(8,128)(2,1)S(1)} async-done(((bf16[64,8,128]{2,1,0:T(8,128)(2,1)}), bf16[64,8,128]{2,1,0:T(8,128)(2,1)S(1)}, u32[]{:S(2)}, u32[]{:S(2)}) %all-to-all-start) | async-done | bytes 131104 | tf_op jit(solution)/shard_map/rotation_rows/all_to_all | solution.py:312
  30.5 3.8 %projections.1 = (f32[2,384,128]{2,1,0:T(8,128)S(1)}, f32[2,384,128]{2,1,0:T(8,128)S(1)}) custom-call(bf16[4,960,384]{2,1,0:T(8,128)(2,1)} %snap_hbm.5, bf16[4,960,384]{2,1,0:T(8,128)(2,1)S(1)} %get-tuple-element.12.weighted, bf16[4,64,384]{2,1,0:T(8,128)(2,1)S(1)} %weighting.3.edges, bf16[64,8,128]{2,1,0:T(8,128)(2,1)S(1)} %all-to-all-done.rot), custom_call_target="tpu_custom_call" | custom-call | flops 800000000 | bytes 6000000 | tf_op jit(solution)/shard_map/projections/pallas_call | solution.py:255
  34.3 2.8 %collective-permute-start.2 = (f32[2,384,128]{2,1,0:T(8,128)S(1)}, f32[2,384,128]{2,1,0:T(8,128)S(1)}, u32[]{:S(2)}, u32[]{:S(2)}) collective-permute-start(f32[2,384,128]{2,1,0:T(8,128)S(1)} %get-tuple-element.18), channel_id=1, source_target_pairs={{0,64},{64,0},{1,65},{65,1},{2,66},{66,2},{3,67},{67,3},{4,68},{68... | collective-permute-start | bytes 1179656 | tf_op jit(solution)/shard_map/sum_core/ppermute | solution.py:321
  37.1 1.3 %collective-permute-done.2 = f32[2,384,128]{2,1,0:T(8,128)S(1)} collective-permute-done((f32[2,384,128]{2,1,0:T(8,128)S(1)}, f32[2,384,128]{2,1,0:T(8,128)S(1)}, u32[]{:S(2)}, u32[]{:S(2)}) %collective-permute-start.2) | collective-permute-done | bytes 393248 | tf_op jit(solution)/shard_map/sum_core/ppermute | solution.py:321
  38.5 0.1 add.3
  38.5 11.6 %all_to_all.20 = f32[16,48,128]{2,1,0:T(8,128)S(1)} all-to-all(f32[16,48,128]{2,1,0:T(8,128)S(1)} %bitcast.7), channel_id=1, replica_groups=mesh['x_lo'=2,'core'=2,'x_hi'=2,'z'=8,'y'=4] {'x_lo','x_hi','y'}, dimensions={0} | all-to-all | bytes 786432 | tf_op jit(solution)/shard_map/sum_plane/all_to_all | solution.py:324
  50.2 11.1 %all_to_all.21 = f32[8,48,128]{2,1,0:T(8,128)S(1)} all-to-all(f32[8,48,128]{2,1,0:T(8,128)S(1)} %broadcast_in_dim.4), channel_id=1, replica_groups=mesh['x_lo'=2,'core'=2,'x_hi'=2,'z'=8,'y'=4] {'z'}, dimensions={0} | all-to-all | bytes 393216 | tf_op jit(solution)/shard_map/sum_z/all_to_all | solution.py:296
  61.4 11.3 %all_to_all.22 = f32[16,48,128]{2,1,0:T(8,128)S(1)} all-to-all(f32[16,48,128]{2,1,0:T(8,128)S(1)} %broadcast_in_dim.5), channel_id=1, replica_groups=mesh['x_lo'=2,'core'=2,'x_hi'=2,'z'=8,'y'=4] {'x_lo','x_hi','y'}, dimensions={0} | all-to-all | bytes 786432 | tf_op jit(solution)/shard_map/share_plane/all_to_all | solution.py:296
  72.7 4.0 %collective-permute-start.3 = (f32[2,384,128]{2,1,0:T(8,128)S(1)}, f32[2,384,128]{2,1,0:T(8,128)S(1)}, u32[]{:S(2)}, u32[]{:S(2)}) collective-permute-start(f32[2,384,128]{2,1,0:T(8,128)S(1)} %bitcast.5), channel_id=1, source_target_pairs={{0,64},{64,0},{1,65},{65,1},{2,66},{66,2},{3,67},{67,3},{4,68},{68... | collective-permute-start | bytes 1179656 | tf_op jit(solution)/shard_map/share_core/ppermute | solution.py:331
  76.7 1.3 %collective-permute-done.3.other = f32[2,384,128]{2,1,0:T(8,128)S(1)} collective-permute-done((f32[2,384,128]{2,1,0:T(8,128)S(1)}, f32[2,384,128]{2,1,0:T(8,128)S(1)}, u32[]{:S(2)}, u32[]{:S(2)}) %collective-permute-start.3) | collective-permute-done | bytes 393248 | tf_op jit(solution)/shard_map/share_core/ppermute | solution.py:331
  78.0 0.9 %share_core.1 = f32[4,384,128]{2,1,0:T(8,128)} custom-call(f32[2,384,128]{2,1,0:T(8,128)S(1)} %bitcast.6, f32[2,384,128]{2,1,0:T(8,128)S(1)} %collective-permute-done.3.other), custom_call_target="tpu_custom_call" | custom-call | tf_op jit(solution)/shard_map/share_core/pallas_call | solution.py:284
  (5 shorter events, 0.1 us)
Async XLA Ops:
  1.6 20.8 %collective-permute-start = (bf16[4,32,384]{2,1,0:T(8,128)(2,1)S(1)}, bf16[4,32,384]{2,1,0:T(8,128)(2,1)S(1)}, u32[]{:S(2)}, u32[]{:S(2)}) collective-permute-start(bf16[4,32,384]{2,1,0:T(8,128)(2,1)S(1)} %get-tuple-element.14), channel_id=1, source_target_pairs={{0,1},{1,2},{2,3},{3,4},{4,5},{5,6},{6,7},{7,8},{8,9},{9,10},{10,1... | collective-permute-start | bytes 294920 | tf_op jit(solution)/shard_map/halo/ppermute | solution.py:309
  3.9 18.6 %collective-permute-start.1 = (bf16[4,32,384]{2,1,0:T(8,128)(2,1)S(1)}, bf16[4,32,384]{2,1,0:T(8,128)(2,1)S(1)}, u32[]{:S(2)}, u32[]{:S(2)}) collective-permute-start(bf16[4,32,384]{2,1,0:T(8,128)(2,1)S(1)} %get-tuple-element.15), channel_id=1, source_target_pairs={{0,255},{1,0},{2,1},{3,2},{4,3},{5,4},{6,5},{7,6},{8,7},{9,8},{10,... | collective-permute-start | bytes 294920 | tf_op jit(solution)/shard_map/halo/ppermute | solution.py:310
  13.7 16.8 %all-to-all-start = ((bf16[64,8,128]{2,1,0:T(8,128)(2,1)}), bf16[64,8,128]{2,1,0:T(8,128)(2,1)S(1)}, u32[]{:S(2)}, u32[]{:S(2)}) async-start(bf16[64,8,128]{2,1,0:T(8,128)(2,1)} %get-tuple-element.16), calls=%async_computation | async-start | bytes 262144 | tf_op jit(solution)/shard_map/rotation_rows/all_to_all | solution.py:312
  34.3 4.2 %collective-permute-start.2 = (f32[2,384,128]{2,1,0:T(8,128)S(1)}, f32[2,384,128]{2,1,0:T(8,128)S(1)}, u32[]{:S(2)}, u32[]{:S(2)}) collective-permute-start(f32[2,384,128]{2,1,0:T(8,128)S(1)} %get-tuple-element.18), channel_id=1, source_target_pairs={{0,64},{64,0},{1,65},{65,1},{2,66},{66,2},{3,67},{67,3},{4,68},{68... | collective-permute-start | bytes 1179656 | tf_op jit(solution)/shard_map/sum_core/ppermute | solution.py:321
  72.7 5.3 %collective-permute-start.3 = (f32[2,384,128]{2,1,0:T(8,128)S(1)}, f32[2,384,128]{2,1,0:T(8,128)S(1)}, u32[]{:S(2)}, u32[]{:S(2)}) collective-permute-start(f32[2,384,128]{2,1,0:T(8,128)S(1)} %bitcast.5), channel_id=1, source_target_pairs={{0,64},{64,0},{1,65},{65,1},{2,66},{66,2},{3,67},{67,3},{4,68},{68... | collective-permute-start | bytes 1179656 | tf_op jit(solution)/shard_map/share_core/ppermute | solution.py:331

commit v4 on v3

--- a/solution.py
+++ b/solution.py
@@ -12,48 +12,44 @@
 BLOCK = 192
 PADDED = 8
 WEIGHT_FLOPS = 1_000_000_000
-EDGE_FLOPS = 10_000_000_000
+EDGE_FLOPS = 1_000_000_000
 TILE_AXES = ("x_hi", "z", "y")
 PLANE_AXES = ("x_lo", "x_hi", "y")
 CELL_AXES = ("x_lo", "core", "x_hi", "z", "y")
 VMEM = pl.BlockSpec(memory_space=pltpu.VMEM)
 HBM = pl.BlockSpec(memory_space=pltpu.HBM)
-PARAMS = pltpu.CompilerParams(vmem_limit_bytes=12 << 20)
+PARAMS = pltpu.CompilerParams(vmem_limit_bytes=16 << 20)
 
 
 def in_hbm(array):
     return pltpu.with_memory_space_constraint(array, pltpu.HBM)
 
 
-def start_kernel(snap, rot_hbm, first, last, spread_rot, rot, sems):
+def start_kernel(snap, rot, first, last, spread_rot, sems):
     cells = snap.shape[1]
+    rows = rot.shape[0]
     copies = [
-        pltpu.make_async_copy(rot_hbm, rot, sems.at[0]),
-        pltpu.make_async_copy(snap.at[:, pl.ds(0, HALO)], first, sems.at[1]),
-        pltpu.make_async_copy(snap.at[:, pl.ds(cells - HALO, HALO)], last, sems.at[2]),
-    ]
+        pltpu.make_async_copy(rot, spread_rot.at[tile, pl.ds(0, rows)], sems.at[tile])
+        for tile in range(spread_rot.shape[0])
+    ]
+    copies.append(pltpu.make_async_copy(snap.at[:, pl.ds(0, HALO)], first, sems.at[len(copies)]))
+    copies.append(pltpu.make_async_copy(snap.at[:, pl.ds(cells - HALO, HALO)], last, sems.at[len(copies)]))
     for copy in copies:
         copy.start()
-    copies[0].wait()
-    rows = rot.shape[0]
-    padding = jnp.zeros((PADDED - rows, rot.shape[1]), jnp.float32)
-    block = jnp.concatenate([rot[...].astype(jnp.float32), padding], axis=0).astype(jnp.bfloat16)
-    for tile in range(spread_rot.shape[0]):
-        spread_rot[tile] = block
-    for copy in copies[1:]:
+    for copy in copies:
         copy.wait()
 
 
 def start(snapshots, rotation, tiles):
     components, _, width = snapshots.shape
-    rows, modes = rotation.shape
+    modes = rotation.shape[1]
     edge = jax.ShapeDtypeStruct((components, HALO, width), jnp.bfloat16)
     return pl.pallas_call(
         start_kernel,
         out_shape=(edge, edge, jax.ShapeDtypeStruct((tiles, PADDED, modes), jnp.bfloat16)),
         in_specs=[HBM, HBM],
-        out_specs=(VMEM, VMEM, VMEM),
-        scratch_shapes=[pltpu.VMEM((rows, modes), jnp.bfloat16), pltpu.SemaphoreType.DMA((3,))],
+        out_specs=(VMEM, VMEM, HBM),
+        scratch_shapes=[pltpu.SemaphoreType.DMA((tiles + 2,))],
         compiler_params=PARAMS,
     )(snapshots, in_hbm(rotation))
 
@@ -85,9 +81,13 @@
 
 
 def weighting_kernel(
-    snap_hbm, dens_hbm, speed_hbm, offs_hbm, weighted, edge_scale, snap, dens, speed, offs, rows_ref, sems
+    snap_hbm, dens_hbm, speed_hbm, offs_hbm,
+    weighted_send, snap_send, weighted_keep, edge_scale,
+    snap, weighted, dens, speed, offs, rows_ref, sems,
 ):
     cells = snap.shape[1]
+    half = COMPONENTS // 2
+    sent = (1 - lax.axis_index("core")) * half
     vectors = ((dens_hbm, dens), (speed_hbm, speed), (offs_hbm, offs))
     small = [
         pltpu.make_async_copy(source, target, sems.at[COMPONENTS + i])
@@ -124,17 +124,25 @@
         )
         for component in range(COMPONENTS):
             weighted[component, begin:stop] = values[component]
+    keep = pltpu.make_async_copy(weighted.at[pl.ds(half - sent, half)], weighted_keep, sems.at[0])
+    keep.start()
+    for place in range(half):
+        weighted_send[place] = weighted[sent + place]
+        snap_send[place] = snap[sent + place]
+    keep.wait()
 
 
 def weigh(snapshots, density, sound_speed, offsets):
     components, cells, width = snapshots.shape
-    field = jax.ShapeDtypeStruct(snapshots.shape, jnp.bfloat16)
+    half = (components // 2, cells, width)
+    field = jax.ShapeDtypeStruct(half, jnp.bfloat16)
     return pl.pallas_call(
         weighting_kernel,
-        out_shape=(field, jax.ShapeDtypeStruct((2 * HALO, 8), jnp.float32)),
+        out_shape=(field, field, pltpu.HBM(half, jnp.bfloat16), jax.ShapeDtypeStruct((2 * HALO, 8), jnp.float32)),
         in_specs=[HBM] * 4,
-        out_specs=(VMEM, VMEM),
+        out_specs=(VMEM, VMEM, HBM, VMEM),
         scratch_shapes=[
+            pltpu.VMEM(snapshots.shape, jnp.bfloat16),
             pltpu.VMEM(snapshots.shape, jnp.bfloat16),
             pltpu.VMEM((1, cells), jnp.float32),
             pltpu.VMEM((1, cells), jnp.float32),
@@ -143,9 +151,7 @@
             pltpu.SemaphoreType.DMA((components + 3,)),
         ],
         compiler_params=PARAMS,
-        cost_estimate=pl.CostEstimate(
-            flops=WEIGHT_FLOPS, bytes_accessed=6_000_000, transcendentals=0
-        ),
+        cost_estimate=pl.CostEstimate(flops=WEIGHT_FLOPS, bytes_accessed=6_000_000, transcendentals=0),
     )(
         snapshots,
         in_hbm(density.reshape(1, cells)),
@@ -199,14 +205,17 @@
     )(snapshots, edge_scale, low, high)
 
 
-def projection_kernel(snap_hbm, weighted, edges, rot, keep, send, snap, sems):
-    cells, width = snap.shape[1:]
-    copies = [
-        pltpu.make_async_copy(snap_hbm.at[component], snap.at[component], sems.at[component])
-        for component in range(COMPONENTS)
-    ]
-    for copy in copies[:2]:
-        copy.start()
+def totals_of(rotation_t, snap, weighted, edges):
+    cells = snap.shape[0]
+    mode = lax.dot_general(
+        rotation_t, snap, (((1,), (1,)), ((), ())), preferred_element_type=jnp.float32
+    ).astype(jnp.bfloat16)
+    parts = [edges[0:HALO], weighted[HALO : cells - HALO], edges[HALO:]]
+    return jnp.dot(mode, jnp.concatenate(parts, axis=0), preferred_element_type=jnp.float32).T
+
+
+def sent_kernel(snap, weighted, edges, rot, send, rotation_t):
+    half, _, width = snap.shape
     tiles, padded, modes = rot.shape
     rows = width // tiles
     shape = (width, tiles * padded)
@@ -215,80 +224,104 @@
     within = source & (padded - 1)
     tile = (source - within) // padded
     chosen = jnp.logical_and(target == tile * rows + within, within < rows)
+    loaded = rot[...].reshape(tiles * padded, modes).astype(jnp.float32)
+    held = lax.broadcasted_iota(jnp.int32, loaded.shape, 0) & (padded - 1)
+    loaded = jnp.where(held < rows, loaded, 0.0).astype(jnp.bfloat16)
     compact = jnp.dot(
-        chosen.astype(jnp.float32).astype(jnp.bfloat16),
-        rot[...].reshape(tiles * padded, modes),
-        preferred_element_type=jnp.float32,
-    )
-    rotation_t = compact.T.astype(jnp.bfloat16)
-    core = lax.axis_index("core")
-    for component in range(COMPONENTS):
-        copies[component].wait()
-        if component + 2 < COMPONENTS:
-            copies[component + 2].start()
-        mode = lax.dot_general(
-            rotation_t,
-            snap[component],
-            (((1,), (1,)), ((), ())),
-            preferred_element_type=jnp.float32,
-        ).astype(jnp.bfloat16)
-        parts = [
-            edges[component, 0:HALO],
-            weighted[component, HALO : cells - HALO],
-            edges[component, HALO:],
-        ]
-        total = jnp.dot(mode, jnp.concatenate(parts, axis=0), preferred_element_type=jnp.float32).T
-        owner, place = divmod(component, 2)
-
-        @pl.when(core == owner)
-        def _():
-            keep[place] = total
-
-        @pl.when(core != owner)
-        def _():
-            send[place] = total
-
-
-def project(snapshots, weighted, edges, rotation):
-    components, _, width = snapshots.shape
-    half = jax.ShapeDtypeStruct((components // 2, width, rotation.shape[2]), jnp.float32)
-    return pl.pallas_call(
-        projection_kernel,
-        out_shape=(half, half),
-        in_specs=[HBM] + [VMEM] * 3,
+        chosen.astype(jnp.float32).astype(jnp.bfloat16), loaded, preferred_element_type=jnp.float32
+    )
+    turned = compact.T.astype(jnp.bfloat16)
+    rotation_t[...] = turned
+    sent = (1 - lax.axis_index("core")) * half
+    for place in range(half):
+        send[place] = totals_of(turned, snap[place], weighted[place], edges[sent + place])
+
+
+def project_sent(snap, weighted, edges, rotation):
+    half, _, width = snap.shape
+    modes = rotation.shape[2]
+    return pl.pallas_call(
+        sent_kernel,
+        out_shape=(
+            jax.ShapeDtypeStruct((half, width, modes), jnp.float32),
+            jax.ShapeDtypeStruct((modes, width), jnp.bfloat16),
+        ),
+        in_specs=[VMEM] * 4,
         out_specs=(VMEM, VMEM),
+        compiler_params=PARAMS,
+        cost_estimate=pl.CostEstimate(flops=400_000_000, bytes_accessed=3_000_000, transcendentals=0),
+    )(snap, weighted, edges, rotation)
+
+
+def kept_kernel(snap_hbm, weighted, edges, rotation_t, keep, snap, sems):
+    half = snap.shape[0]
+    kept = lax.axis_index("core") * half
+    copies = [
+        pltpu.make_async_copy(snap_hbm.at[kept + place], snap.at[place], sems.at[place])
+        for place in range(half)
+    ]
+    for copy in copies:
+        copy.start()
+    for place in range(half):
+        copies[place].wait()
+        keep[place] = totals_of(rotation_t[...], snap[place], weighted[place], edges[kept + place])
+
+
+def project_kept(snapshots, weighted, edges, rotation_t):
+    half, cells, width = weighted.shape
+    modes = rotation_t.shape[0]
+    return pl.pallas_call(
+        kept_kernel,
+        out_shape=jax.ShapeDtypeStruct((half, width, modes), jnp.float32),
+        in_specs=[HBM, VMEM, VMEM, VMEM],
+        out_specs=VMEM,
         scratch_shapes=[
-            pltpu.VMEM(snapshots.shape, jnp.bfloat16),
-            pltpu.SemaphoreType.DMA((components,)),
+            pltpu.VMEM(weighted.shape, jnp.bfloat16),
+            pltpu.SemaphoreType.DMA((half,)),
         ],
         compiler_params=PARAMS,
-        cost_estimate=pl.CostEstimate(flops=800_000_000, bytes_accessed=6_000_000, transcendentals=0),
-    )(snapshots, weighted, edges, rotation)
-
-
-def place_kernel(mine, other, out, sems):
-    core = lax.axis_index("core")
+        cost_estimate=pl.CostEstimate(flops=400_000_000, bytes_accessed=6_000_000, transcendentals=0),
+    )(snapshots, weighted, edges, rotation_t)
+
+
+def place_own_kernel(mine, out, sem):
     half = mine.shape[0]
-    copies = [
-        pltpu.make_async_copy(mine, out.at[pl.ds(core * half, half)], sems.at[0]),
-        pltpu.make_async_copy(other, out.at[pl.ds((1 - core) * half, half)], sems.at[1]),
-    ]
-    for copy in copies:
-        copy.start()
-    for copy in copies:
-        copy.wait()
-
-
-def place(mine, other):
+    copy = pltpu.make_async_copy(mine, out.at[pl.ds(lax.axis_index("core") * half, half)], sem)
+    copy.start()
+    copy.wait()
+
+
+def place_other_kernel(begun, other, out, sem):
+    half = other.shape[0]
+    copy = pltpu.make_async_copy(other, out.at[pl.ds((1 - lax.axis_index("core")) * half, half)], sem)
+    copy.start()
+    copy.wait()
+
+
+def place_own(mine):
     half, width, modes = mine.shape
     return pl.pallas_call(
-        place_kernel,
+        place_own_kernel,
         out_shape=jax.ShapeDtypeStruct((2 * half, width, modes), mine.dtype),
-        in_specs=[VMEM, VMEM],
+        in_specs=[VMEM],
         out_specs=HBM,
-        scratch_shapes=[pltpu.SemaphoreType.DMA((2,))],
-        compiler_params=PARAMS,
-    )(mine, other)
+        scratch_shapes=[pltpu.SemaphoreType.DMA],
+        compiler_params=PARAMS,
+        cost_estimate=pl.CostEstimate(flops=0, bytes_accessed=1_000_000, transcendentals=0),
+    )(mine)
+
+
+def place_other(begun, other):
+    return pl.pallas_call(
+        place_other_kernel,
+        out_shape=jax.ShapeDtypeStruct(begun.shape, begun.dtype),
+        in_specs=[HBM, VMEM],
+        out_specs=HBM,
+        scratch_shapes=[pltpu.SemaphoreType.DMA],
+        input_output_aliases={0: 0},
+        compiler_params=PARAMS,
+        cost_estimate=pl.CostEstimate(flops=0, bytes_accessed=1_000_000, transcendentals=0),
+    )(begun, other)
 
 
 def spread(block, axes):
@@ -311,14 +344,17 @@
     with jax.named_scope("rotation_rows"):
         full_rotation = lax.all_to_all(rows, TILE_AXES, 0, 0)
     with jax.named_scope("weighting"):
-        weighted, edge_scale = weigh(resident, density, sound_speed, offsets)
+        weighted_send, snap_send, weighted_keep, edge_scale = weigh(
+            resident, density, sound_speed, offsets
+        )
         edges = weigh_edges(resident, edge_scale, low, high)
     with jax.named_scope("projections"):
-        keep, send = project(resident, weighted, edges, full_rotation)
-    modes = keep.shape[2]
+        send, rotation_t = project_sent(snap_send, weighted_send, edges, full_rotation)
+        received = lax.ppermute(send, "core", swap)
+        keep = project_kept(resident, weighted_keep, edges, rotation_t)
+        mine = keep + received
+    modes = mine.shape[2]
     members = lax.axis_size(PLANE_AXES)
-    with jax.named_scope("sum_core"):
-        mine = keep + lax.ppermute(send, "core", swap)
     with jax.named_scope("sum_plane"):
         pieces = mine.reshape(members, components * width // (2 * members), modes)
         piece = jnp.sum(lax.all_to_all(pieces, PLANE_AXES, 0, 0), axis=0)
@@ -328,7 +364,8 @@
     with jax.named_scope("share_plane"):
         mine = spread(piece, PLANE_AXES).reshape(components // 2, width, modes)
     with jax.named_scope("share_core"):
-        return place(mine, lax.ppermute(mine, "core", swap))
+        other = lax.ppermute(mine, "core", swap)
+        return place_other(place_own(mine), other)
 
 
 def solution(mesh):

time: 79.3 us -> 82.9 us (1.045)
  waiting for transfers between devices: 9.38 us -> 0.6 us
  Pallas kernels: 11.1 us -> 16.6 us
  starting transfers between devices: 24.1 us -> 27.6 us
  blocking collectives: 34.1 us -> 37.5 us
    all_to_all x1, starting transfers between devices: 5.3 us -> 15.1 us  [on_device(): full_rotation = lax.all_to_all(rows, TILE_AXES, 0, 0)]
    all_to_all x1, waiting for transfers between devices: 6.68 us -> 0.01 us  [on_device(): full_rotation = lax.all_to_all(rows, TILE_AXES, 0, 0)]
    pallas_call x1, Pallas kernels: 1.64 us -> 4.69 us  [start(): pl.pallas_call(start_kernel, out_shape=(edge, edge, jax.ShapeDtypeStruct(...]
    ppermute x2, starting transfers between devices: 6.76 us -> 4.13 us  [the longest x1 4.04 us: on_device(): other = lax.ppermute(mine, 'core', swap)]
    ppermute x1, starting transfers between devices: 9.84 us -> 7.24 us  [on_device(): high = lax.ppermute(first, CELL_AXES, backward)]
    pallas_call x3 -> x5, Pallas kernels: 8.14 us -> 10.6 us  [the longest x1 5.32 us: weigh(): pl.pallas_call(weighting_kernel, out_shape=(field, field, pltpu.HBM(half,...]
    all_to_all x1, blocking collectives: 11.6 us -> 13.9 us  [on_device(): piece = jnp.sum(lax.all_to_all(pieces, PLANE_AXES, 0, 0), axis=0)]
    ppermute x2, waiting for transfers between devices: 2.7 us -> 0.59 us  [the longest x1 0.59 us: on_device(): other = lax.ppermute(mine, 'core', swap)]
  transfers between devices with their start and end apart: 5 -> 5, of which waited for: 3 -> 1; matrix products, arithmetic and copies ran while one was open for 0% -> 0% of each run, Pallas kernels for 6% -> 12%
where the time goes in v4:
time: 82.9 us; the launch traced here: 82.6 us
  blocking collectives  37.5 us (45%)
  starting transfers between devices  27.6 us (33%)
  Pallas kernels  16.6 us (20%)
    all_to_all x2, blocking collectives, spread(): lax.all_to_all(jnp.broadcast_to(block[None], (count,) + block.shape), axe...  23.6 us
    all_to_all x1, starting transfers between devices, on_device(): full_rotation = lax.all_to_all(rows, TILE_AXES, 0, 0)  15.1 us
    all_to_all x1, blocking collectives, on_device(): piece = jnp.sum(lax.all_to_all(pieces, PLANE_AXES, 0, 0), axis=0)  13.9 us
    ppermute x1, starting transfers between devices, on_device(): high = lax.ppermute(first, CELL_AXES, backward)  7.24 us
    pallas_call x1, Pallas kernels, weigh(): pl.pallas_call(weighting_kernel, out_shape=(field, field, pltpu.HBM(half,...  5.32 us
    pallas_call x1, Pallas kernels, start(): pl.pallas_call(start_kernel, out_shape=(edge, edge, jax.ShapeDtypeStruct(...  4.69 us
    ppermute x1, starting transfers between devices, on_device(): other = lax.ppermute(mine, 'core', swap)  4.04 us
    pallas_call x1, Pallas kernels, project_kept(): pl.pallas_call(kept_kernel, out_shape=jax.ShapeDtypeStruct((half, width,...  2.42 us
  transfers between devices with their start and end apart: 5, of which 1 were waited for; matrix products, arithmetic and copies ran while one was open for 0% of the time, Pallas kernels for 12%

profile of v4, /device:TPU:1, one launch (start us, length us, event | category | flops | bytes accessed | tf_op | source)
XLA Modules:
  0.0 82.6 jit_solution(5949255631885739708)
XLA Ops:
  0.0 4.7 %start.1 = (bf16[4,32,384]{2,1,0:T(8,128)(2,1)S(1)}, bf16[4,32,384]{2,1,0:T(8,128)(2,1)S(1)}, bf16[64,8,128]{2,1,0:T(8,128)(2,1)}) custom-call(bf16[4,960,384]{2,1,0:T(8,128)(2,1)} %snap_hbm.5, bf16[6,128]{1,0:T(8,128)(2,1)} %rot.1), custom_call_target="tpu_custom_call" | custom-call | tf_op jit(solution)/shard_map/start/pallas_call | solution.py:47
  4.7 15.1 %all-to-all-start = ((bf16[64,8,128]{2,1,0:T(8,128)(2,1)}), bf16[64,8,128]{2,1,0:T(8,128)(2,1)S(1)}, u32[]{:S(2)}, u32[]{:S(2)}) async-start(bf16[64,8,128]{2,1,0:T(8,128)(2,1)} %get-tuple-element.20), calls=%async_computation | async-start | bytes 262144 | tf_op jit(solution)/shard_map/rotation_rows/all_to_all | solution.py:345
  19.8 1.1 %collective-permute-start = (bf16[4,32,384]{2,1,0:T(8,128)(2,1)S(1)}, bf16[4,32,384]{2,1,0:T(8,128)(2,1)S(1)}, u32[]{:S(2)}, u32[]{:S(2)}) collective-permute-start(bf16[4,32,384]{2,1,0:T(8,128)(2,1)S(1)} %get-tuple-element.16), channel_id=1, source_target_pairs={{0,1},{1,2},{2,3},{3,4},{4,5},{5,6},{6,7},{7,8},{8,9},{9,10},{10,1... | collective-permute-start | bytes 294920 | tf_op jit(solution)/shard_map/halo/ppermute | solution.py:342
  20.9 7.2 %collective-permute-start.1 = (bf16[4,32,384]{2,1,0:T(8,128)(2,1)S(1)}, bf16[4,32,384]{2,1,0:T(8,128)(2,1)S(1)}, u32[]{:S(2)}, u32[]{:S(2)}) collective-permute-start(bf16[4,32,384]{2,1,0:T(8,128)(2,1)S(1)} %get-tuple-element.17), channel_id=1, source_target_pairs={{0,255},{1,0},{2,1},{3,2},{4,3},{5,4},{6,5},{7,6},{8,7},{9,8},{10,... | collective-permute-start | bytes 294920 | tf_op jit(solution)/shard_map/halo/ppermute | solution.py:343
  28.2 5.3 %weighting.2 = (bf16[2,960,384]{2,1,0:T(8,128)(2,1)S(1)}, bf16[2,960,384]{2,1,0:T(8,128)(2,1)S(1)}, bf16[2,960,384]{2,1,0:T(8,128)(2,1)}, f32[64,8]{1,0:T(8,128)S(1)}) custom-call(bf16[4,960,384]{2,1,0:T(8,128)(2,1)} %snap_hbm.5, f32[1,960]{1,0:T(1,128)} %bitcast.8, f32[1,960]{1,0:T(1,128)} %bitcast.9, s32[1,960]{1,0:T(1,128)} %bitcast.10), custom_call_target="tpu_custom_call" | custom-call | flops 1000000000 | bytes 6000000 | tf_op jit(solution)/shard_map/weighting/pallas_call | solution.py:139
  33.5 0.0 collective-permute-done.low
  33.5 0.0 collective-permute-done.1.high
  33.5 1.3 %weighting.3.edges = bf16[4,64,384]{2,1,0:T(8,128)(2,1)S(1)} custom-call(bf16[4,960,384]{2,1,0:T(8,128)(2,1)} %snap_hbm.5, f32[64,8]{1,0:T(8,128)S(1)} %get-tuple-element.15.edge_scale, bf16[4,32,384]{2,1,0:T(8,128)(2,1)S(1)} %collective-permute-done.low, bf16[4,32,384]{2,1,0:T(8,128)(2,1)S(1)} %collective-permute-done.1.high), custom_call_target="tpu_custom_call" | custom-call | flops 1000000000 | bytes 600000 | tf_op jit(solution)/shard_map/weighting/pallas_call | solution.py:193
  34.9 0.0 all-to-all-done.rot
  34.9 0.0 copy-start
  34.9 1.4 %projections.2 = (f32[2,384,128]{2,1,0:T(8,128)S(1)}, bf16[128,384]{1,0:T(8,128)(2,1)S(1)}) custom-call(bf16[2,960,384]{2,1,0:T(8,128)(2,1)S(1)} %get-tuple-element.18.snap, bf16[2,960,384]{2,1,0:T(8,128)(2,1)S(1)} %get-tuple-element.19.weighted, bf16[4,64,384]{2,1,0:T(8,128)(2,1)S(1)} %weighting.3.edges, bf16[64,8,128]{2,1,0:T(8,128)(2,1)S(1)} %all-to-all-done.rot), custom_call_target="tpu_custom_call" | custom-call | flops 400000000 | bytes 3000000 | tf_op jit(solution)/shard_map/projections/pallas_call | solution.py:243
  36.3 0.1 collective-permute-start.2
  36.4 0.0 copy-done
  36.4 2.4 %projections.3 = f32[2,384,128]{2,1,0:T(8,128)S(1)} custom-call(bf16[4,960,384]{2,1,0:T(8,128)(2,1)} %snap_hbm.5, bf16[2,960,384]{2,1,0:T(8,128)(2,1)S(1)} %copy-done, bf16[4,64,384]{2,1,0:T(8,128)(2,1)S(1)} %weighting.3.edges, bf16[128,384]{1,0:T(8,128)(2,1)S(1)} %get-tuple-element.21.rotation_t), custom_call_target="tpu_custom_call" | custom-call | flops 400000000 | bytes 6000000 | tf_op jit(solution)/shard_map/projections/pallas_call | solution.py:273
  38.8 0.0 collective-permute-done.2
  38.9 13.9 %all_to_all.20 = f32[16,48,128]{2,1,0:T(8,128)S(1)} all-to-all(f32[16,48,128]{2,1,0:T(8,128)S(1)} %bitcast.7), channel_id=1, replica_groups=mesh['x_lo'=2,'core'=2,'x_hi'=2,'z'=8,'y'=4] {'x_lo','x_hi','y'}, dimensions={0} | all-to-all | bytes 786432 | tf_op jit(solution)/shard_map/sum_plane/all_to_all | solution.py:360
  52.8 12.4 %all_to_all.21 = f32[8,48,128]{2,1,0:T(8,128)S(1)} all-to-all(f32[8,48,128]{2,1,0:T(8,128)S(1)} %broadcast_in_dim.4), channel_id=1, replica_groups=mesh['x_lo'=2,'core'=2,'x_hi'=2,'z'=8,'y'=4] {'z'}, dimensions={0} | all-to-all | bytes 393216 | tf_op jit(solution)/shard_map/sum_z/all_to_all | solution.py:329
  65.3 11.1 %all_to_all.22 = f32[16,48,128]{2,1,0:T(8,128)S(1)} all-to-all(f32[16,48,128]{2,1,0:T(8,128)S(1)} %broadcast_in_dim.5), channel_id=1, replica_groups=mesh['x_lo'=2,'core'=2,'x_hi'=2,'z'=8,'y'=4] {'x_lo','x_hi','y'}, dimensions={0} | all-to-all | bytes 786432 | tf_op jit(solution)/shard_map/share_plane/all_to_all | solution.py:329
  76.5 4.0 %collective-permute-start.3 = (f32[2,384,128]{2,1,0:T(8,128)S(1)}, f32[2,384,128]{2,1,0:T(8,128)S(1)}, u32[]{:S(2)}, u32[]{:S(2)}) collective-permute-start(f32[2,384,128]{2,1,0:T(8,128)S(1)} %bitcast.5), channel_id=1, source_target_pairs={{0,64},{64,0},{1,65},{65,1},{2,66},{66,2},{3,67},{67,3},{4,68},{68... | collective-permute-start | bytes 1179656 | tf_op jit(solution)/shard_map/share_core/ppermute | solution.py:367
  80.5 0.8 share_core.2.begun
  81.3 0.6 collective-permute-done.3.other
  81.8 0.8 share_core.3
  (6 shorter events, 0.1 us)
Async XLA Ops:
  4.7 30.2 %all-to-all-start = ((bf16[64,8,128]{2,1,0:T(8,128)(2,1)}), bf16[64,8,128]{2,1,0:T(8,128)(2,1)S(1)}, u32[]{:S(2)}, u32[]{:S(2)}) async-start(bf16[64,8,128]{2,1,0:T(8,128)(2,1)} %get-tuple-element.20), calls=%async_computation | async-start | bytes 262144 | tf_op jit(solution)/shard_map/rotation_rows/all_to_all | solution.py:345
  19.8 13.7 %collective-permute-start = (bf16[4,32,384]{2,1,0:T(8,128)(2,1)S(1)}, bf16[4,32,384]{2,1,0:T(8,128)(2,1)S(1)}, u32[]{:S(2)}, u32[]{:S(2)}) collective-permute-start(bf16[4,32,384]{2,1,0:T(8,128)(2,1)S(1)} %get-tuple-element.16), channel_id=1, source_target_pairs={{0,1},{1,2},{2,3},{3,4},{4,5},{5,6},{6,7},{7,8},{8,9},{9,10},{10,1... | collective-permute-start | bytes 294920 | tf_op jit(solution)/shard_map/halo/ppermute | solution.py:342
  20.9 12.6 %collective-permute-start.1 = (bf16[4,32,384]{2,1,0:T(8,128)(2,1)S(1)}, bf16[4,32,384]{2,1,0:T(8,128)(2,1)S(1)}, u32[]{:S(2)}, u32[]{:S(2)}) collective-permute-start(bf16[4,32,384]{2,1,0:T(8,128)(2,1)S(1)} %get-tuple-element.17), channel_id=1, source_target_pairs={{0,255},{1,0},{2,1},{3,2},{4,3},{5,4},{6,5},{7,6},{8,7},{9,8},{10,... | collective-permute-start | bytes 294920 | tf_op jit(solution)/shard_map/halo/ppermute | solution.py:343
  34.9 1.5 %copy-start = (bf16[2,960,384]{2,1,0:T(8,128)(2,1)S(1)}, bf16[2,960,384]{2,1,0:T(8,128)(2,1)}, u32[]{:S(2)}) copy-start(bf16[2,960,384]{2,1,0:T(8,128)(2,1)} %get-tuple-element.14.weighted) | copy-start | bytes 4423684
  36.3 2.5 %collective-permute-start.2 = (f32[2,384,128]{2,1,0:T(8,128)S(1)}, f32[2,384,128]{2,1,0:T(8,128)S(1)}, u32[]{:S(2)}, u32[]{:S(2)}) collective-permute-start(f32[2,384,128]{2,1,0:T(8,128)S(1)} %get-tuple-element.22), channel_id=1, source_target_pairs={{0,64},{64,0},{1,65},{65,1},{2,66},{66,2},{3,67},{67,3},{4,68},{68... | collective-permute-start | bytes 1179656 | tf_op jit(solution)/shard_map/projections/ppermute | solution.py:353
  76.5 5.4 %collective-permute-start.3 = (f32[2,384,128]{2,1,0:T(8,128)S(1)}, f32[2,384,128]{2,1,0:T(8,128)S(1)}, u32[]{:S(2)}, u32[]{:S(2)}) collective-permute-start(f32[2,384,128]{2,1,0:T(8,128)S(1)} %bitcast.5), channel_id=1, source_target_pairs={{0,64},{64,0},{1,65},{65,1},{2,66},{66,2},{3,67},{67,3},{4,68},{68... | collective-permute-start | bytes 1179656 | tf_op jit(solution)/shard_map/share_core/ppermute | solution.py:367

commit v5 on v4

--- a/solution.py
+++ b/solution.py
@@ -25,31 +25,35 @@
     return pltpu.with_memory_space_constraint(array, pltpu.HBM)
 
 
-def start_kernel(snap, rot, first, last, spread_rot, sems):
+def start_kernel(snap, rot_hbm, first, last, spread_rot, rot, sems):
     cells = snap.shape[1]
-    rows = rot.shape[0]
     copies = [
-        pltpu.make_async_copy(rot, spread_rot.at[tile, pl.ds(0, rows)], sems.at[tile])
-        for tile in range(spread_rot.shape[0])
+        pltpu.make_async_copy(rot_hbm, rot, sems.at[0]),
+        pltpu.make_async_copy(snap.at[:, pl.ds(0, HALO)], first, sems.at[1]),
+        pltpu.make_async_copy(snap.at[:, pl.ds(cells - HALO, HALO)], last, sems.at[2]),
     ]
-    copies.append(pltpu.make_async_copy(snap.at[:, pl.ds(0, HALO)], first, sems.at[len(copies)]))
-    copies.append(pltpu.make_async_copy(snap.at[:, pl.ds(cells - HALO, HALO)], last, sems.at[len(copies)]))
     for copy in copies:
         copy.start()
-    for copy in copies:
+    copies[0].wait()
+    rows = rot.shape[0]
+    padding = jnp.zeros((PADDED - rows, rot.shape[1]), jnp.float32)
+    block = jnp.concatenate([rot[...].astype(jnp.float32), padding], axis=0).astype(jnp.bfloat16)
+    for tile in range(spread_rot.shape[0]):
+        spread_rot[tile] = block
+    for copy in copies[1:]:
         copy.wait()
 
 
 def start(snapshots, rotation, tiles):
     components, _, width = snapshots.shape
-    modes = rotation.shape[1]
+    rows, modes = rotation.shape
     edge = jax.ShapeDtypeStruct((components, HALO, width), jnp.bfloat16)
     return pl.pallas_call(
         start_kernel,
         out_shape=(edge, edge, jax.ShapeDtypeStruct((tiles, PADDED, modes), jnp.bfloat16)),
         in_specs=[HBM, HBM],
-        out_specs=(VMEM, VMEM, HBM),
-        scratch_shapes=[pltpu.SemaphoreType.DMA((tiles + 2,))],
+        out_specs=(VMEM, VMEM, VMEM),
+        scratch_shapes=[pltpu.VMEM((rows, modes), jnp.bfloat16), pltpu.SemaphoreType.DMA((3,))],
         compiler_params=PARAMS,
     )(snapshots, in_hbm(rotation))
 
@@ -82,21 +86,21 @@
 
 def weighting_kernel(
     snap_hbm, dens_hbm, speed_hbm, offs_hbm,
-    weighted_send, snap_send, weighted_keep, edge_scale,
-    snap, weighted, dens, speed, offs, rows_ref, sems,
+    weighted, edge_scale, begin_rim, end_rim,
+    snap, dens, speed, offs, rows_ref, sems,
 ):
     cells = snap.shape[1]
-    half = COMPONENTS // 2
-    sent = (1 - lax.axis_index("core")) * half
+    starts = list(range(0, cells, BLOCK))
+    bounds = [0] + [start + HALO for start in starts[1:]] + [cells]
     vectors = ((dens_hbm, dens), (speed_hbm, speed), (offs_hbm, offs))
     small = [
-        pltpu.make_async_copy(source, target, sems.at[COMPONENTS + i])
+        pltpu.make_async_copy(source, target, sems.at[len(starts) + i])
         for i, (source, target) in enumerate(vectors)
     ]
-    copies = [
-        pltpu.make_async_copy(snap_hbm.at[component], snap.at[component], sems.at[component])
-        for component in range(COMPONENTS)
-    ]
+    copies = []
+    for i in range(len(starts)):
+        rows = pl.ds(bounds[i], bounds[i + 1] - bounds[i])
+        copies.append(pltpu.make_async_copy(snap_hbm.at[:, rows], snap.at[:, rows], sems.at[i]))
     for copy in small + copies:
         copy.start()
     for copy in small:
@@ -111,11 +115,10 @@
     columns = rows_ref[...].T
     edge_scale[0:HALO] = columns[0:HALO]
     edge_scale[HALO:] = columns[cells - HALO : cells]
-    for copy in copies:
-        copy.wait()
-    for begin in range(0, cells, BLOCK):
+    for i, begin in enumerate(starts):
+        copies[i].wait()
         stop = begin + BLOCK
-        low, high = max(begin - HALO, 0), min(stop + HALO, cells)
+        low, high = max(begin - HALO, 0), min(stop + HALO, bounds[i + 1])
         values = weigh_rows(
             columns[begin:stop],
             begin - low,
@@ -124,31 +127,30 @@
         )
         for component in range(COMPONENTS):
             weighted[component, begin:stop] = values[component]
-    keep = pltpu.make_async_copy(weighted.at[pl.ds(half - sent, half)], weighted_keep, sems.at[0])
-    keep.start()
-    for place in range(half):
-        weighted_send[place] = weighted[sent + place]
-        snap_send[place] = snap[sent + place]
-    keep.wait()
+    begin_rim[...] = snap[:, 0 : 2 * HALO]
+    end_rim[...] = snap[:, cells - 2 * HALO :]
 
 
 def weigh(snapshots, density, sound_speed, offsets):
     components, cells, width = snapshots.shape
-    half = (components // 2, cells, width)
-    field = jax.ShapeDtypeStruct(half, jnp.bfloat16)
+    rim = jax.ShapeDtypeStruct((components, 2 * HALO, width), jnp.bfloat16)
     return pl.pallas_call(
         weighting_kernel,
-        out_shape=(field, field, pltpu.HBM(half, jnp.bfloat16), jax.ShapeDtypeStruct((2 * HALO, 8), jnp.float32)),
+        out_shape=(
+            jax.ShapeDtypeStruct(snapshots.shape, jnp.bfloat16),
+            jax.ShapeDtypeStruct((2 * HALO, 8), jnp.float32),
+            rim,
+            rim,
+        ),
         in_specs=[HBM] * 4,
-        out_specs=(VMEM, VMEM, HBM, VMEM),
+        out_specs=(VMEM,) * 4,
         scratch_shapes=[
-            pltpu.VMEM(snapshots.shape, jnp.bfloat16),
             pltpu.VMEM(snapshots.shape, jnp.bfloat16),
             pltpu.VMEM((1, cells), jnp.float32),
             pltpu.VMEM((1, cells), jnp.float32),
             pltpu.VMEM((1, cells), jnp.int32),
             pltpu.VMEM((8, 1024), jnp.float32),
-            pltpu.SemaphoreType.DMA((components + 3,)),
+            pltpu.SemaphoreType.DMA((cells // BLOCK + 3,)),
         ],
         compiler_params=PARAMS,
         cost_estimate=pl.CostEstimate(flops=WEIGHT_FLOPS, bytes_accessed=6_000_000, transcendentals=0),
@@ -160,16 +162,7 @@
     )
 
 
-def edge_kernel(snap_hbm, edge_scale, low, high, edges, begin, end, sems):
-    cells = snap_hbm.shape[1]
-    copies = [
-        pltpu.make_async_copy(snap_hbm.at[:, pl.ds(0, 2 * HALO)], begin, sems.at[0]),
-        pltpu.make_async_copy(snap_hbm.at[:, pl.ds(cells - 2 * HALO, 2 * HALO)], end, sems.at[1]),
-    ]
-    for copy in copies:
-        copy.start()
-    for copy in copies:
-        copy.wait()
+def edge_kernel(begin, end, edge_scale, low, high, edges):
     first = weigh_rows(
         edge_scale[0:HALO],
         HALO,
@@ -187,22 +180,15 @@
         edges[component, HALO:] = last[component]
 
 
-def weigh_edges(snapshots, edge_scale, low, high):
-    components, _, width = snapshots.shape
-    rim = (components, 2 * HALO, width)
+def weigh_edges(begin, end, edge_scale, low, high):
     return pl.pallas_call(
         edge_kernel,
-        out_shape=jax.ShapeDtypeStruct(rim, jnp.bfloat16),
-        in_specs=[HBM, VMEM, VMEM, VMEM],
+        out_shape=jax.ShapeDtypeStruct(begin.shape, jnp.bfloat16),
+        in_specs=[VMEM] * 5,
         out_specs=VMEM,
-        scratch_shapes=[
-            pltpu.VMEM(rim, jnp.bfloat16),
-            pltpu.VMEM(rim, jnp.bfloat16),
-            pltpu.SemaphoreType.DMA((2,)),
-        ],
         compiler_params=PARAMS,
         cost_estimate=pl.CostEstimate(flops=EDGE_FLOPS, bytes_accessed=600_000, transcendentals=0),
-    )(snapshots, edge_scale, low, high)
+    )(begin, end, edge_scale, low, high)
 
 
 def totals_of(rotation_t, snap, weighted, edges):
@@ -214,8 +200,17 @@
     return jnp.dot(mode, jnp.concatenate(parts, axis=0), preferred_element_type=jnp.float32).T
 
 
-def sent_kernel(snap, weighted, edges, rot, send, rotation_t):
+def sent_kernel(snap_hbm, weighted, edges, rot, send, rotation_t, snap_keep, snap, sems):
     half, _, width = snap.shape
+    kept = lax.axis_index("core") * half
+    sent = half - kept
+    copies = [
+        pltpu.make_async_copy(snap_hbm.at[sent + place], snap.at[place], sems.at[place])
+        for place in range(half)
+    ]
+    copies.append(pltpu.make_async_copy(snap_hbm.at[pl.ds(kept, half)], snap_keep, sems.at[half]))
+    for copy in copies:
+        copy.start()
     tiles, padded, modes = rot.shape
     rows = width // tiles
     shape = (width, tiles * padded)
@@ -224,64 +219,61 @@
     within = source & (padded - 1)
     tile = (source - within) // padded
     chosen = jnp.logical_and(target == tile * rows + within, within < rows)
-    loaded = rot[...].reshape(tiles * padded, modes).astype(jnp.float32)
-    held = lax.broadcasted_iota(jnp.int32, loaded.shape, 0) & (padded - 1)
-    loaded = jnp.where(held < rows, loaded, 0.0).astype(jnp.bfloat16)
     compact = jnp.dot(
-        chosen.astype(jnp.float32).astype(jnp.bfloat16), loaded, preferred_element_type=jnp.float32
+        chosen.astype(jnp.float32).astype(jnp.bfloat16),
+        rot[...].reshape(tiles * padded, modes),
+        preferred_element_type=jnp.float32,
     )
     turned = compact.T.astype(jnp.bfloat16)
     rotation_t[...] = turned
-    sent = (1 - lax.axis_index("core")) * half
     for place in range(half):
-        send[place] = totals_of(turned, snap[place], weighted[place], edges[sent + place])
-
-
-def project_sent(snap, weighted, edges, rotation):
-    half, _, width = snap.shape
+        copies[place].wait()
+        send[place] = totals_of(turned, snap[place], weighted.at[sent + place], edges.at[sent + place])
+    copies[half].wait()
+
+
+def project_sent(snapshots, weighted, edges, rotation):
+    components, cells, width = snapshots.shape
+    half = (components // 2, cells, width)
     modes = rotation.shape[2]
     return pl.pallas_call(
         sent_kernel,
         out_shape=(
-            jax.ShapeDtypeStruct((half, width, modes), jnp.float32),
+            jax.ShapeDtypeStruct((components // 2, width, modes), jnp.float32),
             jax.ShapeDtypeStruct((modes, width), jnp.bfloat16),
+            jax.ShapeDtypeStruct(half, jnp.bfloat16),
         ),
-        in_specs=[VMEM] * 4,
-        out_specs=(VMEM, VMEM),
+        in_specs=[HBM, VMEM, VMEM, VMEM],
+        out_specs=(VMEM, VMEM, VMEM),
+        scratch_shapes=[
+            pltpu.VMEM(half, jnp.bfloat16),
+            pltpu.SemaphoreType.DMA((components // 2 + 1,)),
+        ],
         compiler_params=PARAMS,
         cost_estimate=pl.CostEstimate(flops=400_000_000, bytes_accessed=3_000_000, transcendentals=0),
-    )(snap, weighted, edges, rotation)
-
-
-def kept_kernel(snap_hbm, weighted, edges, rotation_t, keep, snap, sems):
+    )(snapshots, weighted, edges, rotation)
+
+
+def kept_kernel(snap, weighted, edges, rotation_t, keep):
     half = snap.shape[0]
     kept = lax.axis_index("core") * half
-    copies = [
-        pltpu.make_async_copy(snap_hbm.at[kept + place], snap.at[place], sems.at[place])
-        for place in range(half)
-    ]
-    for copy in copies:
-        copy.start()
     for place in range(half):
-        copies[place].wait()
-        keep[place] = totals_of(rotation_t[...], snap[place], weighted[place], edges[kept + place])
-
-
-def project_kept(snapshots, weighted, edges, rotation_t):
-    half, cells, width = weighted.shape
+        keep[place] = totals_of(
+            rotation_t[...], snap[place], weighted.at[kept + place], edges.at[kept + place]
+        )
+
+
+def project_kept(snap, weighted, edges, rotation_t):
+    half, _, width = snap.shape
     modes = rotation_t.shape[0]
     return pl.pallas_call(
         kept_kernel,
         out_shape=jax.ShapeDtypeStruct((half, width, modes), jnp.float32),
-        in_specs=[HBM, VMEM, VMEM, VMEM],
+        in_specs=[VMEM] * 4,
         out_specs=VMEM,
-        scratch_shapes=[
-            pltpu.VMEM(weighted.shape, jnp.bfloat16),
-            pltpu.SemaphoreType.DMA((half,)),
-        ],
-        compiler_params=PARAMS,
-        cost_estimate=pl.CostEstimate(flops=400_000_000, bytes_accessed=6_000_000, transcendentals=0),
-    )(snapshots, weighted, edges, rotation_t)
+        compiler_params=PARAMS,
+        cost_estimate=pl.CostEstimate(flops=400_000_000, bytes_accessed=3_000_000, transcendentals=0),
+    )(snap, weighted, edges, rotation_t)
 
 
 def place_own_kernel(mine, out, sem):
@@ -344,14 +336,12 @@
     with jax.named_scope("rotation_rows"):
         full_rotation = lax.all_to_all(rows, TILE_AXES, 0, 0)
     with jax.named_scope("weighting"):
-        weighted_send, snap_send, weighted_keep, edge_scale = weigh(
-            resident, density, sound_speed, offsets
-        )
-        edges = weigh_edges(resident, edge_scale, low, high)
+        weighted, edge_scale, begin, end = weigh(resident, density, sound_speed, offsets)
+        edges = weigh_edges(begin, end, edge_scale, low, high)
     with jax.named_scope("projections"):
-        send, rotation_t = project_sent(snap_send, weighted_send, edges, full_rotation)
+        send, rotation_t, snap_keep = project_sent(resident, weighted, edges, full_rotation)
         received = lax.ppermute(send, "core", swap)
-        keep = project_kept(resident, weighted_keep, edges, rotation_t)
+        keep = project_kept(snap_keep, weighted, edges, rotation_t)
         mine = keep + received
     modes = mine.shape[2]
     members = lax.axis_size(PLANE_AXES)

time: 82.9 us -> 78.8 us (0.951)
  Pallas kernels: 16.6 us -> 10.6 us
  starting transfers between devices: 27.6 us -> 29 us
  waiting for transfers between devices: 0.6 us -> 1.8 us
    pallas_call x1, Pallas kernels: 4.69 us -> 1.64 us  [start(): pl.pallas_call(start_kernel, out_shape=(edge, edge, jax.ShapeDtypeStruct(...]
    all_to_all x1, blocking collectives: 13.9 us -> 11.8 us  [on_device(): piece = jnp.sum(lax.all_to_all(pieces, PLANE_AXES, 0, 0), axis=0)]
    pallas_call x3, Pallas kernels: 8.03 us -> 6.39 us  [the longest x1 3.58 us: weigh(): pl.pallas_call(weighting_kernel, out_shape=(jax.ShapeDtypeStruct(snapshot...]
    all_to_all x2, blocking collectives: 23.6 us -> 25 us  [spread(): lax.all_to_all(jnp.broadcast_to(block[None], (count,) + block.shape), axe...]
    pallas_call x1, Pallas kernels: 2.42 us -> 1.05 us  [project_kept(): pl.pallas_call(kept_kernel, out_shape=jax.ShapeDtypeStruct((half, width,...]
    ppermute x1, waiting for transfers between devices: 0.01 us -> 0.91 us  [on_device(): low = lax.ppermute(last, CELL_AXES, forward)]
  transfers between devices with their start and end apart: 5 -> 5, of which waited for: 1 -> 3; matrix products, arithmetic and copies ran while one was open for 0% -> 0% of each run, Pallas kernels for 12% -> 7%
where the time goes in v5:
time: 78.8 us; the launch traced here: 78.4 us
  blocking collectives  36.8 us (47%)
  starting transfers between devices  29 us (37%)
  Pallas kernels  10.6 us (13%)
  waiting for transfers between devices  1.8 us (2%)
    all_to_all x2, blocking collectives, spread(): lax.all_to_all(jnp.broadcast_to(block[None], (count,) + block.shape), axe...  25 us
    all_to_all x1, starting transfers between devices, on_device(): full_rotation = lax.all_to_all(rows, TILE_AXES, 0, 0)  15.1 us
    all_to_all x1, blocking collectives, on_device(): piece = jnp.sum(lax.all_to_all(pieces, PLANE_AXES, 0, 0), axis=0)  11.8 us
    ppermute x1, starting transfers between devices, on_device(): high = lax.ppermute(first, CELL_AXES, backward)  7.24 us
    ppermute x1, starting transfers between devices, on_device(): other = lax.ppermute(mine, 'core', swap)  4.68 us
    pallas_call x1, Pallas kernels, weigh(): pl.pallas_call(weighting_kernel, out_shape=(jax.ShapeDtypeStruct(snapshot...  3.58 us
    pallas_call x1, Pallas kernels, project_sent(): pl.pallas_call(sent_kernel, out_shape=(jax.ShapeDtypeStruct((components /...  2.53 us
    pallas_call x1, Pallas kernels, start(): pl.pallas_call(start_kernel, out_shape=(edge, edge, jax.ShapeDtypeStruct(...  1.64 us
  transfers between devices with their start and end apart: 5, of which 3 were waited for; matrix products, arithmetic and copies ran while one was open for 0% of the time, Pallas kernels for 7%

profile of v5, /device:TPU:1, one launch (start us, length us, event | category | flops | bytes accessed | tf_op | source)
XLA Modules:
  0.0 78.4 jit_solution(16013956658400609558)
XLA Ops:
  0.0 1.6 %start.1 = (bf16[4,32,384]{2,1,0:T(8,128)(2,1)S(1)}, bf16[4,32,384]{2,1,0:T(8,128)(2,1)S(1)}, bf16[64,8,128]{2,1,0:T(8,128)(2,1)}) custom-call(bf16[4,960,384]{2,1,0:T(8,128)(2,1)} %snap_hbm.3, bf16[6,128]{1,0:T(8,128)(2,1)} %rot_hbm.1), custom_call_target="tpu_custom_call" | custom-call | tf_op jit(solution)/shard_map/start/pallas_call | solution.py:51
  1.6 15.1 %all-to-all-start = ((bf16[64,8,128]{2,1,0:T(8,128)(2,1)}), bf16[64,8,128]{2,1,0:T(8,128)(2,1)S(1)}, u32[]{:S(2)}, u32[]{:S(2)}) async-start(bf16[64,8,128]{2,1,0:T(8,128)(2,1)} %get-tuple-element.21), calls=%async_computation | async-start | bytes 262144 | tf_op jit(solution)/shard_map/rotation_rows/all_to_all | solution.py:337
  16.8 1.1 %collective-permute-start = (bf16[4,32,384]{2,1,0:T(8,128)(2,1)S(1)}, bf16[4,32,384]{2,1,0:T(8,128)(2,1)S(1)}, u32[]{:S(2)}, u32[]{:S(2)}) collective-permute-start(bf16[4,32,384]{2,1,0:T(8,128)(2,1)S(1)} %get-tuple-element.19), channel_id=1, source_target_pairs={{0,1},{1,2},{2,3},{3,4},{4,5},{5,6},{6,7},{7,8},{8,9},{9,10},{10,1... | collective-permute-start | bytes 294920 | tf_op jit(solution)/shard_map/halo/ppermute | solution.py:334
  17.9 7.2 %collective-permute-start.1 = (bf16[4,32,384]{2,1,0:T(8,128)(2,1)S(1)}, bf16[4,32,384]{2,1,0:T(8,128)(2,1)S(1)}, u32[]{:S(2)}, u32[]{:S(2)}) collective-permute-start(bf16[4,32,384]{2,1,0:T(8,128)(2,1)S(1)} %get-tuple-element.20), channel_id=1, source_target_pairs={{0,255},{1,0},{2,1},{3,2},{4,3},{5,4},{6,5},{7,6},{8,7},{9,8},{10,... | collective-permute-start | bytes 294920 | tf_op jit(solution)/shard_map/halo/ppermute | solution.py:335
  25.1 3.6 %weighting.2 = (bf16[4,960,384]{2,1,0:T(8,128)(2,1)S(1)}, f32[64,8]{1,0:T(8,128)S(1)}, bf16[4,64,384]{2,1,0:T(8,128)(2,1)S(1)}, bf16[4,64,384]{2,1,0:T(8,128)(2,1)S(1)}) custom-call(bf16[4,960,384]{2,1,0:T(8,128)(2,1)} %snap_hbm.3, f32[1,960]{1,0:T(1,128)} %bitcast.8, f32[1,960]{1,0:T(1,128)} %bitcast.9, s32[1,960]{1,0:T(1,128)} %bitcast.10), custom_call_target="tpu_custom_call" | custom-call | flops 1000000000 | bytes 6000000 | tf_op jit(solution)/shard_map/weighting/pallas_call | solution.py:137
  28.7 0.9 %collective-permute-done.low = bf16[4,32,384]{2,1,0:T(8,128)(2,1)S(1)} collective-permute-done((bf16[4,32,384]{2,1,0:T(8,128)(2,1)S(1)}, bf16[4,32,384]{2,1,0:T(8,128)(2,1)S(1)}, u32[]{:S(2)}, u32[]{:S(2)}) %collective-permute-start) | collective-permute-done | bytes 98336 | tf_op jit(solution)/shard_map/halo/ppermute | solution.py:334
  29.6 0.0 collective-permute-done.1.high
  29.6 0.3 weighting.3.edges
  29.9 0.0 all-to-all-done.rot
  29.9 2.5 %projections.2 = (f32[2,384,128]{2,1,0:T(8,128)S(1)}, bf16[128,384]{1,0:T(8,128)(2,1)S(1)}, bf16[2,960,384]{2,1,0:T(8,128)(2,1)S(1)}) custom-call(bf16[4,960,384]{2,1,0:T(8,128)(2,1)} %snap_hbm.3, bf16[4,960,384]{2,1,0:T(8,128)(2,1)S(1)} %get-tuple-element.15.weighted, bf16[4,64,384]{2,1,0:T(8,128)(2,1)S(1)} %weighting.3.edges, ...), custom_call_target="tpu_custom_call" | custom-call | flops 400000000 | bytes 3000000 | tf_op jit(solution)/shard_map/projections/pallas_call | solution.py:239
  32.4 0.9 %collective-permute-start.2 = (f32[2,384,128]{2,1,0:T(8,128)S(1)}, f32[2,384,128]{2,1,0:T(8,128)S(1)}, u32[]{:S(2)}, u32[]{:S(2)}) collective-permute-start(f32[2,384,128]{2,1,0:T(8,128)S(1)} %get-tuple-element.24), channel_id=1, source_target_pairs={{0,64},{64,0},{1,65},{65,1},{2,66},{66,2},{3,67},{67,3},{4,68},{68... | collective-permute-start | bytes 1179656 | tf_op jit(solution)/shard_map/projections/ppermute | solution.py:343
  33.3 1.1 %projections.3 = f32[2,384,128]{2,1,0:T(8,128)S(1)} custom-call(bf16[2,960,384]{2,1,0:T(8,128)(2,1)S(1)} %get-tuple-element.22.snap, bf16[4,960,384]{2,1,0:T(8,128)(2,1)S(1)} %get-tuple-element.15.weighted, bf16[4,64,384]{2,1,0:T(8,128)(2,1)S(1)} %weighting.3.edges, bf16[128,384]{1,0:T(8,128)(2,1)S(1)} %get-tuple-element.23.rotation_t), custom_call_target="tpu_custom_call" | custom-call | flops 400000000 | bytes 3000000 | tf_op jit(solution)/shard_map/projections/pallas_call | solution.py:269
  34.4 0.3 collective-permute-done.2
  34.7 11.8 %all_to_all.20 = f32[16,48,128]{2,1,0:T(8,128)S(1)} all-to-all(f32[16,48,128]{2,1,0:T(8,128)S(1)} %bitcast.7), channel_id=1, replica_groups=mesh['x_lo'=2,'core'=2,'x_hi'=2,'z'=8,'y'=4] {'x_lo','x_hi','y'}, dimensions={0} | all-to-all | bytes 786432 | tf_op jit(solution)/shard_map/sum_plane/all_to_all | solution.py:350
  46.6 14.2 %all_to_all.21 = f32[8,48,128]{2,1,0:T(8,128)S(1)} all-to-all(f32[8,48,128]{2,1,0:T(8,128)S(1)} %broadcast_in_dim.4), channel_id=1, replica_groups=mesh['x_lo'=2,'core'=2,'x_hi'=2,'z'=8,'y'=4] {'z'}, dimensions={0} | all-to-all | bytes 393216 | tf_op jit(solution)/shard_map/sum_z/all_to_all | solution.py:321
  60.9 10.8 %all_to_all.22 = f32[16,48,128]{2,1,0:T(8,128)S(1)} all-to-all(f32[16,48,128]{2,1,0:T(8,128)S(1)} %broadcast_in_dim.5), channel_id=1, replica_groups=mesh['x_lo'=2,'core'=2,'x_hi'=2,'z'=8,'y'=4] {'x_lo','x_hi','y'}, dimensions={0} | all-to-all | bytes 786432 | tf_op jit(solution)/shard_map/share_plane/all_to_all | solution.py:321
  71.7 4.7 %collective-permute-start.3 = (f32[2,384,128]{2,1,0:T(8,128)S(1)}, f32[2,384,128]{2,1,0:T(8,128)S(1)}, u32[]{:S(2)}, u32[]{:S(2)}) collective-permute-start(f32[2,384,128]{2,1,0:T(8,128)S(1)} %bitcast.5), channel_id=1, source_target_pairs={{0,64},{64,0},{1,65},{65,1},{2,66},{66,2},{3,67},{67,3},{4,68},{68... | collective-permute-start | bytes 1179656 | tf_op jit(solution)/shard_map/share_core/ppermute | solution.py:357
  76.3 0.8 share_core.2.begun
  77.1 0.6 collective-permute-done.3.other
  77.7 0.8 share_core.3
  (6 shorter events, 0.1 us)
Async XLA Ops:
  1.6 28.3 %all-to-all-start = ((bf16[64,8,128]{2,1,0:T(8,128)(2,1)}), bf16[64,8,128]{2,1,0:T(8,128)(2,1)S(1)}, u32[]{:S(2)}, u32[]{:S(2)}) async-start(bf16[64,8,128]{2,1,0:T(8,128)(2,1)} %get-tuple-element.21), calls=%async_computation | async-start | bytes 262144 | tf_op jit(solution)/shard_map/rotation_rows/all_to_all | solution.py:337
  16.8 12.8 %collective-permute-start = (bf16[4,32,384]{2,1,0:T(8,128)(2,1)S(1)}, bf16[4,32,384]{2,1,0:T(8,128)(2,1)S(1)}, u32[]{:S(2)}, u32[]{:S(2)}) collective-permute-start(bf16[4,32,384]{2,1,0:T(8,128)(2,1)S(1)} %get-tuple-element.19), channel_id=1, source_target_pairs={{0,1},{1,2},{2,3},{3,4},{4,5},{5,6},{6,7},{7,8},{8,9},{9,10},{10,1... | collective-permute-start | bytes 294920 | tf_op jit(solution)/shard_map/halo/ppermute | solution.py:334
  17.9 11.7 %collective-permute-start.1 = (bf16[4,32,384]{2,1,0:T(8,128)(2,1)S(1)}, bf16[4,32,384]{2,1,0:T(8,128)(2,1)S(1)}, u32[]{:S(2)}, u32[]{:S(2)}) collective-permute-start(bf16[4,32,384]{2,1,0:T(8,128)(2,1)S(1)} %get-tuple-element.20), channel_id=1, source_target_pairs={{0,255},{1,0},{2,1},{3,2},{4,3},{5,4},{6,5},{7,6},{8,7},{9,8},{10,... | collective-permute-start | bytes 294920 | tf_op jit(solution)/shard_map/halo/ppermute | solution.py:335
  32.4 2.2 %collective-permute-start.2 = (f32[2,384,128]{2,1,0:T(8,128)S(1)}, f32[2,384,128]{2,1,0:T(8,128)S(1)}, u32[]{:S(2)}, u32[]{:S(2)}) collective-permute-start(f32[2,384,128]{2,1,0:T(8,128)S(1)} %get-tuple-element.24), channel_id=1, source_target_pairs={{0,64},{64,0},{1,65},{65,1},{2,66},{66,2},{3,67},{67,3},{4,68},{68... | collective-permute-start | bytes 1179656 | tf_op jit(solution)/shard_map/projections/ppermute | solution.py:343
  71.7 6.0 %collective-permute-start.3 = (f32[2,384,128]{2,1,0:T(8,128)S(1)}, f32[2,384,128]{2,1,0:T(8,128)S(1)}, u32[]{:S(2)}, u32[]{:S(2)}) collective-permute-start(f32[2,384,128]{2,1,0:T(8,128)S(1)} %bitcast.5), channel_id=1, source_target_pairs={{0,64},{64,0},{1,65},{65,1},{2,66},{66,2},{3,67},{67,3},{4,68},{68... | collective-permute-start | bytes 1179656 | tf_op jit(solution)/shard_map/share_core/ppermute | solution.py:357

commit v6 on v5

--- a/solution.py
+++ b/solution.py
@@ -25,12 +25,12 @@
     return pltpu.with_memory_space_constraint(array, pltpu.HBM)
 
 
-def start_kernel(snap, rot_hbm, first, last, spread_rot, rot, sems):
+def start_kernel(snap, rot_hbm, first, last, spread_hbm, begin, end, rot, spread_rot, sems):
     cells = snap.shape[1]
     copies = [
         pltpu.make_async_copy(rot_hbm, rot, sems.at[0]),
-        pltpu.make_async_copy(snap.at[:, pl.ds(0, HALO)], first, sems.at[1]),
-        pltpu.make_async_copy(snap.at[:, pl.ds(cells - HALO, HALO)], last, sems.at[2]),
+        pltpu.make_async_copy(snap.at[:, pl.ds(0, HALO)], begin, sems.at[1]),
+        pltpu.make_async_copy(snap.at[:, pl.ds(cells - HALO, HALO)], end, sems.at[2]),
     ]
     for copy in copies:
         copy.start()
@@ -40,20 +40,33 @@
     block = jnp.concatenate([rot[...].astype(jnp.float32), padding], axis=0).astype(jnp.bfloat16)
     for tile in range(spread_rot.shape[0]):
         spread_rot[tile] = block
-    for copy in copies[1:]:
+    written = pltpu.make_async_copy(spread_rot, spread_hbm, sems.at[0])
+    written.start()
+    for copy, rim, target in ((copies[1], begin, first), (copies[2], end, last)):
         copy.wait()
+        speed = [rim[component].astype(jnp.float32) for component in range(1, COMPONENTS)]
+        target[0] = rim[0]
+        target[1] = ((speed[0] + speed[1]) + speed[2]).astype(jnp.bfloat16)
+    written.wait()
 
 
 def start(snapshots, rotation, tiles):
     components, _, width = snapshots.shape
     rows, modes = rotation.shape
-    edge = jax.ShapeDtypeStruct((components, HALO, width), jnp.bfloat16)
+    edge = jax.ShapeDtypeStruct((2, HALO, width), jnp.bfloat16)
+    rim = pltpu.VMEM((components, HALO, width), jnp.bfloat16)
     return pl.pallas_call(
         start_kernel,
         out_shape=(edge, edge, jax.ShapeDtypeStruct((tiles, PADDED, modes), jnp.bfloat16)),
         in_specs=[HBM, HBM],
-        out_specs=(VMEM, VMEM, VMEM),
-        scratch_shapes=[pltpu.VMEM((rows, modes), jnp.bfloat16), pltpu.SemaphoreType.DMA((3,))],
+        out_specs=(VMEM, VMEM, HBM),
+        scratch_shapes=[
+            rim,
+            rim,
+            pltpu.VMEM((rows, modes), jnp.bfloat16),
+            pltpu.VMEM((tiles, PADDED, modes), jnp.bfloat16),
+            pltpu.SemaphoreType.DMA((3,)),
+        ],
         compiler_params=PARAMS,
     )(snapshots, in_hbm(rotation))
 
@@ -162,17 +175,22 @@
     )
 
 
-def edge_kernel(begin, end, edge_scale, low, high, edges):
+def edge_kernel(begin, end, edge_scale, high, low, edges):
+    blank = jnp.zeros(low.shape[1:], low.dtype)
+
+    def beyond(halo, component):
+        return halo[component] if component < 2 else blank
+
     first = weigh_rows(
         edge_scale[0:HALO],
         HALO,
-        lambda component: jnp.concatenate([low[component], begin[component]], axis=0),
+        lambda component: jnp.concatenate([beyond(low, component), begin[component]], axis=0),
         lambda component: begin[component, 0:HALO],
     )
     last = weigh_rows(
         edge_scale[HALO:],
         HALO,
-        lambda component: jnp.concatenate([end[component], high[component]], axis=0),
+        lambda component: jnp.concatenate([end[component], beyond(high, component)], axis=0),
         lambda component: end[component, HALO:],
     )
     for component in range(COMPONENTS):
@@ -188,7 +206,7 @@
         out_specs=VMEM,
         compiler_params=PARAMS,
         cost_estimate=pl.CostEstimate(flops=EDGE_FLOPS, bytes_accessed=600_000, transcendentals=0),
-    )(begin, end, edge_scale, low, high)
+    )(begin, end, edge_scale, high, low)
 
 
 def totals_of(rotation_t, snap, weighted, edges):
@@ -331,8 +349,8 @@
     with jax.named_scope("start"):
         first, last, rows = start(resident, rotation, lax.axis_size(TILE_AXES))
     with jax.named_scope("halo"):
+        high = lax.ppermute(first, CELL_AXES, backward)
         low = lax.ppermute(last, CELL_AXES, forward)
-        high = lax.ppermute(first, CELL_AXES, backward)
     with jax.named_scope("rotation_rows"):
         full_rotation = lax.all_to_all(rows, TILE_AXES, 0, 0)
     with jax.named_scope("weighting"):

time: 78.8 us -> 79.5 us (level)
  waiting for transfers between devices: 1.8 us -> 6.89 us
  blocking collectives: 36.8 us -> 34.3 us
  starting transfers between devices: 29 us -> 27.4 us
    ppermute x1, waiting for transfers between devices: 0.91 us -> 5.64 us  [on_device(): low = lax.ppermute(last, CELL_AXES, forward)]
    all_to_all x2, blocking collectives: 25 us -> 22.2 us  [spread(): lax.all_to_all(jnp.broadcast_to(block[None], (count,) + block.shape), axe...]
    ppermute x1, starting transfers between devices: 1.09 us -> 0.01 us  [on_device(): low = lax.ppermute(last, CELL_AXES, forward)]
    ppermute x1, starting transfers between devices: 7.24 us -> 8.24 us  [on_device(): high = lax.ppermute(first, CELL_AXES, backward)]
where the time goes in v6:
time: 79.5 us; the launch traced here: 79.1 us
  blocking collectives  34.3 us (43%)
  starting transfers between devices  27.4 us (34%)
  Pallas kernels  10.3 us (13%)
  waiting for transfers between devices  6.89 us (9%)
    all_to_all x2, blocking collectives, spread(): lax.all_to_all(jnp.broadcast_to(block[None], (count,) + block.shape), axe...  22.2 us
    all_to_all x1, starting transfers between devices, on_device(): full_rotation = lax.all_to_all(rows, TILE_AXES, 0, 0)  15.1 us
    all_to_all x1, blocking collectives, on_device(): piece = jnp.sum(lax.all_to_all(pieces, PLANE_AXES, 0, 0), axis=0)  12.1 us
    ppermute x1, starting transfers between devices, on_device(): high = lax.ppermute(first, CELL_AXES, backward)  8.24 us
    ppermute x1, waiting for transfers between devices, on_device(): low = lax.ppermute(last, CELL_AXES, forward)  5.64 us
    ppermute x1, starting transfers between devices, on_device(): other = lax.ppermute(mine, 'core', swap)  3.95 us
    pallas_call x1, Pallas kernels, weigh(): pl.pallas_call(weighting_kernel, out_shape=(jax.ShapeDtypeStruct(snapshot...  3.57 us
    pallas_call x1, Pallas kernels, project_sent(): pl.pallas_call(sent_kernel, out_shape=(jax.ShapeDtypeStruct((components /...  2.53 us
  transfers between devices with their start and end apart: 5, of which 3 were waited for; matrix products, arithmetic and copies ran while one was open for 0% of the time, Pallas kernels for 7%

profile of v6, /device:TPU:1, one launch (start us, length us, event | category | flops | bytes accessed | tf_op | source)
XLA Modules:
  0.0 79.1 jit_solution(12311133898522200097)
XLA Ops:
  0.0 1.4 %start.1 = (bf16[2,32,384]{2,1,0:T(8,128)(2,1)S(1)}, bf16[2,32,384]{2,1,0:T(8,128)(2,1)S(1)}, bf16[64,8,128]{2,1,0:T(8,128)(2,1)}) custom-call(bf16[4,960,384]{2,1,0:T(8,128)(2,1)} %snap_hbm.3, bf16[6,128]{1,0:T(8,128)(2,1)} %rot_hbm.1), custom_call_target="tpu_custom_call" | custom-call | tf_op jit(solution)/shard_map/start/pallas_call | solution.py:58
  1.4 15.1 %all-to-all-start = ((bf16[64,8,128]{2,1,0:T(8,128)(2,1)}), bf16[64,8,128]{2,1,0:T(8,128)(2,1)S(1)}, u32[]{:S(2)}, u32[]{:S(2)}) async-start(bf16[64,8,128]{2,1,0:T(8,128)(2,1)} %get-tuple-element.21), calls=%async_computation | async-start | bytes 262144 | tf_op jit(solution)/shard_map/rotation_rows/all_to_all | solution.py:355
  16.5 8.2 %collective-permute-start = (bf16[2,32,384]{2,1,0:T(8,128)(2,1)S(1)}, bf16[2,32,384]{2,1,0:T(8,128)(2,1)S(1)}, u32[]{:S(2)}, u32[]{:S(2)}) collective-permute-start(bf16[2,32,384]{2,1,0:T(8,128)(2,1)S(1)} %get-tuple-element.19), channel_id=1, source_target_pairs={{0,255},{1,0},{2,1},{3,2},{4,3},{5,4},{6,5},{7,6},{8,7},{9,8},{10,... | collective-permute-start | bytes 147464 | tf_op jit(solution)/shard_map/halo/ppermute | solution.py:352
  24.8 0.0 collective-permute-start.1
  24.8 3.6 %weighting.2 = (bf16[4,960,384]{2,1,0:T(8,128)(2,1)S(1)}, f32[64,8]{1,0:T(8,128)S(1)}, bf16[4,64,384]{2,1,0:T(8,128)(2,1)S(1)}, bf16[4,64,384]{2,1,0:T(8,128)(2,1)S(1)}) custom-call(bf16[4,960,384]{2,1,0:T(8,128)(2,1)} %snap_hbm.3, f32[1,960]{1,0:T(1,128)} %bitcast.8, f32[1,960]{1,0:T(1,128)} %bitcast.9, s32[1,960]{1,0:T(1,128)} %bitcast.10), custom_call_target="tpu_custom_call" | custom-call | flops 1000000000 | bytes 6000000 | tf_op jit(solution)/shard_map/weighting/pallas_call | solution.py:150
  28.3 0.0 collective-permute-done.high
  28.4 5.6 %collective-permute-done.1.low = bf16[2,32,384]{2,1,0:T(8,128)(2,1)S(1)} collective-permute-done((bf16[2,32,384]{2,1,0:T(8,128)(2,1)S(1)}, bf16[2,32,384]{2,1,0:T(8,128)(2,1)S(1)}, u32[]{:S(2)}, u32[]{:S(2)}) %collective-permute-start.1) | collective-permute-done | bytes 49184 | tf_op jit(solution)/shard_map/halo/ppermute | solution.py:353
  34.0 0.3 weighting.3.edges
  34.3 0.0 all-to-all-done.rot
  34.3 2.5 %projections.2 = (f32[2,384,128]{2,1,0:T(8,128)S(1)}, bf16[128,384]{1,0:T(8,128)(2,1)S(1)}, bf16[2,960,384]{2,1,0:T(8,128)(2,1)S(1)}) custom-call(bf16[4,960,384]{2,1,0:T(8,128)(2,1)} %snap_hbm.3, bf16[4,960,384]{2,1,0:T(8,128)(2,1)S(1)} %get-tuple-element.15.weighted, bf16[4,64,384]{2,1,0:T(8,128)(2,1)S(1)} %weighting.3.edges, ...), custom_call_target="tpu_custom_call" | custom-call | flops 400000000 | bytes 3000000 | tf_op jit(solution)/shard_map/projections/pallas_call | solution.py:257
  36.8 0.1 collective-permute-start.2
  36.9 1.1 %projections.3 = f32[2,384,128]{2,1,0:T(8,128)S(1)} custom-call(bf16[2,960,384]{2,1,0:T(8,128)(2,1)S(1)} %get-tuple-element.22.snap, bf16[4,960,384]{2,1,0:T(8,128)(2,1)S(1)} %get-tuple-element.15.weighted, bf16[4,64,384]{2,1,0:T(8,128)(2,1)S(1)} %weighting.3.edges, bf16[128,384]{1,0:T(8,128)(2,1)S(1)} %get-tuple-element.23.rotation_t), custom_call_target="tpu_custom_call" | custom-call | flops 400000000 | bytes 3000000 | tf_op jit(solution)/shard_map/projections/pallas_call | solution.py:287
  38.0 0.7 collective-permute-done.2
  38.7 12.1 %all_to_all.20 = f32[16,48,128]{2,1,0:T(8,128)S(1)} all-to-all(f32[16,48,128]{2,1,0:T(8,128)S(1)} %bitcast.7), channel_id=1, replica_groups=mesh['x_lo'=2,'core'=2,'x_hi'=2,'z'=8,'y'=4] {'x_lo','x_hi','y'}, dimensions={0} | all-to-all | bytes 786432 | tf_op jit(solution)/shard_map/sum_plane/all_to_all | solution.py:368
  50.9 11.0 %all_to_all.21 = f32[8,48,128]{2,1,0:T(8,128)S(1)} all-to-all(f32[8,48,128]{2,1,0:T(8,128)S(1)} %broadcast_in_dim.4), channel_id=1, replica_groups=mesh['x_lo'=2,'core'=2,'x_hi'=2,'z'=8,'y'=4] {'z'}, dimensions={0} | all-to-all | bytes 393216 | tf_op jit(solution)/shard_map/sum_z/all_to_all | solution.py:339
  61.9 11.2 %all_to_all.22 = f32[16,48,128]{2,1,0:T(8,128)S(1)} all-to-all(f32[16,48,128]{2,1,0:T(8,128)S(1)} %broadcast_in_dim.5), channel_id=1, replica_groups=mesh['x_lo'=2,'core'=2,'x_hi'=2,'z'=8,'y'=4] {'x_lo','x_hi','y'}, dimensions={0} | all-to-all | bytes 786432 | tf_op jit(solution)/shard_map/share_plane/all_to_all | solution.py:339
  73.1 4.0 %collective-permute-start.3 = (f32[2,384,128]{2,1,0:T(8,128)S(1)}, f32[2,384,128]{2,1,0:T(8,128)S(1)}, u32[]{:S(2)}, u32[]{:S(2)}) collective-permute-start(f32[2,384,128]{2,1,0:T(8,128)S(1)} %bitcast.5), channel_id=1, source_target_pairs={{0,64},{64,0},{1,65},{65,1},{2,66},{66,2},{3,67},{67,3},{4,68},{68... | collective-permute-start | bytes 1179656 | tf_op jit(solution)/shard_map/share_core/ppermute | solution.py:375
  77.0 0.8 share_core.2.begun
  77.8 0.6 collective-permute-done.3.other
  78.4 0.8 share_core.3
  (6 shorter events, 0.1 us)
Async XLA Ops:
  1.4 32.9 %all-to-all-start = ((bf16[64,8,128]{2,1,0:T(8,128)(2,1)}), bf16[64,8,128]{2,1,0:T(8,128)(2,1)S(1)}, u32[]{:S(2)}, u32[]{:S(2)}) async-start(bf16[64,8,128]{2,1,0:T(8,128)(2,1)} %get-tuple-element.21), calls=%async_computation | async-start | bytes 262144 | tf_op jit(solution)/shard_map/rotation_rows/all_to_all | solution.py:355
  16.5 11.8 %collective-permute-start = (bf16[2,32,384]{2,1,0:T(8,128)(2,1)S(1)}, bf16[2,32,384]{2,1,0:T(8,128)(2,1)S(1)}, u32[]{:S(2)}, u32[]{:S(2)}) collective-permute-start(bf16[2,32,384]{2,1,0:T(8,128)(2,1)S(1)} %get-tuple-element.19), channel_id=1, source_target_pairs={{0,255},{1,0},{2,1},{3,2},{4,3},{5,4},{6,5},{7,6},{8,7},{9,8},{10,... | collective-permute-start | bytes 147464 | tf_op jit(solution)/shard_map/halo/ppermute | solution.py:352
  24.8 9.2 %collective-permute-start.1 = (bf16[2,32,384]{2,1,0:T(8,128)(2,1)S(1)}, bf16[2,32,384]{2,1,0:T(8,128)(2,1)S(1)}, u32[]{:S(2)}, u32[]{:S(2)}) collective-permute-start(bf16[2,32,384]{2,1,0:T(8,128)(2,1)S(1)} %get-tuple-element.20), channel_id=1, source_target_pairs={{0,1},{1,2},{2,3},{3,4},{4,5},{5,6},{6,7},{7,8},{8,9},{9,10},{10,1... | collective-permute-start | bytes 147464 | tf_op jit(solution)/shard_map/halo/ppermute | solution.py:353
  36.8 1.8 %collective-permute-start.2 = (f32[2,384,128]{2,1,0:T(8,128)S(1)}, f32[2,384,128]{2,1,0:T(8,128)S(1)}, u32[]{:S(2)}, u32[]{:S(2)}) collective-permute-start(f32[2,384,128]{2,1,0:T(8,128)S(1)} %get-tuple-element.24), channel_id=1, source_target_pairs={{0,64},{64,0},{1,65},{65,1},{2,66},{66,2},{3,67},{67,3},{4,68},{68... | collective-permute-start | bytes 1179656 | tf_op jit(solution)/shard_map/projections/ppermute | solution.py:361
  73.1 5.3 %collective-permute-start.3 = (f32[2,384,128]{2,1,0:T(8,128)S(1)}, f32[2,384,128]{2,1,0:T(8,128)S(1)}, u32[]{:S(2)}, u32[]{:S(2)}) collective-permute-start(f32[2,384,128]{2,1,0:T(8,128)S(1)} %bitcast.5), channel_id=1, source_target_pairs={{0,64},{64,0},{1,65},{65,1},{2,66},{66,2},{3,67},{67,3},{4,68},{68... | collective-permute-start | bytes 1179656 | tf_op jit(solution)/shard_map/share_core/ppermute | solution.py:375

commit v7 on v6

--- a/solution.py
+++ b/solution.py
@@ -25,12 +25,15 @@
     return pltpu.with_memory_space_constraint(array, pltpu.HBM)
 
 
-def start_kernel(snap, rot_hbm, first, last, spread_hbm, begin, end, rot, spread_rot, sems):
+def start_kernel(snap, rot_hbm, inner, outer, spread_hbm, begin, end, rot, spread_rot, sems):
     cells = snap.shape[1]
+    odd = lax.axis_index("y") % 2
+    inner_at = pl.multiple_of((1 - odd) * (cells - HALO), HALO)
+    outer_at = pl.multiple_of(odd * (cells - HALO), HALO)
     copies = [
         pltpu.make_async_copy(rot_hbm, rot, sems.at[0]),
-        pltpu.make_async_copy(snap.at[:, pl.ds(0, HALO)], begin, sems.at[1]),
-        pltpu.make_async_copy(snap.at[:, pl.ds(cells - HALO, HALO)], end, sems.at[2]),
+        pltpu.make_async_copy(snap.at[:, pl.ds(outer_at, HALO)], begin, sems.at[1]),
+        pltpu.make_async_copy(snap.at[:, pl.ds(inner_at, HALO)], end, sems.at[2]),
     ]
     for copy in copies:
         copy.start()
@@ -42,7 +45,7 @@
         spread_rot[tile] = block
     written = pltpu.make_async_copy(spread_rot, spread_hbm, sems.at[0])
     written.start()
-    for copy, rim, target in ((copies[1], begin, first), (copies[2], end, last)):
+    for copy, rim, target in ((copies[1], begin, outer), (copies[2], end, inner)):
         copy.wait()
         speed = [rim[component].astype(jnp.float32) for component in range(1, COMPONENTS)]
         target[0] = rim[0]
@@ -175,8 +178,12 @@
     )
 
 
-def edge_kernel(begin, end, edge_scale, high, low, edges):
-    blank = jnp.zeros(low.shape[1:], low.dtype)
+def edge_kernel(begin, end, edge_scale, outer, inner, edges):
+    odd = lax.axis_index("y") % 2
+    blank = jnp.zeros(outer.shape[1:], outer.dtype)
+    mask = lax.broadcast_in_dim(odd, outer.shape, ()) == 1
+    low = jnp.where(mask, inner[...], outer[...])
+    high = jnp.where(mask, outer[...], inner[...])
 
     def beyond(halo, component):
         return halo[component] if component < 2 else blank
@@ -198,7 +205,7 @@
         edges[component, HALO:] = last[component]
 
 
-def weigh_edges(begin, end, edge_scale, low, high):
+def weigh_edges(begin, end, edge_scale, outer, inner):
     return pl.pallas_call(
         edge_kernel,
         out_shape=jax.ShapeDtypeStruct(begin.shape, jnp.bfloat16),
@@ -206,7 +213,7 @@
         out_specs=VMEM,
         compiler_params=PARAMS,
         cost_estimate=pl.CostEstimate(flops=EDGE_FLOPS, bytes_accessed=600_000, transcendentals=0),
-    )(begin, end, edge_scale, high, low)
+    )(begin, end, edge_scale, outer, inner)
 
 
 def totals_of(rotation_t, snap, weighted, edges):
@@ -343,19 +350,19 @@
     components, cells, width = snapshots.shape
     count = lax.axis_size(CELL_AXES)
     resident = in_hbm(snapshots)
-    forward = [(i, (i + 1) % count) for i in range(count)]
-    backward = [(i, (i - 1) % count) for i in range(count)]
+    inside = [(i, i ^ 1) for i in range(count)]
+    across = [(i, (i + 1 if i % 2 else i - 1) % count) for i in range(count)]
     swap = [(0, 1), (1, 0)]
     with jax.named_scope("start"):
-        first, last, rows = start(resident, rotation, lax.axis_size(TILE_AXES))
+        inner, outer, rows = start(resident, rotation, lax.axis_size(TILE_AXES))
     with jax.named_scope("halo"):
-        high = lax.ppermute(first, CELL_AXES, backward)
-        low = lax.ppermute(last, CELL_AXES, forward)
+        outer = lax.ppermute(outer, CELL_AXES, across)
+        inner = lax.ppermute(inner, CELL_AXES, inside)
     with jax.named_scope("rotation_rows"):
         full_rotation = lax.all_to_all(rows, TILE_AXES, 0, 0)
     with jax.named_scope("weighting"):
         weighted, edge_scale, begin, end = weigh(resident, density, sound_speed, offsets)
-        edges = weigh_edges(begin, end, edge_scale, low, high)
+        edges = weigh_edges(begin, end, edge_scale, outer, inner)
     with jax.named_scope("projections"):
         send, rotation_t, snap_keep = project_sent(resident, weighted, edges, full_rotation)
         received = lax.ppermute(send, "core", swap)

time: 79.5 us -> 76.6 us (0.964)
  waiting for transfers between devices: 6.89 us -> 0.89 us
  starting transfers between devices: 27.4 us -> 29.9 us
    ppermute x2, waiting for transfers between devices: 5.65 us -> 0.01 us  [the longest x1 0.01 us: on_device(): outer = lax.ppermute(outer, CELL_AXES, across)]
    ppermute x1, starting transfers between devices: 0.09 us -> 1.84 us  [on_device(): received = lax.ppermute(send, 'core', swap)]
    all_to_all x2, blocking collectives: 22.2 us -> 23.4 us  [spread(): lax.all_to_all(jnp.broadcast_to(block[None], (count,) + block.shape), axe...]
  transfers between devices with their start and end apart: 5 -> 5, of which waited for: 3 -> 2; matrix products, arithmetic and copies ran while one was open for 0% -> 0% of each run, Pallas kernels for 7% -> 7%
where the time goes in v7:
time: 76.6 us; the launch traced here: 76.3 us
  blocking collectives  35 us (46%)
  starting transfers between devices  29.9 us (39%)
  Pallas kernels  10.3 us (13%)
  waiting for transfers between devices  0.89 us (1%)
    all_to_all x2, blocking collectives, spread(): lax.all_to_all(jnp.broadcast_to(block[None], (count,) + block.shape), axe...  23.4 us
    all_to_all x1, starting transfers between devices, on_device(): full_rotation = lax.all_to_all(rows, TILE_AXES, 0, 0)  15.1 us
    all_to_all x1, blocking collectives, on_device(): piece = jnp.sum(lax.all_to_all(pieces, PLANE_AXES, 0, 0), axis=0)  11.6 us
    ppermute x1, starting transfers between devices, on_device(): outer = lax.ppermute(outer, CELL_AXES, across)  8.25 us
    ppermute x1, starting transfers between devices, on_device(): other = lax.ppermute(mine, 'core', swap)  4.68 us
    pallas_call x1, Pallas kernels, weigh(): pl.pallas_call(weighting_kernel, out_shape=(jax.ShapeDtypeStruct(snapshot...  3.57 us
    pallas_call x1, Pallas kernels, project_sent(): pl.pallas_call(sent_kernel, out_shape=(jax.ShapeDtypeStruct((components /...  2.53 us
    ppermute x1, starting transfers between devices, on_device(): received = lax.ppermute(send, 'core', swap)  1.84 us
  transfers between devices with their start and end apart: 5, of which 2 were waited for; matrix products, arithmetic and copies ran while one was open for 0% of the time, Pallas kernels for 7%

profile of v7, /device:TPU:1, one launch (start us, length us, event | category | flops | bytes accessed | tf_op | source)
XLA Modules:
  0.0 76.3 jit_solution(9591103444317499727)
XLA Ops:
  0.0 1.4 %start.1 = (bf16[2,32,384]{2,1,0:T(8,128)(2,1)S(1)}, bf16[2,32,384]{2,1,0:T(8,128)(2,1)S(1)}, bf16[64,8,128]{2,1,0:T(8,128)(2,1)}) custom-call(bf16[4,960,384]{2,1,0:T(8,128)(2,1)} %snap_hbm.3, bf16[6,128]{1,0:T(8,128)(2,1)} %rot_hbm.1), custom_call_target="tpu_custom_call" | custom-call | tf_op jit(solution)/shard_map/start/pallas_call | solution.py:61
  1.4 15.1 %all-to-all-start = ((bf16[64,8,128]{2,1,0:T(8,128)(2,1)}), bf16[64,8,128]{2,1,0:T(8,128)(2,1)S(1)}, u32[]{:S(2)}, u32[]{:S(2)}) async-start(bf16[64,8,128]{2,1,0:T(8,128)(2,1)} %get-tuple-element.21), calls=%async_computation | async-start | bytes 262144 | tf_op jit(solution)/shard_map/rotation_rows/all_to_all | solution.py:362
  16.5 8.3 %collective-permute-start = (bf16[2,32,384]{2,1,0:T(8,128)(2,1)S(1)}, bf16[2,32,384]{2,1,0:T(8,128)(2,1)S(1)}, u32[]{:S(2)}, u32[]{:S(2)}) collective-permute-start(bf16[2,32,384]{2,1,0:T(8,128)(2,1)S(1)} %get-tuple-element.19), channel_id=1, source_target_pairs={{0,255},{1,2},{2,1},{3,4},{4,3},{5,6},{6,5},{7,8},{8,7},{9,10},{10... | collective-permute-start | bytes 147464 | tf_op jit(solution)/shard_map/halo/ppermute | solution.py:359
  24.8 0.0 collective-permute-start.1
  24.8 3.6 %weighting.2 = (bf16[4,960,384]{2,1,0:T(8,128)(2,1)S(1)}, f32[64,8]{1,0:T(8,128)S(1)}, bf16[4,64,384]{2,1,0:T(8,128)(2,1)S(1)}, bf16[4,64,384]{2,1,0:T(8,128)(2,1)S(1)}) custom-call(bf16[4,960,384]{2,1,0:T(8,128)(2,1)} %snap_hbm.3, f32[1,960]{1,0:T(1,128)} %bitcast.8, f32[1,960]{1,0:T(1,128)} %bitcast.9, s32[1,960]{1,0:T(1,128)} %bitcast.10), custom_call_target="tpu_custom_call" | custom-call | flops 1000000000 | bytes 6000000 | tf_op jit(solution)/shard_map/weighting/pallas_call | solution.py:153
  28.4 0.0 collective-permute-done.outer
  28.4 0.0 collective-permute-done.1.inner
  28.4 0.3 weighting.3.edges
  28.7 0.0 all-to-all-done.rot
  28.7 2.5 %projections.2 = (f32[2,384,128]{2,1,0:T(8,128)S(1)}, bf16[128,384]{1,0:T(8,128)(2,1)S(1)}, bf16[2,960,384]{2,1,0:T(8,128)(2,1)S(1)}) custom-call(bf16[4,960,384]{2,1,0:T(8,128)(2,1)} %snap_hbm.3, bf16[4,960,384]{2,1,0:T(8,128)(2,1)S(1)} %get-tuple-element.15.weighted, bf16[4,64,384]{2,1,0:T(8,128)(2,1)S(1)} %weighting.3.edges, ...), custom_call_target="tpu_custom_call" | custom-call | flops 400000000 | bytes 3000000 | tf_op jit(solution)/shard_map/projections/pallas_call | solution.py:264
  31.2 1.8 %collective-permute-start.2 = (f32[2,384,128]{2,1,0:T(8,128)S(1)}, f32[2,384,128]{2,1,0:T(8,128)S(1)}, u32[]{:S(2)}, u32[]{:S(2)}) collective-permute-start(f32[2,384,128]{2,1,0:T(8,128)S(1)} %get-tuple-element.24), channel_id=1, source_target_pairs={{0,64},{64,0},{1,65},{65,1},{2,66},{66,2},{3,67},{67,3},{4,68},{68... | collective-permute-start | bytes 1179656 | tf_op jit(solution)/shard_map/projections/ppermute | solution.py:368
  33.0 1.1 %projections.3 = f32[2,384,128]{2,1,0:T(8,128)S(1)} custom-call(bf16[2,960,384]{2,1,0:T(8,128)(2,1)S(1)} %get-tuple-element.22.snap, bf16[4,960,384]{2,1,0:T(8,128)(2,1)S(1)} %get-tuple-element.15.weighted, bf16[4,64,384]{2,1,0:T(8,128)(2,1)S(1)} %weighting.3.edges, bf16[128,384]{1,0:T(8,128)(2,1)S(1)} %get-tuple-element.23.rotation_t), custom_call_target="tpu_custom_call" | custom-call | flops 400000000 | bytes 3000000 | tf_op jit(solution)/shard_map/projections/pallas_call | solution.py:294
  34.1 0.3 collective-permute-done.2
  34.4 11.6 %all_to_all.20 = f32[16,48,128]{2,1,0:T(8,128)S(1)} all-to-all(f32[16,48,128]{2,1,0:T(8,128)S(1)} %bitcast.7), channel_id=1, replica_groups=mesh['x_lo'=2,'core'=2,'x_hi'=2,'z'=8,'y'=4] {'x_lo','x_hi','y'}, dimensions={0} | all-to-all | bytes 786432 | tf_op jit(solution)/shard_map/sum_plane/all_to_all | solution.py:375
  46.1 12.6 %all_to_all.21 = f32[8,48,128]{2,1,0:T(8,128)S(1)} all-to-all(f32[8,48,128]{2,1,0:T(8,128)S(1)} %broadcast_in_dim.4), channel_id=1, replica_groups=mesh['x_lo'=2,'core'=2,'x_hi'=2,'z'=8,'y'=4] {'z'}, dimensions={0} | all-to-all | bytes 393216 | tf_op jit(solution)/shard_map/sum_z/all_to_all | solution.py:346
  58.8 10.8 %all_to_all.22 = f32[16,48,128]{2,1,0:T(8,128)S(1)} all-to-all(f32[16,48,128]{2,1,0:T(8,128)S(1)} %broadcast_in_dim.5), channel_id=1, replica_groups=mesh['x_lo'=2,'core'=2,'x_hi'=2,'z'=8,'y'=4] {'x_lo','x_hi','y'}, dimensions={0} | all-to-all | bytes 786432 | tf_op jit(solution)/shard_map/share_plane/all_to_all | solution.py:346
  69.5 4.7 %collective-permute-start.3 = (f32[2,384,128]{2,1,0:T(8,128)S(1)}, f32[2,384,128]{2,1,0:T(8,128)S(1)}, u32[]{:S(2)}, u32[]{:S(2)}) collective-permute-start(f32[2,384,128]{2,1,0:T(8,128)S(1)} %bitcast.5), channel_id=1, source_target_pairs={{0,64},{64,0},{1,65},{65,1},{2,66},{66,2},{3,67},{67,3},{4,68},{68... | collective-permute-start | bytes 1179656 | tf_op jit(solution)/shard_map/share_core/ppermute | solution.py:382
  74.2 0.8 share_core.2.begun
  75.0 0.6 collective-permute-done.3.other
  75.6 0.8 share_core.3
  (6 shorter events, 0.1 us)
Async XLA Ops:
  1.4 27.3 %all-to-all-start = ((bf16[64,8,128]{2,1,0:T(8,128)(2,1)}), bf16[64,8,128]{2,1,0:T(8,128)(2,1)S(1)}, u32[]{:S(2)}, u32[]{:S(2)}) async-start(bf16[64,8,128]{2,1,0:T(8,128)(2,1)} %get-tuple-element.21), calls=%async_computation | async-start | bytes 262144 | tf_op jit(solution)/shard_map/rotation_rows/all_to_all | solution.py:362
  16.5 11.8 %collective-permute-start = (bf16[2,32,384]{2,1,0:T(8,128)(2,1)S(1)}, bf16[2,32,384]{2,1,0:T(8,128)(2,1)S(1)}, u32[]{:S(2)}, u32[]{:S(2)}) collective-permute-start(bf16[2,32,384]{2,1,0:T(8,128)(2,1)S(1)} %get-tuple-element.19), channel_id=1, source_target_pairs={{0,255},{1,2},{2,1},{3,4},{4,3},{5,6},{6,5},{7,8},{8,7},{9,10},{10... | collective-permute-start | bytes 147464 | tf_op jit(solution)/shard_map/halo/ppermute | solution.py:359
  24.8 3.6 %collective-permute-start.1 = (bf16[2,32,384]{2,1,0:T(8,128)(2,1)S(1)}, bf16[2,32,384]{2,1,0:T(8,128)(2,1)S(1)}, u32[]{:S(2)}, u32[]{:S(2)}) collective-permute-start(bf16[2,32,384]{2,1,0:T(8,128)(2,1)S(1)} %get-tuple-element.20), channel_id=1, source_target_pairs={{0,1},{1,0},{2,3},{3,2},{4,5},{5,4},{6,7},{7,6},{8,9},{9,8},{10,11... | collective-permute-start | bytes 147464 | tf_op jit(solution)/shard_map/halo/ppermute | solution.py:360
  31.2 3.2 %collective-permute-start.2 = (f32[2,384,128]{2,1,0:T(8,128)S(1)}, f32[2,384,128]{2,1,0:T(8,128)S(1)}, u32[]{:S(2)}, u32[]{:S(2)}) collective-permute-start(f32[2,384,128]{2,1,0:T(8,128)S(1)} %get-tuple-element.24), channel_id=1, source_target_pairs={{0,64},{64,0},{1,65},{65,1},{2,66},{66,2},{3,67},{67,3},{4,68},{68... | collective-permute-start | bytes 1179656 | tf_op jit(solution)/shard_map/projections/ppermute | solution.py:368
  69.5 6.0 %collective-permute-start.3 = (f32[2,384,128]{2,1,0:T(8,128)S(1)}, f32[2,384,128]{2,1,0:T(8,128)S(1)}, u32[]{:S(2)}, u32[]{:S(2)}) collective-permute-start(f32[2,384,128]{2,1,0:T(8,128)S(1)} %bitcast.5), channel_id=1, source_target_pairs={{0,64},{64,0},{1,65},{65,1},{2,66},{66,2},{3,67},{67,3},{4,68},{68... | collective-permute-start | bytes 1179656 | tf_op jit(solution)/shard_map/share_core/ppermute | solution.py:382

commit v8 on v7

--- a/solution.py
+++ b/solution.py
@@ -14,7 +14,8 @@
 WEIGHT_FLOPS = 1_000_000_000
 EDGE_FLOPS = 1_000_000_000
 TILE_AXES = ("x_hi", "z", "y")
-PLANE_AXES = ("x_lo", "x_hi", "y")
+SPREAD_AXES = ("z", "y", "x_hi")
+PLANE_AXES = ("y", "x_lo", "x_hi")
 CELL_AXES = ("x_lo", "core", "x_hi", "z", "y")
 VMEM = pl.BlockSpec(memory_space=pltpu.VMEM)
 HBM = pl.BlockSpec(memory_space=pltpu.HBM)
@@ -102,10 +103,13 @@
 
 def weighting_kernel(
     snap_hbm, dens_hbm, speed_hbm, offs_hbm,
-    weighted, edge_scale, begin_rim, end_rim,
-    snap, dens, speed, offs, rows_ref, sems,
+    weighted_send, snap_send, weighted_keep, edge_scale, begin_rim, end_rim,
+    snap, weighted, dens, speed, offs, rows_ref, sems, out_sems,
 ):
     cells = snap.shape[1]
+    half = COMPONENTS // 2
+    kept = lax.axis_index("core") * half
+    sent = half - kept
     starts = list(range(0, cells, BLOCK))
     bounds = [0] + [start + HALO for start in starts[1:]] + [cells]
     vectors = ((dens_hbm, dens), (speed_hbm, speed), (offs_hbm, offs))
@@ -131,8 +135,14 @@
     columns = rows_ref[...].T
     edge_scale[0:HALO] = columns[0:HALO]
     edge_scale[HALO:] = columns[cells - HALO : cells]
+    leaving = []
     for i, begin in enumerate(starts):
         copies[i].wait()
+        if i == 1:
+            leaving.append(
+                pltpu.make_async_copy(snap_hbm.at[pl.ds(sent, half)], snap_send, out_sems.at[2 * len(starts)])
+            )
+            leaving[-1].start()
         stop = begin + BLOCK
         low, high = max(begin - HALO, 0), min(stop + HALO, bounds[i + 1])
         values = weigh_rows(
@@ -143,30 +153,48 @@
         )
         for component in range(COMPONENTS):
             weighted[component, begin:stop] = values[component]
+        for first, target in ((sent, weighted_send), (kept, weighted_keep)):
+            rows = pl.ds(begin, BLOCK)
+            leaving.append(
+                pltpu.make_async_copy(
+                    weighted.at[pl.ds(first, half), rows],
+                    target.at[:, rows],
+                    out_sems.at[2 * i + int(target is weighted_keep)],
+                )
+            )
+            leaving[-1].start()
     begin_rim[...] = snap[:, 0 : 2 * HALO]
     end_rim[...] = snap[:, cells - 2 * HALO :]
+    for copy in leaving:
+        copy.wait()
 
 
 def weigh(snapshots, density, sound_speed, offsets):
     components, cells, width = snapshots.shape
+    half = (components // 2, cells, width)
+    field = jax.ShapeDtypeStruct(half, jnp.bfloat16)
     rim = jax.ShapeDtypeStruct((components, 2 * HALO, width), jnp.bfloat16)
     return pl.pallas_call(
         weighting_kernel,
         out_shape=(
-            jax.ShapeDtypeStruct(snapshots.shape, jnp.bfloat16),
+            field,
+            field,
+            pltpu.HBM(half, jnp.bfloat16),
             jax.ShapeDtypeStruct((2 * HALO, 8), jnp.float32),
             rim,
             rim,
         ),
         in_specs=[HBM] * 4,
-        out_specs=(VMEM,) * 4,
+        out_specs=(VMEM, VMEM, HBM, VMEM, VMEM, VMEM),
         scratch_shapes=[
+            pltpu.VMEM(snapshots.shape, jnp.bfloat16),
             pltpu.VMEM(snapshots.shape, jnp.bfloat16),
             pltpu.VMEM((1, cells), jnp.float32),
             pltpu.VMEM((1, cells), jnp.float32),
             pltpu.VMEM((1, cells), jnp.int32),
             pltpu.VMEM((8, 1024), jnp.float32),
             pltpu.SemaphoreType.DMA((cells // BLOCK + 3,)),
+            pltpu.SemaphoreType.DMA((2 * (cells // BLOCK) + 1,)),
         ],
         compiler_params=PARAMS,
         cost_estimate=pl.CostEstimate(flops=WEIGHT_FLOPS, bytes_accessed=6_000_000, transcendentals=0),
@@ -225,24 +253,20 @@
     return jnp.dot(mode, jnp.concatenate(parts, axis=0), preferred_element_type=jnp.float32).T
 
 
-def sent_kernel(snap_hbm, weighted, edges, rot, send, rotation_t, snap_keep, snap, sems):
+def sent_kernel(snap_hbm, snap, weighted, edges, rot, send, rotation_t, snap_keep, sem):
     half, _, width = snap.shape
     kept = lax.axis_index("core") * half
     sent = half - kept
-    copies = [
-        pltpu.make_async_copy(snap_hbm.at[sent + place], snap.at[place], sems.at[place])
-        for place in range(half)
-    ]
-    copies.append(pltpu.make_async_copy(snap_hbm.at[pl.ds(kept, half)], snap_keep, sems.at[half]))
-    for copy in copies:
-        copy.start()
+    load = pltpu.make_async_copy(snap_hbm.at[pl.ds(kept, half)], snap_keep, sem)
+    load.start()
     tiles, padded, modes = rot.shape
     rows = width // tiles
     shape = (width, tiles * padded)
     target = lax.broadcasted_iota(jnp.int32, shape, 0)
     source = lax.broadcasted_iota(jnp.int32, shape, 1)
     within = source & (padded - 1)
-    tile = (source - within) // padded
+    slot = (source - within) // padded
+    tile = (slot & 1) * (tiles // 2) + (slot >> 1)
     chosen = jnp.logical_and(target == tile * rows + within, within < rows)
     compact = jnp.dot(
         chosen.astype(jnp.float32).astype(jnp.bfloat16),
@@ -252,31 +276,26 @@
     turned = compact.T.astype(jnp.bfloat16)
     rotation_t[...] = turned
     for place in range(half):
-        copies[place].wait()
-        send[place] = totals_of(turned, snap[place], weighted.at[sent + place], edges.at[sent + place])
-    copies[half].wait()
-
-
-def project_sent(snapshots, weighted, edges, rotation):
-    components, cells, width = snapshots.shape
-    half = (components // 2, cells, width)
+        send[place] = totals_of(turned, snap[place], weighted.at[place], edges.at[sent + place])
+    load.wait()
+
+
+def project_sent(snapshots, snap_send, weighted_send, edges, rotation):
+    half, _, width = snap_send.shape
     modes = rotation.shape[2]
     return pl.pallas_call(
         sent_kernel,
         out_shape=(
-            jax.ShapeDtypeStruct((components // 2, width, modes), jnp.float32),
+            jax.ShapeDtypeStruct((half, width, modes), jnp.float32),
             jax.ShapeDtypeStruct((modes, width), jnp.bfloat16),
-            jax.ShapeDtypeStruct(half, jnp.bfloat16),
+            jax.ShapeDtypeStruct(snap_send.shape, jnp.bfloat16),
         ),
-        in_specs=[HBM, VMEM, VMEM, VMEM],
+        in_specs=[HBM, VMEM, VMEM, VMEM, VMEM],
         out_specs=(VMEM, VMEM, VMEM),
-        scratch_shapes=[
-            pltpu.VMEM(half, jnp.bfloat16),
-            pltpu.SemaphoreType.DMA((components // 2 + 1,)),
-        ],
+        scratch_shapes=[pltpu.SemaphoreType.DMA],
         compiler_params=PARAMS,
         cost_estimate=pl.CostEstimate(flops=400_000_000, bytes_accessed=3_000_000, transcendentals=0),
-    )(snapshots, weighted, edges, rotation)
+    )(snapshots, snap_send, weighted_send, edges, rotation)
 
 
 def kept_kernel(snap, weighted, edges, rotation_t, keep):
@@ -284,7 +303,7 @@
     kept = lax.axis_index("core") * half
     for place in range(half):
         keep[place] = totals_of(
-            rotation_t[...], snap[place], weighted.at[kept + place], edges.at[kept + place]
+            rotation_t[...], snap[place], weighted.at[place], edges.at[kept + place]
         )
 
 
@@ -359,14 +378,18 @@
         outer = lax.ppermute(outer, CELL_AXES, across)
         inner = lax.ppermute(inner, CELL_AXES, inside)
     with jax.named_scope("rotation_rows"):
-        full_rotation = lax.all_to_all(rows, TILE_AXES, 0, 0)
+        full_rotation = lax.all_to_all(rows, SPREAD_AXES, 0, 0)
     with jax.named_scope("weighting"):
-        weighted, edge_scale, begin, end = weigh(resident, density, sound_speed, offsets)
+        weighted_send, snap_send, weighted_keep, edge_scale, begin, end = weigh(
+            resident, density, sound_speed, offsets
+        )
         edges = weigh_edges(begin, end, edge_scale, outer, inner)
     with jax.named_scope("projections"):
-        send, rotation_t, snap_keep = project_sent(resident, weighted, edges, full_rotation)
+        send, rotation_t, snap_keep = project_sent(
+            resident, snap_send, weighted_send, edges, full_rotation
+        )
         received = lax.ppermute(send, "core", swap)
-        keep = project_kept(snap_keep, weighted, edges, rotation_t)
+        keep = project_kept(snap_keep, weighted_keep, edges, rotation_t)
         mine = keep + received
     modes = mine.shape[2]
     members = lax.axis_size(PLANE_AXES)

time: 76.6 us -> 75.5 us (0.986)
  starting transfers between devices: 29.9 us -> 28.5 us
    ppermute x1, starting transfers between devices: 1.84 us -> 0.48 us  [on_device(): received = lax.ppermute(send, 'core', swap)]
  transfers between devices with their start and end apart: 5 -> 5, of which waited for: 2 -> 2; matrix products, arithmetic and copies ran while one was open for 0% -> 0% of each run, Pallas kernels for 7% -> 9%
where the time goes in v8:
time: 75.5 us; the launch traced here: 75.2 us
  blocking collectives  35.3 us (47%)
  starting transfers between devices  28.5 us (38%)
  Pallas kernels  10.3 us (14%)
  waiting for transfers between devices  0.88 us (1%)
    all_to_all x2, blocking collectives, spread(): lax.all_to_all(jnp.broadcast_to(block[None], (count,) + block.shape), axe...  24 us
    all_to_all x1, starting transfers between devices, on_device(): full_rotation = lax.all_to_all(rows, SPREAD_AXES, 0, 0)  15.1 us
    all_to_all x1, blocking collectives, on_device(): piece = jnp.sum(lax.all_to_all(pieces, PLANE_AXES, 0, 0), axis=0)  11.3 us
    ppermute x1, starting transfers between devices, on_device(): outer = lax.ppermute(outer, CELL_AXES, across)  8.25 us
    ppermute x1, starting transfers between devices, on_device(): other = lax.ppermute(mine, 'core', swap)  4.59 us
    pallas_call x1, Pallas kernels, weigh(): pl.pallas_call(weighting_kernel, out_shape=(field, field, pltpu.HBM(half,...  4.56 us
  transfers between devices with their start and end apart: 5, of which 2 were waited for; matrix products, arithmetic and copies ran while one was open for 0% of the time, Pallas kernels for 9%

profile of v8, /device:TPU:1, one launch (start us, length us, event | category | flops | bytes accessed | tf_op | source)
XLA Modules:
  0.0 75.2 jit_solution(2310845705926504708)
XLA Ops:
  0.0 1.4 %start.1 = (bf16[2,32,384]{2,1,0:T(8,128)(2,1)S(1)}, bf16[2,32,384]{2,1,0:T(8,128)(2,1)S(1)}, bf16[64,8,128]{2,1,0:T(8,128)(2,1)}) custom-call(bf16[4,960,384]{2,1,0:T(8,128)(2,1)} %snap_hbm.3, bf16[6,128]{1,0:T(8,128)(2,1)} %rot_hbm.1), custom_call_target="tpu_custom_call" | custom-call | tf_op jit(solution)/shard_map/start/pallas_call | solution.py:62
  1.4 15.1 %all-to-all-start = ((bf16[64,8,128]{2,1,0:T(8,128)(2,1)}), bf16[64,8,128]{2,1,0:T(8,128)(2,1)S(1)}, u32[]{:S(2)}, u32[]{:S(2)}) async-start(bf16[64,8,128]{2,1,0:T(8,128)(2,1)} %get-tuple-element.24), calls=%async_computation | async-start | bytes 262144 | tf_op jit(solution)/shard_map/rotation_rows/all_to_all | solution.py:381
  16.5 8.3 %collective-permute-start = (bf16[2,32,384]{2,1,0:T(8,128)(2,1)S(1)}, bf16[2,32,384]{2,1,0:T(8,128)(2,1)S(1)}, u32[]{:S(2)}, u32[]{:S(2)}) collective-permute-start(bf16[2,32,384]{2,1,0:T(8,128)(2,1)S(1)} %get-tuple-element.22), channel_id=1, source_target_pairs={{0,255},{1,2},{2,1},{3,4},{4,3},{5,6},{6,5},{7,8},{8,7},{9,10},{10... | collective-permute-start | bytes 147464 | tf_op jit(solution)/shard_map/halo/ppermute | solution.py:378
  24.8 0.0 collective-permute-start.1
  24.8 4.6 %weighting.2 = (bf16[2,960,384]{2,1,0:T(8,128)(2,1)S(1)}, bf16[2,960,384]{2,1,0:T(8,128)(2,1)S(1)}, bf16[2,960,384]{2,1,0:T(8,128)(2,1)}, f32[64,8]{1,0:T(8,128)...) custom-call(bf16[4,960,384]{2,1,0:T(8,128)(2,1)} %snap_hbm.3, f32[1,960]{1,0:T(1,128)} %bitcast.8, ...), custom_call_target="tpu_custom_call" | custom-call | flops 1000000000 | bytes 6000000 | tf_op jit(solution)/shard_map/weighting/pallas_call | solution.py:177
  29.3 0.0 collective-permute-done.outer
  29.3 0.0 collective-permute-done.1.inner
  29.4 0.3 weighting.3.edges
  29.6 0.0 all-to-all-done.rot
  29.6 0.0 copy-start
  29.7 1.5 %projections.2 = (f32[2,384,128]{2,1,0:T(8,128)S(1)}, bf16[128,384]{1,0:T(8,128)(2,1)S(1)}, bf16[2,960,384]{2,1,0:T(8,128)(2,1)S(1)}) custom-call(bf16[4,960,384]{2,1,0:T(8,128)(2,1)} %snap_hbm.3, bf16[2,960,384]{2,1,0:T(8,128)(2,1)S(1)} %get-tuple-element.17.snap, bf16[2,960,384]{2,1,0:T(8,128)(2,1)S(1)} %get-tuple-element.18.weighted, ...), custom_call_target="tpu_custom_call" | custom-call | flops 400000000 | bytes 3000000 | tf_op jit(solution)/shard_map/projections/pallas_call | solution.py:286
  31.2 0.5 collective-permute-start.2
  31.7 0.0 copy-done
  31.7 1.1 %projections.3 = f32[2,384,128]{2,1,0:T(8,128)S(1)} custom-call(bf16[2,960,384]{2,1,0:T(8,128)(2,1)S(1)} %get-tuple-element.25.snap, bf16[2,960,384]{2,1,0:T(8,128)(2,1)S(1)} %copy-done, bf16[4,64,384]{2,1,0:T(8,128)(2,1)S(1)} %weighting.3.edges, bf16[128,384]{1,0:T(8,128)(2,1)S(1)} %get-tuple-element.27.rotation_t), custom_call_target="tpu_custom_call" | custom-call | flops 400000000 | bytes 3000000 | tf_op jit(solution)/shard_map/projections/pallas_call | solution.py:313
  32.7 0.3 collective-permute-done.2
  33.1 11.3 %all_to_all.20 = f32[16,48,128]{2,1,0:T(8,128)S(1)} all-to-all(f32[16,48,128]{2,1,0:T(8,128)S(1)} %bitcast.7), channel_id=1, replica_groups=mesh['x_lo'=2,'core'=2,'x_hi'=2,'z'=8,'y'=4] {'y','x_lo','x_hi'}, dimensions={0} | all-to-all | bytes 786432 | tf_op jit(solution)/shard_map/sum_plane/all_to_all | solution.py:398
  44.4 12.5 %all_to_all.21 = f32[8,48,128]{2,1,0:T(8,128)S(1)} all-to-all(f32[8,48,128]{2,1,0:T(8,128)S(1)} %broadcast_in_dim.4), channel_id=1, replica_groups=mesh['x_lo'=2,'core'=2,'x_hi'=2,'z'=8,'y'=4] {'z'}, dimensions={0} | all-to-all | bytes 393216 | tf_op jit(solution)/shard_map/sum_z/all_to_all | solution.py:365
  57.0 11.5 %all_to_all.22 = f32[16,48,128]{2,1,0:T(8,128)S(1)} all-to-all(f32[16,48,128]{2,1,0:T(8,128)S(1)} %broadcast_in_dim.5), channel_id=1, replica_groups=mesh['x_lo'=2,'core'=2,'x_hi'=2,'z'=8,'y'=4] {'y','x_lo','x_hi'}, dimensions={0} | all-to-all | bytes 786432 | tf_op jit(solution)/shard_map/share_plane/all_to_all | solution.py:365
  68.5 4.6 %collective-permute-start.3 = (f32[2,384,128]{2,1,0:T(8,128)S(1)}, f32[2,384,128]{2,1,0:T(8,128)S(1)}, u32[]{:S(2)}, u32[]{:S(2)}) collective-permute-start(f32[2,384,128]{2,1,0:T(8,128)S(1)} %bitcast.5), channel_id=1, source_target_pairs={{0,64},{64,0},{1,65},{65,1},{2,66},{66,2},{3,67},{67,3},{4,68},{68... | collective-permute-start | bytes 1179656 | tf_op jit(solution)/shard_map/share_core/ppermute | solution.py:405
  73.1 0.8 %share_core.2.begun = f32[4,384,128]{2,1,0:T(8,128)} custom-call(f32[2,384,128]{2,1,0:T(8,128)S(1)} %bitcast.6), custom_call_target="tpu_custom_call" | custom-call | bytes 1000000 | tf_op jit(solution)/shard_map/share_core/pallas_call | solution.py:339
  73.8 0.6 collective-permute-done.3.other
  74.4 0.8 %share_core.3 = f32[4,384,128]{2,1,0:T(8,128)} custom-call(f32[4,384,128]{2,1,0:T(8,128)} %share_core.2.begun, f32[2,384,128]{2,1,0:T(8,128)S(1)} %collective-permute-done.3.other), custom_call_target="tpu_custom_call", output_to_operand_aliasing={{}: (0, {})} | custom-call | bytes 1000000 | tf_op jit(solution)/shard_map/share_core/pallas_call | solution.py:351
  (6 shorter events, 0.1 us)
Async XLA Ops:
  1.4 28.3 %all-to-all-start = ((bf16[64,8,128]{2,1,0:T(8,128)(2,1)}), bf16[64,8,128]{2,1,0:T(8,128)(2,1)S(1)}, u32[]{:S(2)}, u32[]{:S(2)}) async-start(bf16[64,8,128]{2,1,0:T(8,128)(2,1)} %get-tuple-element.24), calls=%async_computation | async-start | bytes 262144 | tf_op jit(solution)/shard_map/rotation_rows/all_to_all | solution.py:381
  16.5 12.8 %collective-permute-start = (bf16[2,32,384]{2,1,0:T(8,128)(2,1)S(1)}, bf16[2,32,384]{2,1,0:T(8,128)(2,1)S(1)}, u32[]{:S(2)}, u32[]{:S(2)}) collective-permute-start(bf16[2,32,384]{2,1,0:T(8,128)(2,1)S(1)} %get-tuple-element.22), channel_id=1, source_target_pairs={{0,255},{1,2},{2,1},{3,4},{4,3},{5,6},{6,5},{7,8},{8,7},{9,10},{10... | collective-permute-start | bytes 147464 | tf_op jit(solution)/shard_map/halo/ppermute | solution.py:378
  24.8 4.6 %collective-permute-start.1 = (bf16[2,32,384]{2,1,0:T(8,128)(2,1)S(1)}, bf16[2,32,384]{2,1,0:T(8,128)(2,1)S(1)}, u32[]{:S(2)}, u32[]{:S(2)}) collective-permute-start(bf16[2,32,384]{2,1,0:T(8,128)(2,1)S(1)} %get-tuple-element.23), channel_id=1, source_target_pairs={{0,1},{1,0},{2,3},{3,2},{4,5},{5,4},{6,7},{7,6},{8,9},{9,8},{10,11... | collective-permute-start | bytes 147464 | tf_op jit(solution)/shard_map/halo/ppermute | solution.py:379
  29.6 2.0 %copy-start = (bf16[2,960,384]{2,1,0:T(8,128)(2,1)S(1)}, bf16[2,960,384]{2,1,0:T(8,128)(2,1)}, u32[]{:S(2)}) copy-start(bf16[2,960,384]{2,1,0:T(8,128)(2,1)} %get-tuple-element.26.weighted) | copy-start | bytes 4423684
  31.2 1.8 %collective-permute-start.2 = (f32[2,384,128]{2,1,0:T(8,128)S(1)}, f32[2,384,128]{2,1,0:T(8,128)S(1)}, u32[]{:S(2)}, u32[]{:S(2)}) collective-permute-start(f32[2,384,128]{2,1,0:T(8,128)S(1)} %get-tuple-element.28), channel_id=1, source_target_pairs={{0,64},{64,0},{1,65},{65,1},{2,66},{66,2},{3,67},{67,3},{4,68},{68... | collective-permute-start | bytes 1179656 | tf_op jit(solution)/shard_map/projections/ppermute | solution.py:391
  68.5 5.9 %collective-permute-start.3 = (f32[2,384,128]{2,1,0:T(8,128)S(1)}, f32[2,384,128]{2,1,0:T(8,128)S(1)}, u32[]{:S(2)}, u32[]{:S(2)}) collective-permute-start(f32[2,384,128]{2,1,0:T(8,128)S(1)} %bitcast.5), channel_id=1, source_target_pairs={{0,64},{64,0},{1,65},{65,1},{2,66},{66,2},{3,67},{67,3},{4,68},{68... | collective-permute-start | bytes 1179656 | tf_op jit(solution)/shard_map/share_core/ppermute | solution.py:405

commit v9 on v7

--- a/solution.py
+++ b/solution.py
@@ -13,8 +13,10 @@
 PADDED = 8
 WEIGHT_FLOPS = 1_000_000_000
 EDGE_FLOPS = 1_000_000_000
+START_BYTES = 100_000_000
 TILE_AXES = ("x_hi", "z", "y")
-PLANE_AXES = ("x_lo", "x_hi", "y")
+SPREAD_AXES = ("z", "y", "x_hi")
+PLANE_AXES = ("y", "x_lo", "x_hi")
 CELL_AXES = ("x_lo", "core", "x_hi", "z", "y")
 VMEM = pl.BlockSpec(memory_space=pltpu.VMEM)
 HBM = pl.BlockSpec(memory_space=pltpu.HBM)
@@ -71,6 +73,7 @@
             pltpu.SemaphoreType.DMA((3,)),
         ],
         compiler_params=PARAMS,
+        cost_estimate=pl.CostEstimate(flops=0, bytes_accessed=START_BYTES, transcendentals=0),
     )(snapshots, in_hbm(rotation))
 
 
@@ -101,26 +104,11 @@
 
 
 def weighting_kernel(
-    snap_hbm, dens_hbm, speed_hbm, offs_hbm,
-    weighted, edge_scale, begin_rim, end_rim,
-    snap, dens, speed, offs, rows_ref, sems,
+    snap, dens, speed, offs, weighted_hbm, edge_scale, begin_rim, end_rim, weighted, rows_ref, sems
 ):
     cells = snap.shape[1]
-    starts = list(range(0, cells, BLOCK))
-    bounds = [0] + [start + HALO for start in starts[1:]] + [cells]
-    vectors = ((dens_hbm, dens), (speed_hbm, speed), (offs_hbm, offs))
-    small = [
-        pltpu.make_async_copy(source, target, sems.at[len(starts) + i])
-        for i, (source, target) in enumerate(vectors)
-    ]
-    copies = []
-    for i in range(len(starts)):
-        rows = pl.ds(bounds[i], bounds[i + 1] - bounds[i])
-        copies.append(pltpu.make_async_copy(snap_hbm.at[:, rows], snap.at[:, rows], sems.at[i]))
-    for copy in small + copies:
-        copy.start()
-    for copy in small:
-        copy.wait()
+    begin_rim[...] = snap[:, 0 : 2 * HALO]
+    end_rim[...] = snap[:, cells - 2 * HALO :]
     density = dens[...]
     sound = speed[...]
     rows_ref[...] = jnp.zeros_like(rows_ref)
@@ -131,10 +119,10 @@
     columns = rows_ref[...].T
     edge_scale[0:HALO] = columns[0:HALO]
     edge_scale[HALO:] = columns[cells - HALO : cells]
-    for i, begin in enumerate(starts):
-        copies[i].wait()
+    copies = []
+    for begin in range(0, cells, BLOCK):
         stop = begin + BLOCK
-        low, high = max(begin - HALO, 0), min(stop + HALO, bounds[i + 1])
+        low, high = max(begin - HALO, 0), min(stop + HALO, cells)
         values = weigh_rows(
             columns[begin:stop],
             begin - low,
@@ -143,8 +131,13 @@
         )
         for component in range(COMPONENTS):
             weighted[component, begin:stop] = values[component]
-    begin_rim[...] = snap[:, 0 : 2 * HALO]
-    end_rim[...] = snap[:, cells - 2 * HALO :]
+        rows = pl.ds(begin, BLOCK)
+        copies.append(
+            pltpu.make_async_copy(weighted.at[:, rows], weighted_hbm.at[:, rows], sems.at[len(copies)])
+        )
+        copies[-1].start()
+    for copy in copies:
+        copy.wait()
 
 
 def weigh(snapshots, density, sound_speed, offsets):
@@ -153,28 +146,25 @@
     return pl.pallas_call(
         weighting_kernel,
         out_shape=(
-            jax.ShapeDtypeStruct(snapshots.shape, jnp.bfloat16),
+            pltpu.HBM(snapshots.shape, jnp.bfloat16),
             jax.ShapeDtypeStruct((2 * HALO, 8), jnp.float32),
             rim,
             rim,
         ),
-        in_specs=[HBM] * 4,
-        out_specs=(VMEM,) * 4,
+        in_specs=[VMEM] * 4,
+        out_specs=(HBM, VMEM, VMEM, VMEM),
         scratch_shapes=[
             pltpu.VMEM(snapshots.shape, jnp.bfloat16),
-            pltpu.VMEM((1, cells), jnp.float32),
-            pltpu.VMEM((1, cells), jnp.float32),
-            pltpu.VMEM((1, cells), jnp.int32),
             pltpu.VMEM((8, 1024), jnp.float32),
-            pltpu.SemaphoreType.DMA((cells // BLOCK + 3,)),
+            pltpu.SemaphoreType.DMA((cells // BLOCK,)),
         ],
         compiler_params=PARAMS,
         cost_estimate=pl.CostEstimate(flops=WEIGHT_FLOPS, bytes_accessed=6_000_000, transcendentals=0),
     )(
         snapshots,
-        in_hbm(density.reshape(1, cells)),
-        in_hbm(sound_speed.reshape(1, cells)),
-        in_hbm(offsets.reshape(1, cells)),
+        density.reshape(1, cells),
+        sound_speed.reshape(1, cells),
+        offsets.reshape(1, cells),
     )
 
 
@@ -216,24 +206,31 @@
     )(begin, end, edge_scale, outer, inner)
 
 
-def totals_of(rotation_t, snap, weighted, edges):
-    cells = snap.shape[0]
-    mode = lax.dot_general(
+def modes_of(rotation_t, snap):
+    return lax.dot_general(
         rotation_t, snap, (((1,), (1,)), ((), ())), preferred_element_type=jnp.float32
     ).astype(jnp.bfloat16)
+
+
+def totals_of(mode, weighted, edges):
+    cells = weighted.shape[0]
     parts = [edges[0:HALO], weighted[HALO : cells - HALO], edges[HALO:]]
     return jnp.dot(mode, jnp.concatenate(parts, axis=0), preferred_element_type=jnp.float32).T
 
 
-def sent_kernel(snap_hbm, weighted, edges, rot, send, rotation_t, snap_keep, snap, sems):
-    half, _, width = snap.shape
+def sent_kernel(
+    weighted_hbm, snap, edges, rot, send, rotation_t, weighted_keep, weighted, sems
+):
+    half, _, width = weighted.shape
     kept = lax.axis_index("core") * half
     sent = half - kept
     copies = [
-        pltpu.make_async_copy(snap_hbm.at[sent + place], snap.at[place], sems.at[place])
+        pltpu.make_async_copy(weighted_hbm.at[sent + place], weighted.at[place], sems.at[place])
         for place in range(half)
     ]
-    copies.append(pltpu.make_async_copy(snap_hbm.at[pl.ds(kept, half)], snap_keep, sems.at[half]))
+    copies.append(
+        pltpu.make_async_copy(weighted_hbm.at[pl.ds(kept, half)], weighted_keep, sems.at[half])
+    )
     for copy in copies:
         copy.start()
     tiles, padded, modes = rot.shape
@@ -242,7 +239,8 @@
     target = lax.broadcasted_iota(jnp.int32, shape, 0)
     source = lax.broadcasted_iota(jnp.int32, shape, 1)
     within = source & (padded - 1)
-    tile = (source - within) // padded
+    slot = (source - within) // padded
+    tile = (slot & 1) * (tiles // 2) + (slot >> 1)
     chosen = jnp.logical_and(target == tile * rows + within, within < rows)
     compact = jnp.dot(
         chosen.astype(jnp.float32).astype(jnp.bfloat16),
@@ -251,45 +249,45 @@
     )
     turned = compact.T.astype(jnp.bfloat16)
     rotation_t[...] = turned
+    mode = [modes_of(turned, snap[sent + place]) for place in range(half)]
     for place in range(half):
         copies[place].wait()
-        send[place] = totals_of(turned, snap[place], weighted.at[sent + place], edges.at[sent + place])
+        send[place] = totals_of(mode[place], weighted.at[place], edges.at[sent + place])
     copies[half].wait()
 
 
-def project_sent(snapshots, weighted, edges, rotation):
+def project_sent(weighted, snapshots, edges, rotation):
     components, cells, width = snapshots.shape
-    half = (components // 2, cells, width)
+    half = components // 2
     modes = rotation.shape[2]
     return pl.pallas_call(
         sent_kernel,
         out_shape=(
-            jax.ShapeDtypeStruct((components // 2, width, modes), jnp.float32),
+            jax.ShapeDtypeStruct((half, width, modes), jnp.float32),
             jax.ShapeDtypeStruct((modes, width), jnp.bfloat16),
-            jax.ShapeDtypeStruct(half, jnp.bfloat16),
+            jax.ShapeDtypeStruct((half, cells, width), jnp.bfloat16),
         ),
         in_specs=[HBM, VMEM, VMEM, VMEM],
         out_specs=(VMEM, VMEM, VMEM),
         scratch_shapes=[
-            pltpu.VMEM(half, jnp.bfloat16),
-            pltpu.SemaphoreType.DMA((components // 2 + 1,)),
+            pltpu.VMEM((half, cells, width), jnp.bfloat16),
+            pltpu.SemaphoreType.DMA((half + 1,)),
         ],
         compiler_params=PARAMS,
         cost_estimate=pl.CostEstimate(flops=400_000_000, bytes_accessed=3_000_000, transcendentals=0),
-    )(snapshots, weighted, edges, rotation)
+    )(in_hbm(weighted), snapshots, edges, rotation)
 
 
 def kept_kernel(snap, weighted, edges, rotation_t, keep):
-    half = snap.shape[0]
+    half = weighted.shape[0]
     kept = lax.axis_index("core") * half
     for place in range(half):
-        keep[place] = totals_of(
-            rotation_t[...], snap[place], weighted.at[kept + place], edges.at[kept + place]
-        )
-
-
-def project_kept(snap, weighted, edges, rotation_t):
-    half, _, width = snap.shape
+        mode = modes_of(rotation_t[...], snap[kept + place])
+        keep[place] = totals_of(mode, weighted.at[place], edges.at[kept + place])
+
+
+def project_kept(snapshots, weighted, edges, rotation_t):
+    half, _, width = weighted.shape
     modes = rotation_t.shape[0]
     return pl.pallas_call(
         kept_kernel,
@@ -298,7 +296,7 @@
         out_specs=VMEM,
         compiler_params=PARAMS,
         cost_estimate=pl.CostEstimate(flops=400_000_000, bytes_accessed=3_000_000, transcendentals=0),
-    )(snap, weighted, edges, rotation_t)
+    )(snapshots, weighted, edges, rotation_t)
 
 
 def place_own_kernel(mine, out, sem):
@@ -349,24 +347,23 @@
 def on_device(snapshots, density, sound_speed, offsets, rotation):
     components, cells, width = snapshots.shape
     count = lax.axis_size(CELL_AXES)
-    resident = in_hbm(snapshots)
     inside = [(i, i ^ 1) for i in range(count)]
     across = [(i, (i + 1 if i % 2 else i - 1) % count) for i in range(count)]
     swap = [(0, 1), (1, 0)]
     with jax.named_scope("start"):
-        inner, outer, rows = start(resident, rotation, lax.axis_size(TILE_AXES))
+        inner, outer, rows = start(in_hbm(snapshots), rotation, lax.axis_size(TILE_AXES))
     with jax.named_scope("halo"):
         outer = lax.ppermute(outer, CELL_AXES, across)
         inner = lax.ppermute(inner, CELL_AXES, inside)
     with jax.named_scope("rotation_rows"):
-        full_rotation = lax.all_to_all(rows, TILE_AXES, 0, 0)
+        full_rotation = lax.all_to_all(rows, SPREAD_AXES, 0, 0)
     with jax.named_scope("weighting"):
-        weighted, edge_scale, begin, end = weigh(resident, density, sound_speed, offsets)
+        weighted, edge_scale, begin, end = weigh(snapshots, density, sound_speed, offsets)
         edges = weigh_edges(begin, end, edge_scale, outer, inner)
     with jax.named_scope("projections"):
-        send, rotation_t, snap_keep = project_sent(resident, weighted, edges, full_rotation)
+        send, rotation_t, weighted_keep = project_sent(weighted, snapshots, edges, full_rotation)
         received = lax.ppermute(send, "core", swap)
-        keep = project_kept(snap_keep, weighted, edges, rotation_t)
+        keep = project_kept(snapshots, weighted_keep, edges, rotation_t)
         mine = keep + received
     modes = mine.shape[2]
     members = lax.axis_size(PLANE_AXES)

time: 76.6 us -> 76.9 us (level)
  transfers between devices with their start and end apart: 5 -> 5, of which waited for: 2 -> 3; matrix products, arithmetic and copies ran while one was open for 0% -> 0% of each run, Pallas kernels for 7% -> 6%
where the time goes in v9:
time: 76.9 us; the launch traced here: 76.6 us
  blocking collectives  35.3 us (46%)
  starting transfers between devices  29.6 us (38%)
  Pallas kernels  9.85 us (13%)
  waiting for transfers between devices  1.55 us (2%)
    all_to_all x2, blocking collectives, spread(): lax.all_to_all(jnp.broadcast_to(block[None], (count,) + block.shape), axe...  24 us
    all_to_all x1, starting transfers between devices, on_device(): full_rotation = lax.all_to_all(rows, SPREAD_AXES, 0, 0)  15.1 us
    all_to_all x1, blocking collectives, on_device(): piece = jnp.sum(lax.all_to_all(pieces, PLANE_AXES, 0, 0), axis=0)  11.3 us
    ppermute x1, starting transfers between devices, on_device(): outer = lax.ppermute(outer, CELL_AXES, across)  8.25 us
    ppermute x1, starting transfers between devices, on_device(): other = lax.ppermute(mine, 'core', swap)  4.59 us
    pallas_call x1, Pallas kernels, project_sent(): pl.pallas_call(sent_kernel, out_shape=(jax.ShapeDtypeStruct((half, width,...  2.78 us
    pallas_call x1, Pallas kernels, weigh(): pl.pallas_call(weighting_kernel, out_shape=(pltpu.HBM(snapshots.shape, jn...  2.72 us
    ppermute x1, starting transfers between devices, on_device(): received = lax.ppermute(send, 'core', swap)  1.66 us
  transfers between devices with their start and end apart: 5, of which 3 were waited for; matrix products, arithmetic and copies ran while one was open for 0% of the time, Pallas kernels for 6%

profile of v9, /device:TPU:1, one launch (start us, length us, event | category | flops | bytes accessed | tf_op | source)
XLA Modules:
  0.0 76.6 jit_solution(2968599890888441921)
XLA Ops:
  0.0 0.0 copy-start
  0.0 0.0 copy-start.3
  0.0 0.0 copy-start.2
  0.0 0.0 copy-start.1
  0.0 1.5 %start.1 = (bf16[2,32,384]{2,1,0:T(8,128)(2,1)S(1)}, bf16[2,32,384]{2,1,0:T(8,128)(2,1)S(1)}, bf16[64,8,128]{2,1,0:T(8,128)(2,1)}) custom-call(bf16[4,960,384]{2,1,0:T(8,128)(2,1)} %snap.7, bf16[6,128]{1,0:T(8,128)(2,1)} %rot_hbm.1), custom_call_target="tpu_custom_call" | custom-call | bytes 100000000 | tf_op jit(solution)/shard_map/start/pallas_call | solution.py:63
  1.6 15.1 %all-to-all-start = ((bf16[64,8,128]{2,1,0:T(8,128)(2,1)}), bf16[64,8,128]{2,1,0:T(8,128)(2,1)S(1)}, u32[]{:S(2)}, u32[]{:S(2)}) async-start(bf16[64,8,128]{2,1,0:T(8,128)(2,1)} %get-tuple-element.21), calls=%async_computation | async-start | bytes 262144 | tf_op jit(solution)/shard_map/rotation_rows/all_to_all | solution.py:359
  16.7 8.3 %collective-permute-start = (bf16[2,32,384]{2,1,0:T(8,128)(2,1)S(1)}, bf16[2,32,384]{2,1,0:T(8,128)(2,1)S(1)}, u32[]{:S(2)}, u32[]{:S(2)}) collective-permute-start(bf16[2,32,384]{2,1,0:T(8,128)(2,1)S(1)} %get-tuple-element.19), channel_id=1, source_target_pairs={{0,255},{1,2},{2,1},{3,4},{4,3},{5,6},{6,5},{7,8},{8,7},{9,10},{10... | collective-permute-start | bytes 147464 | tf_op jit(solution)/shard_map/halo/ppermute | solution.py:356
  24.9 0.0 collective-permute-start.1
  24.9 0.0 copy-done
  24.9 0.0 copy-done.3
  24.9 0.0 copy-done.2
  25.0 0.0 copy-done.1
  25.0 2.7 %weighting.2 = (bf16[4,960,384]{2,1,0:T(8,128)(2,1)}, f32[64,8]{1,0:T(8,128)S(1)}, bf16[4,64,384]{2,1,0:T(8,128)(2,1)S(1)}, bf16[4,64,384]{2,1,0:T(8,128)(2,1)S(1)}) custom-call(bf16[4,960,384]{2,1,0:T(8,128)(2,1)S(1)} %copy-done, f32[1,960]{1,0:T(1,128)S(1)} %bitcast.7, f32[1,960]{1,0:T(1,128)S(1)} %bitcast.8, s32[1,960]{1,0:T(1,128)S(1)} %bitcast.9), custom_call_target="tpu_custom_call" | custom-call | flops 1000000000 | bytes 6000000 | tf_op jit(solution)/shard_map/weighting/pallas_call | solution.py:146
  27.7 0.7 collective-permute-done.outer
  28.4 0.0 collective-permute-done.1.inner
  28.4 0.3 weighting.3.edges
  28.6 0.0 all-to-all-done.rot
  28.6 2.8 %projections.2 = (f32[2,384,128]{2,1,0:T(8,128)S(1)}, bf16[128,384]{1,0:T(8,128)(2,1)S(1)}, bf16[2,960,384]{2,1,0:T(8,128)(2,1)S(1)}) custom-call(bf16[4,960,384]{2,1,0:T(8,128)(2,1)} %get-tuple-element.15.weighted_hbm, bf16[4,960,384]{2,1,0:T(8,128)(2,1)S(1)} %copy-done, bf16[4,64,384]{2,1,0:T(8,128)(2,1)S(1)} %weighting.3.edges, ...), custom_call_target="tpu_custom_call" | custom-call | flops 400000000 | bytes 3000000 | tf_op jit(solution)/shard_map/projections/pallas_call | solution.py:263
  31.4 1.7 %collective-permute-start.2 = (f32[2,384,128]{2,1,0:T(8,128)S(1)}, f32[2,384,128]{2,1,0:T(8,128)S(1)}, u32[]{:S(2)}, u32[]{:S(2)}) collective-permute-start(f32[2,384,128]{2,1,0:T(8,128)S(1)} %get-tuple-element.24), channel_id=1, source_target_pairs={{0,64},{64,0},{1,65},{65,1},{2,66},{66,2},{3,67},{67,3},{4,68},{68... | collective-permute-start | bytes 1179656 | tf_op jit(solution)/shard_map/projections/ppermute | solution.py:365
  33.1 1.0 %projections.3 = f32[2,384,128]{2,1,0:T(8,128)S(1)} custom-call(bf16[4,960,384]{2,1,0:T(8,128)(2,1)S(1)} %copy-done, bf16[2,960,384]{2,1,0:T(8,128)(2,1)S(1)} %get-tuple-element.22.weighted, bf16[4,64,384]{2,1,0:T(8,128)(2,1)S(1)} %weighting.3.edges, bf16[128,384]{1,0:T(8,128)(2,1)S(1)} %get-tuple-element.23.rotation_t), custom_call_target="tpu_custom_call" | custom-call | flops 400000000 | bytes 3000000 | tf_op jit(solution)/shard_map/projections/pallas_call | solution.py:292
  34.1 0.3 collective-permute-done.2
  34.5 11.3 %all_to_all.20 = f32[16,48,128]{2,1,0:T(8,128)S(1)} all-to-all(f32[16,48,128]{2,1,0:T(8,128)S(1)} %bitcast.10), channel_id=1, replica_groups=mesh['x_lo'=2,'core'=2,'x_hi'=2,'z'=8,'y'=4] {'y','x_lo','x_hi'}, dimensions={0} | all-to-all | bytes 786432 | tf_op jit(solution)/shard_map/sum_plane/all_to_all | solution.py:372
  45.8 12.5 %all_to_all.21 = f32[8,48,128]{2,1,0:T(8,128)S(1)} all-to-all(f32[8,48,128]{2,1,0:T(8,128)S(1)} %broadcast_in_dim.4), channel_id=1, replica_groups=mesh['x_lo'=2,'core'=2,'x_hi'=2,'z'=8,'y'=4] {'z'}, dimensions={0} | all-to-all | bytes 393216 | tf_op jit(solution)/shard_map/sum_z/all_to_all | solution.py:344
  58.4 11.5 %all_to_all.22 = f32[16,48,128]{2,1,0:T(8,128)S(1)} all-to-all(f32[16,48,128]{2,1,0:T(8,128)S(1)} %broadcast_in_dim.5), channel_id=1, replica_groups=mesh['x_lo'=2,'core'=2,'x_hi'=2,'z'=8,'y'=4] {'y','x_lo','x_hi'}, dimensions={0} | all-to-all | bytes 786432 | tf_op jit(solution)/shard_map/share_plane/all_to_all | solution.py:344
  69.9 4.6 %collective-permute-start.3 = (f32[2,384,128]{2,1,0:T(8,128)S(1)}, f32[2,384,128]{2,1,0:T(8,128)S(1)}, u32[]{:S(2)}, u32[]{:S(2)}) collective-permute-start(f32[2,384,128]{2,1,0:T(8,128)S(1)} %bitcast.5), channel_id=1, source_target_pairs={{0,64},{64,0},{1,65},{65,1},{2,66},{66,2},{3,67},{67,3},{4,68},{68... | collective-permute-start | bytes 1179656 | tf_op jit(solution)/shard_map/share_core/ppermute | solution.py:379
  74.5 0.8 share_core.2.begun
  75.3 0.6 collective-permute-done.3.other
  75.9 0.8 share_core.3
  (6 shorter events, 0.1 us)
Async XLA Ops:
  0.0 24.9 %copy-start = (bf16[4,960,384]{2,1,0:T(8,128)(2,1)S(1)}, bf16[4,960,384]{2,1,0:T(8,128)(2,1)}, u32[]{:S(2)}) copy-start(bf16[4,960,384]{2,1,0:T(8,128)(2,1)} %snap.7) | copy-start | bytes 8847364
  0.0 24.9 %copy-start.3 = (s32[960]{0:T(1024)S(1)}, s32[960]{0:T(1024)}, u32[]{:S(2)}) copy-start(s32[960]{0:T(1024)} %param.8) | copy-start | bytes 11524
  0.0 24.9 %copy-start.2 = (f32[960]{0:T(1024)S(1)}, f32[960]{0:T(1024)}, u32[]{:S(2)}) copy-start(f32[960]{0:T(1024)} %param.7) | copy-start | bytes 11524
  0.0 25.0 %copy-start.1 = (f32[960]{0:T(1024)S(1)}, f32[960]{0:T(1024)}, u32[]{:S(2)}) copy-start(f32[960]{0:T(1024)} %param.6) | copy-start | bytes 11524
  1.6 27.1 %all-to-all-start = ((bf16[64,8,128]{2,1,0:T(8,128)(2,1)}), bf16[64,8,128]{2,1,0:T(8,128)(2,1)S(1)}, u32[]{:S(2)}, u32[]{:S(2)}) async-start(bf16[64,8,128]{2,1,0:T(8,128)(2,1)} %get-tuple-element.21), calls=%async_computation | async-start | bytes 262144 | tf_op jit(solution)/shard_map/rotation_rows/all_to_all | solution.py:359
  16.7 11.7 %collective-permute-start = (bf16[2,32,384]{2,1,0:T(8,128)(2,1)S(1)}, bf16[2,32,384]{2,1,0:T(8,128)(2,1)S(1)}, u32[]{:S(2)}, u32[]{:S(2)}) collective-permute-start(bf16[2,32,384]{2,1,0:T(8,128)(2,1)S(1)} %get-tuple-element.19), channel_id=1, source_target_pairs={{0,255},{1,2},{2,1},{3,4},{4,3},{5,6},{6,5},{7,8},{8,7},{9,10},{10... | collective-permute-start | bytes 147464 | tf_op jit(solution)/shard_map/halo/ppermute | solution.py:356
  24.9 3.4 %collective-permute-start.1 = (bf16[2,32,384]{2,1,0:T(8,128)(2,1)S(1)}, bf16[2,32,384]{2,1,0:T(8,128)(2,1)S(1)}, u32[]{:S(2)}, u32[]{:S(2)}) collective-permute-start(bf16[2,32,384]{2,1,0:T(8,128)(2,1)S(1)} %get-tuple-element.20), channel_id=1, source_target_pairs={{0,1},{1,0},{2,3},{3,2},{4,5},{5,4},{6,7},{7,6},{8,9},{9,8},{10,11... | collective-permute-start | bytes 147464 | tf_op jit(solution)/shard_map/halo/ppermute | solution.py:357
  31.4 3.0 %collective-permute-start.2 = (f32[2,384,128]{2,1,0:T(8,128)S(1)}, f32[2,384,128]{2,1,0:T(8,128)S(1)}, u32[]{:S(2)}, u32[]{:S(2)}) collective-permute-start(f32[2,384,128]{2,1,0:T(8,128)S(1)} %get-tuple-element.24), channel_id=1, source_target_pairs={{0,64},{64,0},{1,65},{65,1},{2,66},{66,2},{3,67},{67,3},{4,68},{68... | collective-permute-start | bytes 1179656 | tf_op jit(solution)/shard_map/projections/ppermute | solution.py:365
  69.9 5.9 %collective-permute-start.3 = (f32[2,384,128]{2,1,0:T(8,128)S(1)}, f32[2,384,128]{2,1,0:T(8,128)S(1)}, u32[]{:S(2)}, u32[]{:S(2)}) collective-permute-start(f32[2,384,128]{2,1,0:T(8,128)S(1)} %bitcast.5), channel_id=1, source_target_pairs={{0,64},{64,0},{1,65},{65,1},{2,66},{66,2},{3,67},{67,3},{4,68},{68... | collective-permute-start | bytes 1179656 | tf_op jit(solution)/shard_map/share_core/ppermute | solution.py:379

commit v10 on v9

--- a/solution.py
+++ b/solution.py
@@ -218,9 +218,7 @@
     return jnp.dot(mode, jnp.concatenate(parts, axis=0), preferred_element_type=jnp.float32).T
 
 
-def sent_kernel(
-    weighted_hbm, snap, edges, rot, send, rotation_t, weighted_keep, weighted, sems
-):
+def sent_kernel(weighted_hbm, snap, edges, rot, send, rotation_t, weighted, sems):
     half, _, width = weighted.shape
     kept = lax.axis_index("core") * half
     sent = half - kept
@@ -228,9 +226,6 @@
         pltpu.make_async_copy(weighted_hbm.at[sent + place], weighted.at[place], sems.at[place])
         for place in range(half)
     ]
-    copies.append(
-        pltpu.make_async_copy(weighted_hbm.at[pl.ds(kept, half)], weighted_keep, sems.at[half])
-    )
     for copy in copies:
         copy.start()
     tiles, padded, modes = rot.shape
@@ -253,7 +248,6 @@
     for place in range(half):
         copies[place].wait()
         send[place] = totals_of(mode[place], weighted.at[place], edges.at[sent + place])
-    copies[half].wait()
 
 
 def project_sent(weighted, snapshots, edges, rotation):
@@ -265,38 +259,49 @@
         out_shape=(
             jax.ShapeDtypeStruct((half, width, modes), jnp.float32),
             jax.ShapeDtypeStruct((modes, width), jnp.bfloat16),
-            jax.ShapeDtypeStruct((half, cells, width), jnp.bfloat16),
         ),
         in_specs=[HBM, VMEM, VMEM, VMEM],
-        out_specs=(VMEM, VMEM, VMEM),
+        out_specs=(VMEM, VMEM),
         scratch_shapes=[
             pltpu.VMEM((half, cells, width), jnp.bfloat16),
-            pltpu.SemaphoreType.DMA((half + 1,)),
+            pltpu.SemaphoreType.DMA((half,)),
         ],
         compiler_params=PARAMS,
         cost_estimate=pl.CostEstimate(flops=400_000_000, bytes_accessed=3_000_000, transcendentals=0),
     )(in_hbm(weighted), snapshots, edges, rotation)
 
 
-def kept_kernel(snap, weighted, edges, rotation_t, keep):
+def kept_kernel(weighted_hbm, snap, edges, rotation_t, keep, weighted, sems):
     half = weighted.shape[0]
     kept = lax.axis_index("core") * half
+    copies = [
+        pltpu.make_async_copy(weighted_hbm.at[kept + place], weighted.at[place], sems.at[place])
+        for place in range(half)
+    ]
+    for copy in copies:
+        copy.start()
+    mode = [modes_of(rotation_t[...], snap[kept + place]) for place in range(half)]
     for place in range(half):
-        mode = modes_of(rotation_t[...], snap[kept + place])
-        keep[place] = totals_of(mode, weighted.at[place], edges.at[kept + place])
-
-
-def project_kept(snapshots, weighted, edges, rotation_t):
-    half, _, width = weighted.shape
+        copies[place].wait()
+        keep[place] = totals_of(mode[place], weighted.at[place], edges.at[kept + place])
+
+
+def project_kept(weighted, snapshots, edges, rotation_t):
+    components, cells, width = snapshots.shape
+    half = components // 2
     modes = rotation_t.shape[0]
     return pl.pallas_call(
         kept_kernel,
         out_shape=jax.ShapeDtypeStruct((half, width, modes), jnp.float32),
-        in_specs=[VMEM] * 4,
+        in_specs=[HBM, VMEM, VMEM, VMEM],
         out_specs=VMEM,
+        scratch_shapes=[
+            pltpu.VMEM((half, cells, width), jnp.bfloat16),
+            pltpu.SemaphoreType.DMA((half,)),
+        ],
         compiler_params=PARAMS,
         cost_estimate=pl.CostEstimate(flops=400_000_000, bytes_accessed=3_000_000, transcendentals=0),
-    )(snapshots, weighted, edges, rotation_t)
+    )(in_hbm(weighted), snapshots, edges, rotation_t)
 
 
 def place_own_kernel(mine, out, sem):
@@ -361,9 +366,9 @@
         weighted, edge_scale, begin, end = weigh(snapshots, density, sound_speed, offsets)
         edges = weigh_edges(begin, end, edge_scale, outer, inner)
     with jax.named_scope("projections"):
-        send, rotation_t, weighted_keep = project_sent(weighted, snapshots, edges, full_rotation)
+        send, rotation_t = project_sent(weighted, snapshots, edges, full_rotation)
         received = lax.ppermute(send, "core", swap)
-        keep = project_kept(snapshots, weighted_keep, edges, rotation_t)
+        keep = project_kept(weighted, snapshots, edges, rotation_t)
         mine = keep + received
     modes = mine.shape[2]
     members = lax.axis_size(PLANE_AXES)

time: 76.9 us -> 77.9 us (1.013)
  Pallas kernels: 9.85 us -> 11.2 us
    pallas_call x1, Pallas kernels: 1.04 us -> 2.38 us  [project_kept(): pl.pallas_call(kept_kernel, out_shape=jax.ShapeDtypeStruct((half, width,...]
  transfers between devices with their start and end apart: 5 -> 5, of which waited for: 3 -> 2; matrix products, arithmetic and copies ran while one was open for 0% -> 0% of each run, Pallas kernels for 6% -> 8%
where the time goes in v10:
time: 77.9 us; the launch traced here: 77.6 us
  blocking collectives  35.7 us (46%)
  starting transfers between devices  29.2 us (37%)
  Pallas kernels  11.2 us (14%)
  waiting for transfers between devices  1.25 us (2%)
    all_to_all x2, blocking collectives, spread(): lax.all_to_all(jnp.broadcast_to(block[None], (count,) + block.shape), axe...  24.1 us
    all_to_all x1, starting transfers between devices, on_device(): full_rotation = lax.all_to_all(rows, SPREAD_AXES, 0, 0)  15.1 us
    all_to_all x1, blocking collectives, on_device(): piece = jnp.sum(lax.all_to_all(pieces, PLANE_AXES, 0, 0), axis=0)  11.6 us
    ppermute x1, starting transfers between devices, on_device(): outer = lax.ppermute(outer, CELL_AXES, across)  8.25 us
    ppermute x1, starting transfers between devices, on_device(): other = lax.ppermute(mine, 'core', swap)  4.2 us
    pallas_call x1, Pallas kernels, project_sent(): pl.pallas_call(sent_kernel, out_shape=(jax.ShapeDtypeStruct((half, width,...  2.77 us
    pallas_call x1, Pallas kernels, weigh(): pl.pallas_call(weighting_kernel, out_shape=(pltpu.HBM(snapshots.shape, jn...  2.72 us
    pallas_call x1, Pallas kernels, project_kept(): pl.pallas_call(kept_kernel, out_shape=jax.ShapeDtypeStruct((half, width,...  2.38 us
  transfers between devices with their start and end apart: 5, of which 2 were waited for; matrix products, arithmetic and copies ran while one was open for 0% of the time, Pallas kernels for 8%

profile of v10, /device:TPU:1, one launch (start us, length us, event | category | flops | bytes accessed | tf_op | source)
XLA Modules:
  0.0 77.6 jit_solution(13267210689913144058)
XLA Ops:
  0.0 0.0 copy-start
  0.0 0.0 copy-start.3
  0.0 0.0 copy-start.2
  0.0 0.0 copy-start.1
  0.0 1.5 %start.1 = (bf16[2,32,384]{2,1,0:T(8,128)(2,1)S(1)}, bf16[2,32,384]{2,1,0:T(8,128)(2,1)S(1)}, bf16[64,8,128]{2,1,0:T(8,128)(2,1)}) custom-call(bf16[4,960,384]{2,1,0:T(8,128)(2,1)} %snap.7, bf16[6,128]{1,0:T(8,128)(2,1)} %rot_hbm.1), custom_call_target="tpu_custom_call" | custom-call | bytes 100000000 | tf_op jit(solution)/shard_map/start/pallas_call | solution.py:63
  1.6 15.1 %all-to-all-start = ((bf16[64,8,128]{2,1,0:T(8,128)(2,1)}), bf16[64,8,128]{2,1,0:T(8,128)(2,1)S(1)}, u32[]{:S(2)}, u32[]{:S(2)}) async-start(bf16[64,8,128]{2,1,0:T(8,128)(2,1)} %get-tuple-element.20), calls=%async_computation | async-start | bytes 262144 | tf_op jit(solution)/shard_map/rotation_rows/all_to_all | solution.py:364
  16.7 8.3 %collective-permute-start = (bf16[2,32,384]{2,1,0:T(8,128)(2,1)S(1)}, bf16[2,32,384]{2,1,0:T(8,128)(2,1)S(1)}, u32[]{:S(2)}, u32[]{:S(2)}) collective-permute-start(bf16[2,32,384]{2,1,0:T(8,128)(2,1)S(1)} %get-tuple-element.18), channel_id=1, source_target_pairs={{0,255},{1,2},{2,1},{3,4},{4,3},{5,6},{6,5},{7,8},{8,7},{9,10},{10... | collective-permute-start | bytes 147464 | tf_op jit(solution)/shard_map/halo/ppermute | solution.py:361
  24.9 0.0 collective-permute-start.1
  24.9 0.0 copy-done
  24.9 0.0 copy-done.3
  24.9 0.0 copy-done.2
  25.0 0.0 copy-done.1
  25.0 2.7 %weighting.2 = (bf16[4,960,384]{2,1,0:T(8,128)(2,1)}, f32[64,8]{1,0:T(8,128)S(1)}, bf16[4,64,384]{2,1,0:T(8,128)(2,1)S(1)}, bf16[4,64,384]{2,1,0:T(8,128)(2,1)S(1)}) custom-call(bf16[4,960,384]{2,1,0:T(8,128)(2,1)S(1)} %copy-done, f32[1,960]{1,0:T(1,128)S(1)} %bitcast.7, f32[1,960]{1,0:T(1,128)S(1)} %bitcast.8, s32[1,960]{1,0:T(1,128)S(1)} %bitcast.9), custom_call_target="tpu_custom_call" | custom-call | flops 1000000000 | bytes 6000000 | tf_op jit(solution)/shard_map/weighting/pallas_call | solution.py:146
  27.7 0.7 collective-permute-done.outer
  28.4 0.0 collective-permute-done.1.inner
  28.4 0.3 weighting.3.edges
  28.6 0.0 all-to-all-done.rot
  28.6 2.8 %projections.2 = (f32[2,384,128]{2,1,0:T(8,128)S(1)}, bf16[128,384]{1,0:T(8,128)(2,1)S(1)}) custom-call(bf16[4,960,384]{2,1,0:T(8,128)(2,1)} %get-tuple-element.14.weighted_hbm, bf16[4,960,384]{2,1,0:T(8,128)(2,1)S(1)} %copy-done, bf16[4,64,384]{2,1,0:T(8,128)(2,1)S(1)} %weighting.3.edges, bf16[64,8,128]{2,1,0:T(8,128)(2,1)S(1)} %all-to-all-done.rot), custom_call_target="tpu_custom_call" | custom-call | flops 400000000 | bytes 3000000 | tf_op jit(solution)/shard_map/projections/pallas_call | solution.py:257
  31.4 1.7 %collective-permute-start.2 = (f32[2,384,128]{2,1,0:T(8,128)S(1)}, f32[2,384,128]{2,1,0:T(8,128)S(1)}, u32[]{:S(2)}, u32[]{:S(2)}) collective-permute-start(f32[2,384,128]{2,1,0:T(8,128)S(1)} %get-tuple-element.22), channel_id=1, source_target_pairs={{0,64},{64,0},{1,65},{65,1},{2,66},{66,2},{3,67},{67,3},{4,68},{68... | collective-permute-start | bytes 1179656 | tf_op jit(solution)/shard_map/projections/ppermute | solution.py:370
  33.1 2.4 %projections.3 = f32[2,384,128]{2,1,0:T(8,128)S(1)} custom-call(bf16[4,960,384]{2,1,0:T(8,128)(2,1)} %get-tuple-element.14.weighted_hbm, bf16[4,960,384]{2,1,0:T(8,128)(2,1)S(1)} %copy-done, bf16[4,64,384]{2,1,0:T(8,128)(2,1)S(1)} %weighting.3.edges, bf16[128,384]{1,0:T(8,128)(2,1)S(1)} %get-tuple-element.21.rotation_t), custom_call_target="tpu_custom_call" | custom-call | flops 400000000 | bytes 3000000 | tf_op jit(solution)/shard_map/projections/pallas_call | solution.py:293
  35.5 0.0 collective-permute-done.2
  35.5 11.6 %all_to_all.20 = f32[16,48,128]{2,1,0:T(8,128)S(1)} all-to-all(f32[16,48,128]{2,1,0:T(8,128)S(1)} %bitcast.10), channel_id=1, replica_groups=mesh['x_lo'=2,'core'=2,'x_hi'=2,'z'=8,'y'=4] {'y','x_lo','x_hi'}, dimensions={0} | all-to-all | bytes 786432 | tf_op jit(solution)/shard_map/sum_plane/all_to_all | solution.py:377
  47.2 12.5 %all_to_all.21 = f32[8,48,128]{2,1,0:T(8,128)S(1)} all-to-all(f32[8,48,128]{2,1,0:T(8,128)S(1)} %broadcast_in_dim.4), channel_id=1, replica_groups=mesh['x_lo'=2,'core'=2,'x_hi'=2,'z'=8,'y'=4] {'z'}, dimensions={0} | all-to-all | bytes 393216 | tf_op jit(solution)/shard_map/sum_z/all_to_all | solution.py:349
  59.8 11.6 %all_to_all.22 = f32[16,48,128]{2,1,0:T(8,128)S(1)} all-to-all(f32[16,48,128]{2,1,0:T(8,128)S(1)} %broadcast_in_dim.5), channel_id=1, replica_groups=mesh['x_lo'=2,'core'=2,'x_hi'=2,'z'=8,'y'=4] {'y','x_lo','x_hi'}, dimensions={0} | all-to-all | bytes 786432 | tf_op jit(solution)/shard_map/share_plane/all_to_all | solution.py:349
  71.3 4.2 %collective-permute-start.3 = (f32[2,384,128]{2,1,0:T(8,128)S(1)}, f32[2,384,128]{2,1,0:T(8,128)S(1)}, u32[]{:S(2)}, u32[]{:S(2)}) collective-permute-start(f32[2,384,128]{2,1,0:T(8,128)S(1)} %bitcast.5), channel_id=1, source_target_pairs={{0,64},{64,0},{1,65},{65,1},{2,66},{66,2},{3,67},{67,3},{4,68},{68... | collective-permute-start | bytes 1179656 | tf_op jit(solution)/shard_map/share_core/ppermute | solution.py:384
  75.5 0.8 share_core.2.begun
  76.3 0.6 collective-permute-done.3.other
  76.9 0.8 share_core.3
  (6 shorter events, 0.1 us)
Async XLA Ops:
  0.0 24.9 %copy-start = (bf16[4,960,384]{2,1,0:T(8,128)(2,1)S(1)}, bf16[4,960,384]{2,1,0:T(8,128)(2,1)}, u32[]{:S(2)}) copy-start(bf16[4,960,384]{2,1,0:T(8,128)(2,1)} %snap.7) | copy-start | bytes 8847364
  0.0 24.9 %copy-start.3 = (s32[960]{0:T(1024)S(1)}, s32[960]{0:T(1024)}, u32[]{:S(2)}) copy-start(s32[960]{0:T(1024)} %param.8) | copy-start | bytes 11524
  0.0 24.9 %copy-start.2 = (f32[960]{0:T(1024)S(1)}, f32[960]{0:T(1024)}, u32[]{:S(2)}) copy-start(f32[960]{0:T(1024)} %param.7) | copy-start | bytes 11524
  0.0 25.0 %copy-start.1 = (f32[960]{0:T(1024)S(1)}, f32[960]{0:T(1024)}, u32[]{:S(2)}) copy-start(f32[960]{0:T(1024)} %param.6) | copy-start | bytes 11524
  1.6 27.1 %all-to-all-start = ((bf16[64,8,128]{2,1,0:T(8,128)(2,1)}), bf16[64,8,128]{2,1,0:T(8,128)(2,1)S(1)}, u32[]{:S(2)}, u32[]{:S(2)}) async-start(bf16[64,8,128]{2,1,0:T(8,128)(2,1)} %get-tuple-element.20), calls=%async_computation | async-start | bytes 262144 | tf_op jit(solution)/shard_map/rotation_rows/all_to_all | solution.py:364
  16.7 11.7 %collective-permute-start = (bf16[2,32,384]{2,1,0:T(8,128)(2,1)S(1)}, bf16[2,32,384]{2,1,0:T(8,128)(2,1)S(1)}, u32[]{:S(2)}, u32[]{:S(2)}) collective-permute-start(bf16[2,32,384]{2,1,0:T(8,128)(2,1)S(1)} %get-tuple-element.18), channel_id=1, source_target_pairs={{0,255},{1,2},{2,1},{3,4},{4,3},{5,6},{6,5},{7,8},{8,7},{9,10},{10... | collective-permute-start | bytes 147464 | tf_op jit(solution)/shard_map/halo/ppermute | solution.py:361
  24.9 3.4 %collective-permute-start.1 = (bf16[2,32,384]{2,1,0:T(8,128)(2,1)S(1)}, bf16[2,32,384]{2,1,0:T(8,128)(2,1)S(1)}, u32[]{:S(2)}, u32[]{:S(2)}) collective-permute-start(bf16[2,32,384]{2,1,0:T(8,128)(2,1)S(1)} %get-tuple-element.19), channel_id=1, source_target_pairs={{0,1},{1,0},{2,3},{3,2},{4,5},{5,4},{6,7},{7,6},{8,9},{9,8},{10,11... | collective-permute-start | bytes 147464 | tf_op jit(solution)/shard_map/halo/ppermute | solution.py:362
  31.4 4.1 %collective-permute-start.2 = (f32[2,384,128]{2,1,0:T(8,128)S(1)}, f32[2,384,128]{2,1,0:T(8,128)S(1)}, u32[]{:S(2)}, u32[]{:S(2)}) collective-permute-start(f32[2,384,128]{2,1,0:T(8,128)S(1)} %get-tuple-element.22), channel_id=1, source_target_pairs={{0,64},{64,0},{1,65},{65,1},{2,66},{66,2},{3,67},{67,3},{4,68},{68... | collective-permute-start | bytes 1179656 | tf_op jit(solution)/shard_map/projections/ppermute | solution.py:370
  71.3 5.6 %collective-permute-start.3 = (f32[2,384,128]{2,1,0:T(8,128)S(1)}, f32[2,384,128]{2,1,0:T(8,128)S(1)}, u32[]{:S(2)}, u32[]{:S(2)}) collective-permute-start(f32[2,384,128]{2,1,0:T(8,128)S(1)} %bitcast.5), channel_id=1, source_target_pairs={{0,64},{64,0},{1,65},{65,1},{2,66},{66,2},{3,67},{67,3},{4,68},{68... | collective-permute-start | bytes 1179656 | tf_op jit(solution)/shard_map/share_core/ppermute | solution.py:384

commit v11 on v9

--- a/solution.py
+++ b/solution.py
@@ -11,11 +11,12 @@
 COMPONENTS = 4
 BLOCK = 192
 PADDED = 8
+ROWS = 6
 WEIGHT_FLOPS = 1_000_000_000
 EDGE_FLOPS = 1_000_000_000
 START_BYTES = 100_000_000
 TILE_AXES = ("x_hi", "z", "y")
-SPREAD_AXES = ("z", "y", "x_hi")
+SPREAD_AXES = ("z", "y")
 PLANE_AXES = ("y", "x_lo", "x_hi")
 CELL_AXES = ("x_lo", "core", "x_hi", "z", "y")
 VMEM = pl.BlockSpec(memory_space=pltpu.VMEM)
@@ -103,10 +104,25 @@
     return values
 
 
+def compact_of(rot):
+    pieces, padded, modes = rot.shape
+    shape = (pieces * ROWS, pieces * padded)
+    target = lax.broadcasted_iota(jnp.int32, shape, 0)
+    source = lax.broadcasted_iota(jnp.int32, shape, 1)
+    within = source & (padded - 1)
+    chosen = jnp.logical_and(target == (source - within) // padded * ROWS + within, within < ROWS)
+    return jnp.dot(
+        chosen.astype(jnp.float32).astype(jnp.bfloat16),
+        rot[...].reshape(pieces * padded, modes),
+        preferred_element_type=jnp.float32,
+    )
+
+
 def weighting_kernel(
-    snap, dens, speed, offs, weighted_hbm, edge_scale, begin_rim, end_rim, weighted, rows_ref, sems
+    snap, dens, speed, offs, rot, weighted, edge_scale, begin_rim, end_rim, own_rows, rows_ref
 ):
     cells = snap.shape[1]
+    own_rows[...] = compact_of(rot)
     begin_rim[...] = snap[:, 0 : 2 * HALO]
     end_rim[...] = snap[:, cells - 2 * HALO :]
     density = dens[...]
@@ -119,7 +135,6 @@
     columns = rows_ref[...].T
     edge_scale[0:HALO] = columns[0:HALO]
     edge_scale[HALO:] = columns[cells - HALO : cells]
-    copies = []
     for begin in range(0, cells, BLOCK):
         stop = begin + BLOCK
         low, high = max(begin - HALO, 0), min(stop + HALO, cells)
@@ -131,33 +146,23 @@
         )
         for component in range(COMPONENTS):
             weighted[component, begin:stop] = values[component]
-        rows = pl.ds(begin, BLOCK)
-        copies.append(
-            pltpu.make_async_copy(weighted.at[:, rows], weighted_hbm.at[:, rows], sems.at[len(copies)])
-        )
-        copies[-1].start()
-    for copy in copies:
-        copy.wait()
-
-
-def weigh(snapshots, density, sound_speed, offsets):
+
+
+def weigh(snapshots, density, sound_speed, offsets, rotation):
     components, cells, width = snapshots.shape
     rim = jax.ShapeDtypeStruct((components, 2 * HALO, width), jnp.bfloat16)
     return pl.pallas_call(
         weighting_kernel,
         out_shape=(
-            pltpu.HBM(snapshots.shape, jnp.bfloat16),
+            jax.ShapeDtypeStruct(snapshots.shape, jnp.bfloat16),
             jax.ShapeDtypeStruct((2 * HALO, 8), jnp.float32),
             rim,
             rim,
+            jax.ShapeDtypeStruct((rotation.shape[0] * ROWS, rotation.shape[2]), jnp.float32),
         ),
-        in_specs=[VMEM] * 4,
-        out_specs=(HBM, VMEM, VMEM, VMEM),
-        scratch_shapes=[
-            pltpu.VMEM(snapshots.shape, jnp.bfloat16),
-            pltpu.VMEM((8, 1024), jnp.float32),
-            pltpu.SemaphoreType.DMA((cells // BLOCK,)),
-        ],
+        in_specs=[VMEM] * 5,
+        out_specs=(VMEM,) * 5,
+        scratch_shapes=[pltpu.VMEM((8, 1024), jnp.float32)],
         compiler_params=PARAMS,
         cost_estimate=pl.CostEstimate(flops=WEIGHT_FLOPS, bytes_accessed=6_000_000, transcendentals=0),
     )(
@@ -165,6 +170,7 @@
         density.reshape(1, cells),
         sound_speed.reshape(1, cells),
         offsets.reshape(1, cells),
+        rotation,
     )
 
 
@@ -218,80 +224,50 @@
     return jnp.dot(mode, jnp.concatenate(parts, axis=0), preferred_element_type=jnp.float32).T
 
 
-def sent_kernel(
-    weighted_hbm, snap, edges, rot, send, rotation_t, weighted_keep, weighted, sems
-):
-    half, _, width = weighted.shape
-    kept = lax.axis_index("core") * half
-    sent = half - kept
-    copies = [
-        pltpu.make_async_copy(weighted_hbm.at[sent + place], weighted.at[place], sems.at[place])
-        for place in range(half)
-    ]
-    copies.append(
-        pltpu.make_async_copy(weighted_hbm.at[pl.ds(kept, half)], weighted_keep, sems.at[half])
-    )
-    for copy in copies:
-        copy.start()
-    tiles, padded, modes = rot.shape
-    rows = width // tiles
-    shape = (width, tiles * padded)
-    target = lax.broadcasted_iota(jnp.int32, shape, 0)
-    source = lax.broadcasted_iota(jnp.int32, shape, 1)
-    within = source & (padded - 1)
-    slot = (source - within) // padded
-    tile = (slot & 1) * (tiles // 2) + (slot >> 1)
-    chosen = jnp.logical_and(target == tile * rows + within, within < rows)
-    compact = jnp.dot(
-        chosen.astype(jnp.float32).astype(jnp.bfloat16),
-        rot[...].reshape(tiles * padded, modes),
-        preferred_element_type=jnp.float32,
-    )
-    turned = compact.T.astype(jnp.bfloat16)
+def sent_kernel(snap, weighted, edges, own_rows, rot, send, rotation_t):
+    half = send.shape[0]
+    sent = (1 - lax.axis_index("core")) * half
+    own = own_rows[...]
+    other = compact_of(rot)
+    first = lax.broadcast_in_dim(lax.axis_index("x_hi"), own.shape, ()) == 0
+    rows = jnp.concatenate([jnp.where(first, own, other), jnp.where(first, other, own)], axis=0)
+    turned = rows.T.astype(jnp.bfloat16)
     rotation_t[...] = turned
-    mode = [modes_of(turned, snap[sent + place]) for place in range(half)]
     for place in range(half):
-        copies[place].wait()
-        send[place] = totals_of(mode[place], weighted.at[place], edges.at[sent + place])
-    copies[half].wait()
-
-
-def project_sent(weighted, snapshots, edges, rotation):
-    components, cells, width = snapshots.shape
-    half = components // 2
+        mode = modes_of(turned, snap[sent + place])
+        send[place] = totals_of(mode, weighted.at[sent + place], edges.at[sent + place])
+
+
+def project_sent(snapshots, weighted, edges, own_rows, rotation):
+    components, _, width = snapshots.shape
     modes = rotation.shape[2]
     return pl.pallas_call(
         sent_kernel,
         out_shape=(
-            jax.ShapeDtypeStruct((half, width, modes), jnp.float32),
+            jax.ShapeDtypeStruct((components // 2, width, modes), jnp.float32),
             jax.ShapeDtypeStruct((modes, width), jnp.bfloat16),
-            jax.ShapeDtypeStruct((half, cells, width), jnp.bfloat16),
         ),
-        in_specs=[HBM, VMEM, VMEM, VMEM],
-        out_specs=(VMEM, VMEM, VMEM),
-        scratch_shapes=[
-            pltpu.VMEM((half, cells, width), jnp.bfloat16),
-            pltpu.SemaphoreType.DMA((half + 1,)),
-        ],
+        in_specs=[VMEM] * 5,
+        out_specs=(VMEM, VMEM),
         compiler_params=PARAMS,
         cost_estimate=pl.CostEstimate(flops=400_000_000, bytes_accessed=3_000_000, transcendentals=0),
-    )(in_hbm(weighted), snapshots, edges, rotation)
+    )(snapshots, weighted, edges, own_rows, rotation)
 
 
 def kept_kernel(snap, weighted, edges, rotation_t, keep):
-    half = weighted.shape[0]
+    half = keep.shape[0]
     kept = lax.axis_index("core") * half
     for place in range(half):
         mode = modes_of(rotation_t[...], snap[kept + place])
-        keep[place] = totals_of(mode, weighted.at[place], edges.at[kept + place])
+        keep[place] = totals_of(mode, weighted.at[kept + place], edges.at[kept + place])
 
 
 def project_kept(snapshots, weighted, edges, rotation_t):
-    half, _, width = weighted.shape
+    components, _, width = snapshots.shape
     modes = rotation_t.shape[0]
     return pl.pallas_call(
         kept_kernel,
-        out_shape=jax.ShapeDtypeStruct((half, width, modes), jnp.float32),
+        out_shape=jax.ShapeDtypeStruct((components // 2, width, modes), jnp.float32),
         in_specs=[VMEM] * 4,
         out_specs=VMEM,
         compiler_params=PARAMS,
@@ -351,19 +327,22 @@
     across = [(i, (i + 1 if i % 2 else i - 1) % count) for i in range(count)]
     swap = [(0, 1), (1, 0)]
     with jax.named_scope("start"):
-        inner, outer, rows = start(in_hbm(snapshots), rotation, lax.axis_size(TILE_AXES))
+        inner, outer, rows = start(in_hbm(snapshots), rotation, lax.axis_size(SPREAD_AXES))
     with jax.named_scope("halo"):
         outer = lax.ppermute(outer, CELL_AXES, across)
         inner = lax.ppermute(inner, CELL_AXES, inside)
     with jax.named_scope("rotation_rows"):
-        full_rotation = lax.all_to_all(rows, SPREAD_AXES, 0, 0)
+        own_pieces = lax.all_to_all(rows, SPREAD_AXES, 0, 0)
+        other_pieces = lax.ppermute(own_pieces, "x_hi", swap)
     with jax.named_scope("weighting"):
-        weighted, edge_scale, begin, end = weigh(snapshots, density, sound_speed, offsets)
+        weighted, edge_scale, begin, end, own_rows = weigh(
+            snapshots, density, sound_speed, offsets, own_pieces
+        )
         edges = weigh_edges(begin, end, edge_scale, outer, inner)
     with jax.named_scope("projections"):
-        send, rotation_t, weighted_keep = project_sent(weighted, snapshots, edges, full_rotation)
+        send, rotation_t = project_sent(snapshots, weighted, edges, own_rows, other_pieces)
         received = lax.ppermute(send, "core", swap)
-        keep = project_kept(snapshots, weighted_keep, edges, rotation_t)
+        keep = project_kept(snapshots, weighted, edges, rotation_t)
         mine = keep + received
     modes = mine.shape[2]
     members = lax.axis_size(PLANE_AXES)

time: 76.9 us -> 75.3 us (0.979)
  Pallas kernels: 9.85 us -> 7.42 us
    all_to_all x1, starting transfers between devices: 15.1 us -> 12 us  [on_device(): own_pieces = lax.all_to_all(rows, SPREAD_AXES, 0, 0)]
    ppermute x0 -> x1, starting transfers between devices: none -> 2.74 us  [on_device(): other_pieces = lax.ppermute(own_pieces, 'x_hi', swap)]
    pallas_call x3, Pallas kernels: 6.54 us -> 4.13 us  [the longest x1 1.86 us: weigh(): pl.pallas_call(weighting_kernel, out_shape=(jax.ShapeDtypeStruct(snapshot...]
    all_to_all x1, blocking collectives: 11.3 us -> 12.9 us  [on_device(): piece = jnp.sum(lax.all_to_all(pieces, PLANE_AXES, 0, 0), axis=0)]
    ppermute x1, starting transfers between devices: 1.66 us -> 3.05 us  [on_device(): received = lax.ppermute(send, 'core', swap)]
    all_to_all x2, blocking collectives: 24 us -> 22.7 us  [spread(): lax.all_to_all(jnp.broadcast_to(block[None], (count,) + block.shape), axe...]
  transfers between devices with their start and end apart: 5 -> 6, of which waited for: 3 -> 3; matrix products, arithmetic and copies ran while one was open for 0% -> 0% of each run, Pallas kernels for 6% -> 5%
where the time goes in v11:
time: 75.3 us; the launch traced here: 75.1 us
  blocking collectives  35.6 us (47%)
  starting transfers between devices  30.3 us (40%)
  Pallas kernels  7.42 us (10%)
  waiting for transfers between devices  1.43 us (2%)
    all_to_all x2, blocking collectives, spread(): lax.all_to_all(jnp.broadcast_to(block[None], (count,) + block.shape), axe...  22.7 us
    all_to_all x1, blocking collectives, on_device(): piece = jnp.sum(lax.all_to_all(pieces, PLANE_AXES, 0, 0), axis=0)  12.9 us
    all_to_all x1, starting transfers between devices, on_device(): own_pieces = lax.all_to_all(rows, SPREAD_AXES, 0, 0)  12 us
    ppermute x1, starting transfers between devices, on_device(): outer = lax.ppermute(outer, CELL_AXES, across)  8.31 us
    ppermute x1, starting transfers between devices, on_device(): other = lax.ppermute(mine, 'core', swap)  4.2 us
    ppermute x1, starting transfers between devices, on_device(): received = lax.ppermute(send, 'core', swap)  3.05 us
    ppermute x1, starting transfers between devices, on_device(): other_pieces = lax.ppermute(own_pieces, 'x_hi', swap)  2.74 us
    pallas_call x1, Pallas kernels, weigh(): pl.pallas_call(weighting_kernel, out_shape=(jax.ShapeDtypeStruct(snapshot...  1.86 us
  transfers between devices with their start and end apart: 6, of which 3 were waited for; matrix products, arithmetic and copies ran while one was open for 0% of the time, Pallas kernels for 5%

profile of v11, /device:TPU:1, one launch (start us, length us, event | category | flops | bytes accessed | tf_op | source)
XLA Modules:
  0.0 75.1 jit_solution(2159863735088678726)
XLA Ops:
  0.0 0.0 copy-start
  0.0 0.0 copy-start.3
  0.0 0.0 copy-start.2
  0.0 0.0 copy-start.1
  0.0 1.5 %start.1 = (bf16[2,32,384]{2,1,0:T(8,128)(2,1)S(1)}, bf16[2,32,384]{2,1,0:T(8,128)(2,1)S(1)}, bf16[32,8,128]{2,1,0:T(8,128)(2,1)}) custom-call(bf16[4,960,384]{2,1,0:T(8,128)(2,1)} %snap.7, bf16[6,128]{1,0:T(8,128)(2,1)} %rot_hbm.1), custom_call_target="tpu_custom_call" | custom-call | bytes 100000000 | tf_op jit(solution)/shard_map/start/pallas_call | solution.py:64
  1.5 12.0 %all-to-all-start = ((bf16[32,8,128]{2,1,0:T(8,128)(2,1)}), bf16[32,8,128]{2,1,0:T(8,128)(2,1)S(1)}, u32[]{:S(2)}, u32[]{:S(2)}) async-start(bf16[32,8,128]{2,1,0:T(8,128)(2,1)} %get-tuple-element.15), calls=%async_computation | async-start | bytes 131072 | tf_op jit(solution)/shard_map/rotation_rows/all_to_all | solution.py:335
  13.6 8.3 %collective-permute-start = (bf16[2,32,384]{2,1,0:T(8,128)(2,1)S(1)}, bf16[2,32,384]{2,1,0:T(8,128)(2,1)S(1)}, u32[]{:S(2)}, u32[]{:S(2)}) collective-permute-start(bf16[2,32,384]{2,1,0:T(8,128)(2,1)S(1)} %get-tuple-element.20), channel_id=1, source_target_pairs={{0,255},{1,2},{2,1},{3,4},{4,3},{5,6},{6,5},{7,8},{8,7},{9,10},{10... | collective-permute-start | bytes 147464 | tf_op jit(solution)/shard_map/halo/ppermute | solution.py:332
  21.9 0.0 collective-permute-start.1
  21.9 0.5 all-to-all-done.rot
  22.4 2.7 %collective-permute-start.2 = (bf16[32,8,128]{2,1,0:T(8,128)(2,1)S(1)}, bf16[32,8,128]{2,1,0:T(8,128)(2,1)S(1)}, u32[]{:S(2)}, u32[]{:S(2)}) collective-permute-start(bf16[32,8,128]{2,1,0:T(8,128)(2,1)S(1)} %all-to-all-done.rot), channel_id=1, source_target_pairs={{0,32},{32,0},{1,33},{33,1},{2,34},{34,2},{3,35},{35,3},{4,36},{36... | collective-permute-start | bytes 196616 | tf_op jit(solution)/shard_map/rotation_rows/ppermute | solution.py:336
  25.2 0.0 copy-done
  25.2 0.0 copy-done.3
  25.2 0.0 copy-done.2
  25.2 0.0 copy-done.1
  25.2 1.9 %weighting.2 = (bf16[4,960,384]{2,1,0:T(8,128)(2,1)S(1)}, f32[64,8]{1,0:T(8,128)S(1)}, bf16[4,64,384]{2,1,0:T(8,128)(2,1)S(1)}, bf16[4,64,384]{2,1,0:T(8,128)(2,1)S(1)}, f32[192,128]{1,0:T(8,128)S(1)}) custom-call(bf16[4,960,384]{2,1,0:T(8,128)(2,1)S(1)} %copy-done, f32[1,960]{1,0:T(1,128)S(1)} %bitcast.7, f32[1,960]{1,0:T(1,128)S(1)} %bitcast.8, ...), custom_call_target="tpu_custom_call" | custom-call | flops 1000000000 | bytes 6000000 | tf_op jit(solution)/shard_map/weighting/pallas_call | solution.py:154
  27.0 0.0 collective-permute-done.outer
  27.0 0.0 collective-permute-done.1.inner
  27.1 0.3 weighting.3.edges
  27.3 0.0 collective-permute-done.2.rot
  27.3 1.2 %projections.2 = (f32[2,384,128]{2,1,0:T(8,128)S(1)}, bf16[128,384]{1,0:T(8,128)(2,1)S(1)}) custom-call(bf16[4,960,384]{2,1,0:T(8,128)(2,1)S(1)} %copy-done, bf16[4,960,384]{2,1,0:T(8,128)(2,1)S(1)} %get-tuple-element.16.weighted, bf16[4,64,384]{2,1,0:T(8,128)(2,1)S(1)} %weighting.3.edges, f32[192,128]{1,0:T(8,128)S(1)} %get-tuple-element.22.own_rows, ...), custom_call_target="tpu_custom_call" | custom-call | flops 400000000 | bytes 3000000 | tf_op jit(solution)/shard_map/projections/pallas_call | solution.py:244
  28.6 3.0 %collective-permute-start.3 = (f32[2,384,128]{2,1,0:T(8,128)S(1)}, f32[2,384,128]{2,1,0:T(8,128)S(1)}, u32[]{:S(2)}, u32[]{:S(2)}) collective-permute-start(f32[2,384,128]{2,1,0:T(8,128)S(1)} %get-tuple-element.24), channel_id=1, source_target_pairs={{0,64},{64,0},{1,65},{65,1},{2,66},{66,2},{3,67},{67,3},{4,68},{68... | collective-permute-start | bytes 1179656 | tf_op jit(solution)/shard_map/projections/ppermute | solution.py:344
  31.6 1.0 %projections.3 = f32[2,384,128]{2,1,0:T(8,128)S(1)} custom-call(bf16[4,960,384]{2,1,0:T(8,128)(2,1)S(1)} %copy-done, bf16[4,960,384]{2,1,0:T(8,128)(2,1)S(1)} %get-tuple-element.16.weighted, bf16[4,64,384]{2,1,0:T(8,128)(2,1)S(1)} %weighting.3.edges, bf16[128,384]{1,0:T(8,128)(2,1)S(1)} %get-tuple-element.23.rotation_t), custom_call_target="tpu_custom_call" | custom-call | flops 400000000 | bytes 3000000 | tf_op jit(solution)/shard_map/projections/pallas_call | solution.py:268
  32.7 0.3 collective-permute-done.3
  33.0 12.9 %all_to_all.20 = f32[16,48,128]{2,1,0:T(8,128)S(1)} all-to-all(f32[16,48,128]{2,1,0:T(8,128)S(1)} %bitcast.10), channel_id=1, replica_groups=mesh['x_lo'=2,'core'=2,'x_hi'=2,'z'=8,'y'=4] {'y','x_lo','x_hi'}, dimensions={0} | all-to-all | bytes 786432 | tf_op jit(solution)/shard_map/sum_plane/all_to_all | solution.py:351
  46.0 11.0 %all_to_all.21 = f32[8,48,128]{2,1,0:T(8,128)S(1)} all-to-all(f32[8,48,128]{2,1,0:T(8,128)S(1)} %broadcast_in_dim.4), channel_id=1, replica_groups=mesh['x_lo'=2,'core'=2,'x_hi'=2,'z'=8,'y'=4] {'z'}, dimensions={0} | all-to-all | bytes 393216 | tf_op jit(solution)/shard_map/sum_z/all_to_all | solution.py:320
  57.1 11.7 %all_to_all.22 = f32[16,48,128]{2,1,0:T(8,128)S(1)} all-to-all(f32[16,48,128]{2,1,0:T(8,128)S(1)} %broadcast_in_dim.5), channel_id=1, replica_groups=mesh['x_lo'=2,'core'=2,'x_hi'=2,'z'=8,'y'=4] {'y','x_lo','x_hi'}, dimensions={0} | all-to-all | bytes 786432 | tf_op jit(solution)/shard_map/share_plane/all_to_all | solution.py:320
  68.8 4.2 %collective-permute-start.4 = (f32[2,384,128]{2,1,0:T(8,128)S(1)}, f32[2,384,128]{2,1,0:T(8,128)S(1)}, u32[]{:S(2)}, u32[]{:S(2)}) collective-permute-start(f32[2,384,128]{2,1,0:T(8,128)S(1)} %bitcast.5), channel_id=1, source_target_pairs={{0,64},{64,0},{1,65},{65,1},{2,66},{66,2},{3,67},{67,3},{4,68},{68... | collective-permute-start | bytes 1179656 | tf_op jit(solution)/shard_map/share_core/ppermute | solution.py:358
  73.0 0.8 %share_core.2.begun = f32[4,384,128]{2,1,0:T(8,128)} custom-call(f32[2,384,128]{2,1,0:T(8,128)S(1)} %bitcast.6), custom_call_target="tpu_custom_call" | custom-call | bytes 1000000 | tf_op jit(solution)/shard_map/share_core/pallas_call | solution.py:294
  73.8 0.6 collective-permute-done.4.other
  74.3 0.8 %share_core.3 = f32[4,384,128]{2,1,0:T(8,128)} custom-call(f32[4,384,128]{2,1,0:T(8,128)} %share_core.2.begun, f32[2,384,128]{2,1,0:T(8,128)S(1)} %collective-permute-done.4.other), custom_call_target="tpu_custom_call", output_to_operand_aliasing={{}: (0, {})} | custom-call | bytes 1000000 | tf_op jit(solution)/shard_map/share_core/pallas_call | solution.py:306
  (6 shorter events, 0.1 us)
Async XLA Ops:
  0.0 25.2 %copy-start = (bf16[4,960,384]{2,1,0:T(8,128)(2,1)S(1)}, bf16[4,960,384]{2,1,0:T(8,128)(2,1)}, u32[]{:S(2)}) copy-start(bf16[4,960,384]{2,1,0:T(8,128)(2,1)} %snap.7) | copy-start | bytes 8847364
  0.0 25.2 %copy-start.3 = (s32[960]{0:T(1024)S(1)}, s32[960]{0:T(1024)}, u32[]{:S(2)}) copy-start(s32[960]{0:T(1024)} %param.8) | copy-start | bytes 11524
  0.0 25.2 %copy-start.2 = (f32[960]{0:T(1024)S(1)}, f32[960]{0:T(1024)}, u32[]{:S(2)}) copy-start(f32[960]{0:T(1024)} %param.7) | copy-start | bytes 11524
  0.0 25.2 %copy-start.1 = (f32[960]{0:T(1024)S(1)}, f32[960]{0:T(1024)}, u32[]{:S(2)}) copy-start(f32[960]{0:T(1024)} %param.6) | copy-start | bytes 11524
  1.5 20.9 %all-to-all-start = ((bf16[32,8,128]{2,1,0:T(8,128)(2,1)}), bf16[32,8,128]{2,1,0:T(8,128)(2,1)S(1)}, u32[]{:S(2)}, u32[]{:S(2)}) async-start(bf16[32,8,128]{2,1,0:T(8,128)(2,1)} %get-tuple-element.15), calls=%async_computation | async-start | bytes 131072 | tf_op jit(solution)/shard_map/rotation_rows/all_to_all | solution.py:335
  13.6 13.5 %collective-permute-start = (bf16[2,32,384]{2,1,0:T(8,128)(2,1)S(1)}, bf16[2,32,384]{2,1,0:T(8,128)(2,1)S(1)}, u32[]{:S(2)}, u32[]{:S(2)}) collective-permute-start(bf16[2,32,384]{2,1,0:T(8,128)(2,1)S(1)} %get-tuple-element.20), channel_id=1, source_target_pairs={{0,255},{1,2},{2,1},{3,4},{4,3},{5,6},{6,5},{7,8},{8,7},{9,10},{10... | collective-permute-start | bytes 147464 | tf_op jit(solution)/shard_map/halo/ppermute | solution.py:332
  21.9 5.2 %collective-permute-start.1 = (bf16[2,32,384]{2,1,0:T(8,128)(2,1)S(1)}, bf16[2,32,384]{2,1,0:T(8,128)(2,1)S(1)}, u32[]{:S(2)}, u32[]{:S(2)}) collective-permute-start(bf16[2,32,384]{2,1,0:T(8,128)(2,1)S(1)} %get-tuple-element.21), channel_id=1, source_target_pairs={{0,1},{1,0},{2,3},{3,2},{4,5},{5,4},{6,7},{7,6},{8,9},{9,8},{10,11... | collective-permute-start | bytes 147464 | tf_op jit(solution)/shard_map/halo/ppermute | solution.py:333
  22.4 4.9 %collective-permute-start.2 = (bf16[32,8,128]{2,1,0:T(8,128)(2,1)S(1)}, bf16[32,8,128]{2,1,0:T(8,128)(2,1)S(1)}, u32[]{:S(2)}, u32[]{:S(2)}) collective-permute-start(bf16[32,8,128]{2,1,0:T(8,128)(2,1)S(1)} %all-to-all-done.rot), channel_id=1, source_target_pairs={{0,32},{32,0},{1,33},{33,1},{2,34},{34,2},{3,35},{35,3},{4,36},{36... | collective-permute-start | bytes 196616 | tf_op jit(solution)/shard_map/rotation_rows/ppermute | solution.py:336
  28.6 4.4 %collective-permute-start.3 = (f32[2,384,128]{2,1,0:T(8,128)S(1)}, f32[2,384,128]{2,1,0:T(8,128)S(1)}, u32[]{:S(2)}, u32[]{:S(2)}) collective-permute-start(f32[2,384,128]{2,1,0:T(8,128)S(1)} %get-tuple-element.24), channel_id=1, source_target_pairs={{0,64},{64,0},{1,65},{65,1},{2,66},{66,2},{3,67},{67,3},{4,68},{68... | collective-permute-start | bytes 1179656 | tf_op jit(solution)/shard_map/projections/ppermute | solution.py:344
  68.8 5.5 %collective-permute-start.4 = (f32[2,384,128]{2,1,0:T(8,128)S(1)}, f32[2,384,128]{2,1,0:T(8,128)S(1)}, u32[]{:S(2)}, u32[]{:S(2)}) collective-permute-start(f32[2,384,128]{2,1,0:T(8,128)S(1)} %bitcast.5), channel_id=1, source_target_pairs={{0,64},{64,0},{1,65},{65,1},{2,66},{66,2},{3,67},{67,3},{4,68},{68... | collective-permute-start | bytes 1179656 | tf_op jit(solution)/shard_map/share_core/ppermute | solution.py:358

commit v12 on v11

--- a/solution.py
+++ b/solution.py
@@ -333,7 +333,7 @@
         inner = lax.ppermute(inner, CELL_AXES, inside)
     with jax.named_scope("rotation_rows"):
         own_pieces = lax.all_to_all(rows, SPREAD_AXES, 0, 0)
-        other_pieces = lax.ppermute(own_pieces, "x_hi", swap)
+        other_pieces = lax.ppermute(own_pieces, ("x_lo", "x_hi"), [(i, 3 - i) for i in range(4)])
     with jax.named_scope("weighting"):
         weighted, edge_scale, begin, end, own_rows = weigh(
             snapshots, density, sound_speed, offsets, own_pieces

time: 75.3 us -> 74.8 us (level)
  no operation moved by 1% of the time
where the time goes in v12:
time: 74.8 us; the launch traced here: 74.5 us
  blocking collectives  35.4 us (47%)
  starting transfers between devices  30.1 us (40%)
  Pallas kernels  7.41 us (10%)
  waiting for transfers between devices  1.43 us (2%)
    all_to_all x2, blocking collectives, spread(): lax.all_to_all(jnp.broadcast_to(block[None], (count,) + block.shape), axe...  22.7 us
    all_to_all x1, blocking collectives, on_device(): piece = jnp.sum(lax.all_to_all(pieces, PLANE_AXES, 0, 0), axis=0)  12.6 us
    all_to_all x1, starting transfers between devices, on_device(): own_pieces = lax.all_to_all(rows, SPREAD_AXES, 0, 0)  12 us
    ppermute x1, starting transfers between devices, on_device(): outer = lax.ppermute(outer, CELL_AXES, across)  8.31 us
    ppermute x1, starting transfers between devices, on_device(): other = lax.ppermute(mine, 'core', swap)  4.2 us
    ppermute x1, starting transfers between devices, on_device(): received = lax.ppermute(send, 'core', swap)  3 us
    ppermute x1, starting transfers between devices, on_device(): lax.ppermute(own_pieces, ('x_lo', 'x_hi'), [(i, 3 - i) for i in range(4)])  2.5 us
    pallas_call x1, Pallas kernels, weigh(): pl.pallas_call(weighting_kernel, out_shape=(jax.ShapeDtypeStruct(snapshot...  1.85 us
  transfers between devices with their start and end apart: 6, of which 3 were waited for; matrix products, arithmetic and copies ran while one was open for 0% of the time, Pallas kernels for 5%

profile of v12, /device:TPU:1, one launch (start us, length us, event | category | flops | bytes accessed | tf_op | source)
XLA Modules:
  0.0 74.5 jit_solution(11190627875239123779)
XLA Ops:
  0.0 0.0 copy-start
  0.0 0.0 copy-start.3
  0.0 0.0 copy-start.2
  0.0 0.0 copy-start.1
  0.0 1.5 %start.1 = (bf16[2,32,384]{2,1,0:T(8,128)(2,1)S(1)}, bf16[2,32,384]{2,1,0:T(8,128)(2,1)S(1)}, bf16[32,8,128]{2,1,0:T(8,128)(2,1)}) custom-call(bf16[4,960,384]{2,1,0:T(8,128)(2,1)} %snap.7, bf16[6,128]{1,0:T(8,128)(2,1)} %rot_hbm.1), custom_call_target="tpu_custom_call" | custom-call | bytes 100000000 | tf_op jit(solution)/shard_map/start/pallas_call | solution.py:64
  1.5 12.0 %all-to-all-start = ((bf16[32,8,128]{2,1,0:T(8,128)(2,1)}), bf16[32,8,128]{2,1,0:T(8,128)(2,1)S(1)}, u32[]{:S(2)}, u32[]{:S(2)}) async-start(bf16[32,8,128]{2,1,0:T(8,128)(2,1)} %get-tuple-element.15), calls=%async_computation | async-start | bytes 131072 | tf_op jit(solution)/shard_map/rotation_rows/all_to_all | solution.py:335
  13.6 8.3 %collective-permute-start = (bf16[2,32,384]{2,1,0:T(8,128)(2,1)S(1)}, bf16[2,32,384]{2,1,0:T(8,128)(2,1)S(1)}, u32[]{:S(2)}, u32[]{:S(2)}) collective-permute-start(bf16[2,32,384]{2,1,0:T(8,128)(2,1)S(1)} %get-tuple-element.20), channel_id=1, source_target_pairs={{0,255},{1,2},{2,1},{3,4},{4,3},{5,6},{6,5},{7,8},{8,7},{9,10},{10... | collective-permute-start | bytes 147464 | tf_op jit(solution)/shard_map/halo/ppermute | solution.py:332
  21.9 0.0 collective-permute-start.1
  21.9 0.5 all-to-all-done.rot
  22.4 2.5 %collective-permute-start.2 = (bf16[32,8,128]{2,1,0:T(8,128)(2,1)S(1)}, bf16[32,8,128]{2,1,0:T(8,128)(2,1)S(1)}, u32[]{:S(2)}, u32[]{:S(2)}) collective-permute-start(bf16[32,8,128]{2,1,0:T(8,128)(2,1)S(1)} %all-to-all-done.rot), channel_id=1, source_target_pairs={{0,160},{32,128},{128,32},{160,0},{1,161},{33,129},{129,33},{161,1... | collective-permute-start | bytes 196616 | tf_op jit(solution)/shard_map/rotation_rows/ppermute | solution.py:336
  24.9 0.0 copy-done
  24.9 0.0 copy-done.3
  24.9 0.0 copy-done.2
  24.9 0.0 copy-done.1
  24.9 1.9 %weighting.2 = (bf16[4,960,384]{2,1,0:T(8,128)(2,1)S(1)}, f32[64,8]{1,0:T(8,128)S(1)}, bf16[4,64,384]{2,1,0:T(8,128)(2,1)S(1)}, bf16[4,64,384]{2,1,0:T(8,128)(2,1)S(1)}, f32[192,128]{1,0:T(8,128)S(1)}) custom-call(bf16[4,960,384]{2,1,0:T(8,128)(2,1)S(1)} %copy-done, f32[1,960]{1,0:T(1,128)S(1)} %bitcast.7, f32[1,960]{1,0:T(1,128)S(1)} %bitcast.8, ...), custom_call_target="tpu_custom_call" | custom-call | flops 1000000000 | bytes 6000000 | tf_op jit(solution)/shard_map/weighting/pallas_call | solution.py:154
  26.8 0.0 collective-permute-done.outer
  26.8 0.0 collective-permute-done.1.inner
  26.8 0.3 weighting.3.edges
  27.1 0.0 collective-permute-done.2.rot
  27.1 1.2 %projections.2 = (f32[2,384,128]{2,1,0:T(8,128)S(1)}, bf16[128,384]{1,0:T(8,128)(2,1)S(1)}) custom-call(bf16[4,960,384]{2,1,0:T(8,128)(2,1)S(1)} %copy-done, bf16[4,960,384]{2,1,0:T(8,128)(2,1)S(1)} %get-tuple-element.16.weighted, bf16[4,64,384]{2,1,0:T(8,128)(2,1)S(1)} %weighting.3.edges, f32[192,128]{1,0:T(8,128)S(1)} %get-tuple-element.22.own_rows, ...), custom_call_target="tpu_custom_call" | custom-call | flops 400000000 | bytes 3000000 | tf_op jit(solution)/shard_map/projections/pallas_call | solution.py:244
  28.3 3.0 %collective-permute-start.3 = (f32[2,384,128]{2,1,0:T(8,128)S(1)}, f32[2,384,128]{2,1,0:T(8,128)S(1)}, u32[]{:S(2)}, u32[]{:S(2)}) collective-permute-start(f32[2,384,128]{2,1,0:T(8,128)S(1)} %get-tuple-element.24), channel_id=1, source_target_pairs={{0,64},{64,0},{1,65},{65,1},{2,66},{66,2},{3,67},{67,3},{4,68},{68... | collective-permute-start | bytes 1179656 | tf_op jit(solution)/shard_map/projections/ppermute | solution.py:344
  31.3 1.0 %projections.3 = f32[2,384,128]{2,1,0:T(8,128)S(1)} custom-call(bf16[4,960,384]{2,1,0:T(8,128)(2,1)S(1)} %copy-done, bf16[4,960,384]{2,1,0:T(8,128)(2,1)S(1)} %get-tuple-element.16.weighted, bf16[4,64,384]{2,1,0:T(8,128)(2,1)S(1)} %weighting.3.edges, bf16[128,384]{1,0:T(8,128)(2,1)S(1)} %get-tuple-element.23.rotation_t), custom_call_target="tpu_custom_call" | custom-call | flops 400000000 | bytes 3000000 | tf_op jit(solution)/shard_map/projections/pallas_call | solution.py:268
  32.4 0.3 collective-permute-done.3
  32.7 12.6 %all_to_all.20 = f32[16,48,128]{2,1,0:T(8,128)S(1)} all-to-all(f32[16,48,128]{2,1,0:T(8,128)S(1)} %bitcast.10), channel_id=1, replica_groups=mesh['x_lo'=2,'core'=2,'x_hi'=2,'z'=8,'y'=4] {'y','x_lo','x_hi'}, dimensions={0} | all-to-all | bytes 786432 | tf_op jit(solution)/shard_map/sum_plane/all_to_all | solution.py:351
  45.4 11.0 %all_to_all.21 = f32[8,48,128]{2,1,0:T(8,128)S(1)} all-to-all(f32[8,48,128]{2,1,0:T(8,128)S(1)} %broadcast_in_dim.4), channel_id=1, replica_groups=mesh['x_lo'=2,'core'=2,'x_hi'=2,'z'=8,'y'=4] {'z'}, dimensions={0} | all-to-all | bytes 393216 | tf_op jit(solution)/shard_map/sum_z/all_to_all | solution.py:320
  56.5 11.7 %all_to_all.22 = f32[16,48,128]{2,1,0:T(8,128)S(1)} all-to-all(f32[16,48,128]{2,1,0:T(8,128)S(1)} %broadcast_in_dim.5), channel_id=1, replica_groups=mesh['x_lo'=2,'core'=2,'x_hi'=2,'z'=8,'y'=4] {'y','x_lo','x_hi'}, dimensions={0} | all-to-all | bytes 786432 | tf_op jit(solution)/shard_map/share_plane/all_to_all | solution.py:320
  68.2 4.2 %collective-permute-start.4 = (f32[2,384,128]{2,1,0:T(8,128)S(1)}, f32[2,384,128]{2,1,0:T(8,128)S(1)}, u32[]{:S(2)}, u32[]{:S(2)}) collective-permute-start(f32[2,384,128]{2,1,0:T(8,128)S(1)} %bitcast.5), channel_id=1, source_target_pairs={{0,64},{64,0},{1,65},{65,1},{2,66},{66,2},{3,67},{67,3},{4,68},{68... | collective-permute-start | bytes 1179656 | tf_op jit(solution)/shard_map/share_core/ppermute | solution.py:358
  72.4 0.8 %share_core.2.begun = f32[4,384,128]{2,1,0:T(8,128)} custom-call(f32[2,384,128]{2,1,0:T(8,128)S(1)} %bitcast.6), custom_call_target="tpu_custom_call" | custom-call | bytes 1000000 | tf_op jit(solution)/shard_map/share_core/pallas_call | solution.py:294
  73.2 0.6 collective-permute-done.4.other
  73.8 0.8 %share_core.3 = f32[4,384,128]{2,1,0:T(8,128)} custom-call(f32[4,384,128]{2,1,0:T(8,128)} %share_core.2.begun, f32[2,384,128]{2,1,0:T(8,128)S(1)} %collective-permute-done.4.other), custom_call_target="tpu_custom_call", output_to_operand_aliasing={{}: (0, {})} | custom-call | bytes 1000000 | tf_op jit(solution)/shard_map/share_core/pallas_call | solution.py:306
  (6 shorter events, 0.1 us)
Async XLA Ops:
  0.0 24.9 %copy-start = (bf16[4,960,384]{2,1,0:T(8,128)(2,1)S(1)}, bf16[4,960,384]{2,1,0:T(8,128)(2,1)}, u32[]{:S(2)}) copy-start(bf16[4,960,384]{2,1,0:T(8,128)(2,1)} %snap.7) | copy-start | bytes 8847364
  0.0 24.9 %copy-start.3 = (s32[960]{0:T(1024)S(1)}, s32[960]{0:T(1024)}, u32[]{:S(2)}) copy-start(s32[960]{0:T(1024)} %param.8) | copy-start | bytes 11524
  0.0 24.9 %copy-start.2 = (f32[960]{0:T(1024)S(1)}, f32[960]{0:T(1024)}, u32[]{:S(2)}) copy-start(f32[960]{0:T(1024)} %param.7) | copy-start | bytes 11524
  0.0 24.9 %copy-start.1 = (f32[960]{0:T(1024)S(1)}, f32[960]{0:T(1024)}, u32[]{:S(2)}) copy-start(f32[960]{0:T(1024)} %param.6) | copy-start | bytes 11524
  1.5 20.9 %all-to-all-start = ((bf16[32,8,128]{2,1,0:T(8,128)(2,1)}), bf16[32,8,128]{2,1,0:T(8,128)(2,1)S(1)}, u32[]{:S(2)}, u32[]{:S(2)}) async-start(bf16[32,8,128]{2,1,0:T(8,128)(2,1)} %get-tuple-element.15), calls=%async_computation | async-start | bytes 131072 | tf_op jit(solution)/shard_map/rotation_rows/all_to_all | solution.py:335
  13.6 13.2 %collective-permute-start = (bf16[2,32,384]{2,1,0:T(8,128)(2,1)S(1)}, bf16[2,32,384]{2,1,0:T(8,128)(2,1)S(1)}, u32[]{:S(2)}, u32[]{:S(2)}) collective-permute-start(bf16[2,32,384]{2,1,0:T(8,128)(2,1)S(1)} %get-tuple-element.20), channel_id=1, source_target_pairs={{0,255},{1,2},{2,1},{3,4},{4,3},{5,6},{6,5},{7,8},{8,7},{9,10},{10... | collective-permute-start | bytes 147464 | tf_op jit(solution)/shard_map/halo/ppermute | solution.py:332
  21.9 4.9 %collective-permute-start.1 = (bf16[2,32,384]{2,1,0:T(8,128)(2,1)S(1)}, bf16[2,32,384]{2,1,0:T(8,128)(2,1)S(1)}, u32[]{:S(2)}, u32[]{:S(2)}) collective-permute-start(bf16[2,32,384]{2,1,0:T(8,128)(2,1)S(1)} %get-tuple-element.21), channel_id=1, source_target_pairs={{0,1},{1,0},{2,3},{3,2},{4,5},{5,4},{6,7},{7,6},{8,9},{9,8},{10,11... | collective-permute-start | bytes 147464 | tf_op jit(solution)/shard_map/halo/ppermute | solution.py:333
  22.4 4.7 %collective-permute-start.2 = (bf16[32,8,128]{2,1,0:T(8,128)(2,1)S(1)}, bf16[32,8,128]{2,1,0:T(8,128)(2,1)S(1)}, u32[]{:S(2)}, u32[]{:S(2)}) collective-permute-start(bf16[32,8,128]{2,1,0:T(8,128)(2,1)S(1)} %all-to-all-done.rot), channel_id=1, source_target_pairs={{0,160},{32,128},{128,32},{160,0},{1,161},{33,129},{129,33},{161,1... | collective-permute-start | bytes 196616 | tf_op jit(solution)/shard_map/rotation_rows/ppermute | solution.py:336
  28.3 4.3 %collective-permute-start.3 = (f32[2,384,128]{2,1,0:T(8,128)S(1)}, f32[2,384,128]{2,1,0:T(8,128)S(1)}, u32[]{:S(2)}, u32[]{:S(2)}) collective-permute-start(f32[2,384,128]{2,1,0:T(8,128)S(1)} %get-tuple-element.24), channel_id=1, source_target_pairs={{0,64},{64,0},{1,65},{65,1},{2,66},{66,2},{3,67},{67,3},{4,68},{68... | collective-permute-start | bytes 1179656 | tf_op jit(solution)/shard_map/projections/ppermute | solution.py:344
  68.2 5.5 %collective-permute-start.4 = (f32[2,384,128]{2,1,0:T(8,128)S(1)}, f32[2,384,128]{2,1,0:T(8,128)S(1)}, u32[]{:S(2)}, u32[]{:S(2)}) collective-permute-start(f32[2,384,128]{2,1,0:T(8,128)S(1)} %bitcast.5), channel_id=1, source_target_pairs={{0,64},{64,0},{1,65},{65,1},{2,66},{66,2},{3,67},{67,3},{4,68},{68... | collective-permute-start | bytes 1179656 | tf_op jit(solution)/shard_map/share_core/ppermute | solution.py:358

commit v13 on v12

--- a/solution.py
+++ b/solution.py
@@ -15,6 +15,7 @@
 WEIGHT_FLOPS = 1_000_000_000
 EDGE_FLOPS = 1_000_000_000
 START_BYTES = 100_000_000
+RIM_BYTES = 1_000_000
 TILE_AXES = ("x_hi", "z", "y")
 SPREAD_AXES = ("z", "y")
 PLANE_AXES = ("y", "x_lo", "x_hi")
@@ -28,54 +29,69 @@
     return pltpu.with_memory_space_constraint(array, pltpu.HBM)
 
 
-def start_kernel(snap, rot_hbm, inner, outer, spread_hbm, begin, end, rot, spread_rot, sems):
+def rows_kernel(rot_hbm, spread_hbm, rot, spread_rot, sem):
+    load = pltpu.make_async_copy(rot_hbm, rot, sem)
+    load.start()
+    load.wait()
+    rows = rot.shape[0]
+    padding = jnp.zeros((PADDED - rows, rot.shape[1]), jnp.float32)
+    block = jnp.concatenate([rot[...].astype(jnp.float32), padding], axis=0).astype(jnp.bfloat16)
+    for tile in range(spread_rot.shape[0]):
+        spread_rot[tile] = block
+    written = pltpu.make_async_copy(spread_rot, spread_hbm, sem)
+    written.start()
+    written.wait()
+
+
+def spread_rows(rotation, tiles):
+    rows, modes = rotation.shape
+    shape = (tiles, PADDED, modes)
+    return pl.pallas_call(
+        rows_kernel,
+        out_shape=jax.ShapeDtypeStruct(shape, jnp.bfloat16),
+        in_specs=[HBM],
+        out_specs=HBM,
+        scratch_shapes=[
+            pltpu.VMEM((rows, modes), jnp.bfloat16),
+            pltpu.VMEM(shape, jnp.bfloat16),
+            pltpu.SemaphoreType.DMA,
+        ],
+        compiler_params=PARAMS,
+        cost_estimate=pl.CostEstimate(flops=0, bytes_accessed=START_BYTES, transcendentals=0),
+    )(in_hbm(rotation))
+
+
+def rims_kernel(snap, inner, outer, begin, end, sems):
     cells = snap.shape[1]
     odd = lax.axis_index("y") % 2
     inner_at = pl.multiple_of((1 - odd) * (cells - HALO), HALO)
     outer_at = pl.multiple_of(odd * (cells - HALO), HALO)
     copies = [
-        pltpu.make_async_copy(rot_hbm, rot, sems.at[0]),
-        pltpu.make_async_copy(snap.at[:, pl.ds(outer_at, HALO)], begin, sems.at[1]),
-        pltpu.make_async_copy(snap.at[:, pl.ds(inner_at, HALO)], end, sems.at[2]),
+        pltpu.make_async_copy(snap.at[:, pl.ds(outer_at, HALO)], begin, sems.at[0]),
+        pltpu.make_async_copy(snap.at[:, pl.ds(inner_at, HALO)], end, sems.at[1]),
     ]
     for copy in copies:
         copy.start()
-    copies[0].wait()
-    rows = rot.shape[0]
-    padding = jnp.zeros((PADDED - rows, rot.shape[1]), jnp.float32)
-    block = jnp.concatenate([rot[...].astype(jnp.float32), padding], axis=0).astype(jnp.bfloat16)
-    for tile in range(spread_rot.shape[0]):
-        spread_rot[tile] = block
-    written = pltpu.make_async_copy(spread_rot, spread_hbm, sems.at[0])
-    written.start()
-    for copy, rim, target in ((copies[1], begin, outer), (copies[2], end, inner)):
+    for copy, rim, target in ((copies[0], begin, outer), (copies[1], end, inner)):
         copy.wait()
         speed = [rim[component].astype(jnp.float32) for component in range(1, COMPONENTS)]
         target[0] = rim[0]
         target[1] = ((speed[0] + speed[1]) + speed[2]).astype(jnp.bfloat16)
-    written.wait()
-
-
-def start(snapshots, rotation, tiles):
+
+
+def rims(snapshots):
     components, _, width = snapshots.shape
-    rows, modes = rotation.shape
     edge = jax.ShapeDtypeStruct((2, HALO, width), jnp.bfloat16)
     rim = pltpu.VMEM((components, HALO, width), jnp.bfloat16)
     return pl.pallas_call(
-        start_kernel,
-        out_shape=(edge, edge, jax.ShapeDtypeStruct((tiles, PADDED, modes), jnp.bfloat16)),
-        in_specs=[HBM, HBM],
-        out_specs=(VMEM, VMEM, HBM),
-        scratch_shapes=[
-            rim,
-            rim,
-            pltpu.VMEM((rows, modes), jnp.bfloat16),
-            pltpu.VMEM((tiles, PADDED, modes), jnp.bfloat16),
-            pltpu.SemaphoreType.DMA((3,)),
-        ],
-        compiler_params=PARAMS,
-        cost_estimate=pl.CostEstimate(flops=0, bytes_accessed=START_BYTES, transcendentals=0),
-    )(snapshots, in_hbm(rotation))
+        rims_kernel,
+        out_shape=(edge, edge),
+        in_specs=[HBM],
+        out_specs=(VMEM, VMEM),
+        scratch_shapes=[rim, rim, pltpu.SemaphoreType.DMA((2,))],
+        compiler_params=PARAMS,
+        cost_estimate=pl.CostEstimate(flops=0, bytes_accessed=RIM_BYTES, transcendentals=0),
+    )(in_hbm(snapshots))
 
 
 def stencil_of(shift, window, offset):
@@ -327,7 +343,8 @@
     across = [(i, (i + 1 if i % 2 else i - 1) % count) for i in range(count)]
     swap = [(0, 1), (1, 0)]
     with jax.named_scope("start"):
-        inner, outer, rows = start(in_hbm(snapshots), rotation, lax.axis_size(SPREAD_AXES))
+        rows = spread_rows(rotation, lax.axis_size(SPREAD_AXES))
+        inner, outer = rims(snapshots)
     with jax.named_scope("halo"):
         outer = lax.ppermute(outer, CELL_AXES, across)
         inner = lax.ppermute(inner, CELL_AXES, inside)

time: 74.8 us -> 75.1 us (level)
  Pallas kernels: 7.41 us -> 8.38 us
    pallas_call x1 -> x2, Pallas kernels: 1.49 us -> 2.46 us  [the longest x1 1.48 us: spread_rows(): pl.pallas_call(rows_kernel, out_shape=jax.ShapeDtypeStruct(shape, jnp.bfl...]
  transfers between devices with their start and end apart: 6 -> 6, of which waited for: 3 -> 3; matrix products, arithmetic and copies ran while one was open for 0% -> 0% of each run, Pallas kernels for 5% -> 7%
where the time goes in v13:
time: 75.1 us; the launch traced here: 74.8 us
  blocking collectives  35.3 us (47%)
  starting transfers between devices  29.9 us (40%)
  Pallas kernels  8.38 us (11%)
  waiting for transfers between devices  0.98 us (1%)
    all_to_all x2, blocking collectives, spread(): lax.all_to_all(jnp.broadcast_to(block[None], (count,) + block.shape), axe...  22.7 us
    all_to_all x1, blocking collectives, on_device(): piece = jnp.sum(lax.all_to_all(pieces, PLANE_AXES, 0, 0), axis=0)  12.6 us
    all_to_all x1, starting transfers between devices, on_device(): own_pieces = lax.all_to_all(rows, SPREAD_AXES, 0, 0)  12 us
    ppermute x1, starting transfers between devices, on_device(): outer = lax.ppermute(outer, CELL_AXES, across)  8.31 us
    ppermute x1, starting transfers between devices, on_device(): other = lax.ppermute(mine, 'core', swap)  4.2 us
    ppermute x1, starting transfers between devices, on_device(): received = lax.ppermute(send, 'core', swap)  3.25 us
    ppermute x1, starting transfers between devices, on_device(): lax.ppermute(own_pieces, ('x_lo', 'x_hi'), [(i, 3 - i) for i in range(4)])  2.07 us
    pallas_call x1, Pallas kernels, weigh(): pl.pallas_call(weighting_kernel, out_shape=(jax.ShapeDtypeStruct(snapshot...  1.86 us
  transfers between devices with their start and end apart: 6, of which 3 were waited for; matrix products, arithmetic and copies ran while one was open for 0% of the time, Pallas kernels for 7%

profile of v13, /device:TPU:1, one launch (start us, length us, event | category | flops | bytes accessed | tf_op | source)
XLA Modules:
  0.0 74.8 jit_solution(4145060903823035495)
XLA Ops:
  0.0 0.0 copy-start
  0.0 0.0 copy-start.3
  0.0 0.0 copy-start.2
  0.0 0.0 copy-start.1
  0.0 1.5 %start.2 = bf16[32,8,128]{2,1,0:T(8,128)(2,1)} custom-call(bf16[6,128]{1,0:T(8,128)(2,1)} %rot_hbm.1), custom_call_target="tpu_custom_call" | custom-call | bytes 100000000 | tf_op jit(solution)/shard_map/start/pallas_call | solution.py:49
  1.5 12.0 %all-to-all-start = ((bf16[32,8,128]{2,1,0:T(8,128)(2,1)}), bf16[32,8,128]{2,1,0:T(8,128)(2,1)S(1)}, u32[]{:S(2)}, u32[]{:S(2)}) async-start(bf16[32,8,128]{2,1,0:T(8,128)(2,1)} %start.2), calls=%async_computation | async-start | bytes 131072 | tf_op jit(solution)/shard_map/rotation_rows/all_to_all | solution.py:352
  13.6 1.0 %start.3 = (bf16[2,32,384]{2,1,0:T(8,128)(2,1)S(1)}, bf16[2,32,384]{2,1,0:T(8,128)(2,1)S(1)}) custom-call(bf16[4,960,384]{2,1,0:T(8,128)(2,1)} %snap.7), custom_call_target="tpu_custom_call" | custom-call | bytes 1000000 | tf_op jit(solution)/shard_map/start/pallas_call | solution.py:86
  14.6 8.3 %collective-permute-start = (bf16[2,32,384]{2,1,0:T(8,128)(2,1)S(1)}, bf16[2,32,384]{2,1,0:T(8,128)(2,1)S(1)}, u32[]{:S(2)}, u32[]{:S(2)}) collective-permute-start(bf16[2,32,384]{2,1,0:T(8,128)(2,1)S(1)} %get-tuple-element.18), channel_id=1, source_target_pairs={{0,255},{1,2},{2,1},{3,4},{4,3},{5,6},{6,5},{7,8},{8,7},{9,10},{10... | collective-permute-start | bytes 147464 | tf_op jit(solution)/shard_map/halo/ppermute | solution.py:349
  22.9 0.0 collective-permute-start.1
  22.9 0.0 all-to-all-done.rot
  22.9 2.1 %collective-permute-start.2 = (bf16[32,8,128]{2,1,0:T(8,128)(2,1)S(1)}, bf16[32,8,128]{2,1,0:T(8,128)(2,1)S(1)}, u32[]{:S(2)}, u32[]{:S(2)}) collective-permute-start(bf16[32,8,128]{2,1,0:T(8,128)(2,1)S(1)} %all-to-all-done.rot), channel_id=1, source_target_pairs={{0,160},{32,128},{128,32},{160,0},{1,161},{33,129},{129,33},{161,1... | collective-permute-start | bytes 196616 | tf_op jit(solution)/shard_map/rotation_rows/ppermute | solution.py:353
  24.9 0.0 copy-done
  24.9 0.0 copy-done.3
  24.9 0.0 copy-done.2
  24.9 0.0 copy-done.1
  25.0 1.9 %weighting.2 = (bf16[4,960,384]{2,1,0:T(8,128)(2,1)S(1)}, f32[64,8]{1,0:T(8,128)S(1)}, bf16[4,64,384]{2,1,0:T(8,128)(2,1)S(1)}, bf16[4,64,384]{2,1,0:T(8,128)(2,1)S(1)}, f32[192,128]{1,0:T(8,128)S(1)}) custom-call(bf16[4,960,384]{2,1,0:T(8,128)(2,1)S(1)} %copy-done, f32[1,960]{1,0:T(1,128)S(1)} %bitcast.7, f32[1,960]{1,0:T(1,128)S(1)} %bitcast.8, ...), custom_call_target="tpu_custom_call" | custom-call | flops 1000000000 | bytes 6000000 | tf_op jit(solution)/shard_map/weighting/pallas_call | solution.py:170
  26.8 0.0 collective-permute-done.outer
  26.8 0.0 collective-permute-done.1.inner
  26.8 0.3 weighting.3.edges
  27.1 0.1 collective-permute-done.2.rot
  27.2 1.2 %projections.2 = (f32[2,384,128]{2,1,0:T(8,128)S(1)}, bf16[128,384]{1,0:T(8,128)(2,1)S(1)}) custom-call(bf16[4,960,384]{2,1,0:T(8,128)(2,1)S(1)} %copy-done, bf16[4,960,384]{2,1,0:T(8,128)(2,1)S(1)} %get-tuple-element.14.weighted, bf16[4,64,384]{2,1,0:T(8,128)(2,1)S(1)} %weighting.3.edges, f32[192,128]{1,0:T(8,128)S(1)} %get-tuple-element.20.own_rows, ...), custom_call_target="tpu_custom_call" | custom-call | flops 400000000 | bytes 3000000 | tf_op jit(solution)/shard_map/projections/pallas_call | solution.py:260
  28.4 3.2 %collective-permute-start.3 = (f32[2,384,128]{2,1,0:T(8,128)S(1)}, f32[2,384,128]{2,1,0:T(8,128)S(1)}, u32[]{:S(2)}, u32[]{:S(2)}) collective-permute-start(f32[2,384,128]{2,1,0:T(8,128)S(1)} %get-tuple-element.22), channel_id=1, source_target_pairs={{0,64},{64,0},{1,65},{65,1},{2,66},{66,2},{3,67},{67,3},{4,68},{68... | collective-permute-start | bytes 1179656 | tf_op jit(solution)/shard_map/projections/ppermute | solution.py:361
  31.7 1.0 %projections.3 = f32[2,384,128]{2,1,0:T(8,128)S(1)} custom-call(bf16[4,960,384]{2,1,0:T(8,128)(2,1)S(1)} %copy-done, bf16[4,960,384]{2,1,0:T(8,128)(2,1)S(1)} %get-tuple-element.14.weighted, bf16[4,64,384]{2,1,0:T(8,128)(2,1)S(1)} %weighting.3.edges, bf16[128,384]{1,0:T(8,128)(2,1)S(1)} %get-tuple-element.21.rotation_t), custom_call_target="tpu_custom_call" | custom-call | flops 400000000 | bytes 3000000 | tf_op jit(solution)/shard_map/projections/pallas_call | solution.py:284
  32.7 0.3 collective-permute-done.3
  33.1 12.6 %all_to_all.20 = f32[16,48,128]{2,1,0:T(8,128)S(1)} all-to-all(f32[16,48,128]{2,1,0:T(8,128)S(1)} %bitcast.10), channel_id=1, replica_groups=mesh['x_lo'=2,'core'=2,'x_hi'=2,'z'=8,'y'=4] {'y','x_lo','x_hi'}, dimensions={0} | all-to-all | bytes 786432 | tf_op jit(solution)/shard_map/sum_plane/all_to_all | solution.py:368
  45.7 11.0 %all_to_all.21 = f32[8,48,128]{2,1,0:T(8,128)S(1)} all-to-all(f32[8,48,128]{2,1,0:T(8,128)S(1)} %broadcast_in_dim.4), channel_id=1, replica_groups=mesh['x_lo'=2,'core'=2,'x_hi'=2,'z'=8,'y'=4] {'z'}, dimensions={0} | all-to-all | bytes 393216 | tf_op jit(solution)/shard_map/sum_z/all_to_all | solution.py:336
  56.8 11.7 %all_to_all.22 = f32[16,48,128]{2,1,0:T(8,128)S(1)} all-to-all(f32[16,48,128]{2,1,0:T(8,128)S(1)} %broadcast_in_dim.5), channel_id=1, replica_groups=mesh['x_lo'=2,'core'=2,'x_hi'=2,'z'=8,'y'=4] {'y','x_lo','x_hi'}, dimensions={0} | all-to-all | bytes 786432 | tf_op jit(solution)/shard_map/share_plane/all_to_all | solution.py:336
  68.5 4.2 %collective-permute-start.4 = (f32[2,384,128]{2,1,0:T(8,128)S(1)}, f32[2,384,128]{2,1,0:T(8,128)S(1)}, u32[]{:S(2)}, u32[]{:S(2)}) collective-permute-start(f32[2,384,128]{2,1,0:T(8,128)S(1)} %bitcast.5), channel_id=1, source_target_pairs={{0,64},{64,0},{1,65},{65,1},{2,66},{66,2},{3,67},{67,3},{4,68},{68... | collective-permute-start | bytes 1179656 | tf_op jit(solution)/shard_map/share_core/ppermute | solution.py:375
  72.7 0.8 %share_core.2.begun = f32[4,384,128]{2,1,0:T(8,128)} custom-call(f32[2,384,128]{2,1,0:T(8,128)S(1)} %bitcast.6), custom_call_target="tpu_custom_call" | custom-call | bytes 1000000 | tf_op jit(solution)/shard_map/share_core/pallas_call | solution.py:310
  73.5 0.6 collective-permute-done.4.other
  74.1 0.8 %share_core.3 = f32[4,384,128]{2,1,0:T(8,128)} custom-call(f32[4,384,128]{2,1,0:T(8,128)} %share_core.2.begun, f32[2,384,128]{2,1,0:T(8,128)S(1)} %collective-permute-done.4.other), custom_call_target="tpu_custom_call", output_to_operand_aliasing={{}: (0, {})} | custom-call | bytes 1000000 | tf_op jit(solution)/shard_map/share_core/pallas_call | solution.py:322
  (6 shorter events, 0.1 us)
Async XLA Ops:
  0.0 24.9 %copy-start = (bf16[4,960,384]{2,1,0:T(8,128)(2,1)S(1)}, bf16[4,960,384]{2,1,0:T(8,128)(2,1)}, u32[]{:S(2)}) copy-start(bf16[4,960,384]{2,1,0:T(8,128)(2,1)} %snap.7) | copy-start | bytes 8847364
  0.0 24.9 %copy-start.3 = (s32[960]{0:T(1024)S(1)}, s32[960]{0:T(1024)}, u32[]{:S(2)}) copy-start(s32[960]{0:T(1024)} %param.8) | copy-start | bytes 11524
  0.0 24.9 %copy-start.2 = (f32[960]{0:T(1024)S(1)}, f32[960]{0:T(1024)}, u32[]{:S(2)}) copy-start(f32[960]{0:T(1024)} %param.7) | copy-start | bytes 11524
  0.0 24.9 %copy-start.1 = (f32[960]{0:T(1024)S(1)}, f32[960]{0:T(1024)}, u32[]{:S(2)}) copy-start(f32[960]{0:T(1024)} %param.6) | copy-start | bytes 11524
  1.5 21.4 %all-to-all-start = ((bf16[32,8,128]{2,1,0:T(8,128)(2,1)}), bf16[32,8,128]{2,1,0:T(8,128)(2,1)S(1)}, u32[]{:S(2)}, u32[]{:S(2)}) async-start(bf16[32,8,128]{2,1,0:T(8,128)(2,1)} %start.2), calls=%async_computation | async-start | bytes 131072 | tf_op jit(solution)/shard_map/rotation_rows/all_to_all | solution.py:352
  14.6 12.3 %collective-permute-start = (bf16[2,32,384]{2,1,0:T(8,128)(2,1)S(1)}, bf16[2,32,384]{2,1,0:T(8,128)(2,1)S(1)}, u32[]{:S(2)}, u32[]{:S(2)}) collective-permute-start(bf16[2,32,384]{2,1,0:T(8,128)(2,1)S(1)} %get-tuple-element.18), channel_id=1, source_target_pairs={{0,255},{1,2},{2,1},{3,4},{4,3},{5,6},{6,5},{7,8},{8,7},{9,10},{10... | collective-permute-start | bytes 147464 | tf_op jit(solution)/shard_map/halo/ppermute | solution.py:349
  22.9 4.0 %collective-permute-start.1 = (bf16[2,32,384]{2,1,0:T(8,128)(2,1)S(1)}, bf16[2,32,384]{2,1,0:T(8,128)(2,1)S(1)}, u32[]{:S(2)}, u32[]{:S(2)}) collective-permute-start(bf16[2,32,384]{2,1,0:T(8,128)(2,1)S(1)} %get-tuple-element.19), channel_id=1, source_target_pairs={{0,1},{1,0},{2,3},{3,2},{4,5},{5,4},{6,7},{7,6},{8,9},{9,8},{10,11... | collective-permute-start | bytes 147464 | tf_op jit(solution)/shard_map/halo/ppermute | solution.py:350
  22.9 4.3 %collective-permute-start.2 = (bf16[32,8,128]{2,1,0:T(8,128)(2,1)S(1)}, bf16[32,8,128]{2,1,0:T(8,128)(2,1)S(1)}, u32[]{:S(2)}, u32[]{:S(2)}) collective-permute-start(bf16[32,8,128]{2,1,0:T(8,128)(2,1)S(1)} %all-to-all-done.rot), channel_id=1, source_target_pairs={{0,160},{32,128},{128,32},{160,0},{1,161},{33,129},{129,33},{161,1... | collective-permute-start | bytes 196616 | tf_op jit(solution)/shard_map/rotation_rows/ppermute | solution.py:353
  28.4 4.6 %collective-permute-start.3 = (f32[2,384,128]{2,1,0:T(8,128)S(1)}, f32[2,384,128]{2,1,0:T(8,128)S(1)}, u32[]{:S(2)}, u32[]{:S(2)}) collective-permute-start(f32[2,384,128]{2,1,0:T(8,128)S(1)} %get-tuple-element.22), channel_id=1, source_target_pairs={{0,64},{64,0},{1,65},{65,1},{2,66},{66,2},{3,67},{67,3},{4,68},{68... | collective-permute-start | bytes 1179656 | tf_op jit(solution)/shard_map/projections/ppermute | solution.py:361
  68.5 5.5 %collective-permute-start.4 = (f32[2,384,128]{2,1,0:T(8,128)S(1)}, f32[2,384,128]{2,1,0:T(8,128)S(1)}, u32[]{:S(2)}, u32[]{:S(2)}) collective-permute-start(f32[2,384,128]{2,1,0:T(8,128)S(1)} %bitcast.5), channel_id=1, source_target_pairs={{0,64},{64,0},{1,65},{65,1},{2,66},{66,2},{3,67},{67,3},{4,68},{68... | collective-permute-start | bytes 1179656 | tf_op jit(solution)/shard_map/share_core/ppermute | solution.py:375

commit v14 on v12

--- a/solution.py
+++ b/solution.py
@@ -51,15 +51,18 @@
     for copy, rim, target in ((copies[1], begin, outer), (copies[2], end, inner)):
         copy.wait()
         speed = [rim[component].astype(jnp.float32) for component in range(1, COMPONENTS)]
+        total = (speed[0] + speed[1]) + speed[2]
+        rounded = total.astype(jnp.bfloat16)
         target[0] = rim[0]
-        target[1] = ((speed[0] + speed[1]) + speed[2]).astype(jnp.bfloat16)
+        target[1] = rounded
+        target[2] = (total - rounded.astype(jnp.float32)).astype(jnp.bfloat16)
     written.wait()
 
 
 def start(snapshots, rotation, tiles):
     components, _, width = snapshots.shape
     rows, modes = rotation.shape
-    edge = jax.ShapeDtypeStruct((2, HALO, width), jnp.bfloat16)
+    edge = jax.ShapeDtypeStruct((3, HALO, width), jnp.bfloat16)
     rim = pltpu.VMEM((components, HALO, width), jnp.bfloat16)
     return pl.pallas_call(
         start_kernel,
@@ -182,7 +185,7 @@
     high = jnp.where(mask, outer[...], inner[...])
 
     def beyond(halo, component):
-        return halo[component] if component < 2 else blank
+        return halo[component] if component < 3 else blank
 
     first = weigh_rows(
         edge_scale[0:HALO],

time: 74.8 us -> 74.9 us (level)
  no operation moved by 1% of the time
where the time goes in v14:
time: 74.9 us; the launch traced here: 74.6 us
  blocking collectives  35.4 us (47%)
  starting transfers between devices  30.1 us (40%)
  Pallas kernels  7.43 us (10%)
  waiting for transfers between devices  1.42 us (2%)
    all_to_all x2, blocking collectives, spread(): lax.all_to_all(jnp.broadcast_to(block[None], (count,) + block.shape), axe...  22.7 us
    all_to_all x1, blocking collectives, on_device(): piece = jnp.sum(lax.all_to_all(pieces, PLANE_AXES, 0, 0), axis=0)  12.6 us
    all_to_all x1, starting transfers between devices, on_device(): own_pieces = lax.all_to_all(rows, SPREAD_AXES, 0, 0)  12 us
    ppermute x1, starting transfers between devices, on_device(): outer = lax.ppermute(outer, CELL_AXES, across)  8.31 us
    ppermute x1, starting transfers between devices, on_device(): other = lax.ppermute(mine, 'core', swap)  4.2 us
    ppermute x1, starting transfers between devices, on_device(): received = lax.ppermute(send, 'core', swap)  3.07 us
    ppermute x1, starting transfers between devices, on_device(): lax.ppermute(own_pieces, ('x_lo', 'x_hi'), [(i, 3 - i) for i in range(4)])  2.5 us
    pallas_call x1, Pallas kernels, weigh(): pl.pallas_call(weighting_kernel, out_shape=(jax.ShapeDtypeStruct(snapshot...  1.85 us
  transfers between devices with their start and end apart: 6, of which 3 were waited for; matrix products, arithmetic and copies ran while one was open for 0% of the time, Pallas kernels for 5%

profile of v14, /device:TPU:1, one launch (start us, length us, event | category | flops | bytes accessed | tf_op | source)
XLA Modules:
  0.0 74.6 jit_solution(17031215291403677156)
XLA Ops:
  0.0 0.0 copy-start
  0.0 0.0 copy-start.3
  0.0 0.0 copy-start.2
  0.0 0.0 copy-start.1
  0.0 1.5 %start.1 = (bf16[3,32,384]{2,1,0:T(8,128)(2,1)S(1)}, bf16[3,32,384]{2,1,0:T(8,128)(2,1)S(1)}, bf16[32,8,128]{2,1,0:T(8,128)(2,1)}) custom-call(bf16[4,960,384]{2,1,0:T(8,128)(2,1)} %snap.7, bf16[6,128]{1,0:T(8,128)(2,1)} %rot_hbm.1), custom_call_target="tpu_custom_call" | custom-call | bytes 100000000 | tf_op jit(solution)/shard_map/start/pallas_call | solution.py:67
  1.5 12.0 %all-to-all-start = ((bf16[32,8,128]{2,1,0:T(8,128)(2,1)}), bf16[32,8,128]{2,1,0:T(8,128)(2,1)S(1)}, u32[]{:S(2)}, u32[]{:S(2)}) async-start(bf16[32,8,128]{2,1,0:T(8,128)(2,1)} %get-tuple-element.15), calls=%async_computation | async-start | bytes 131072 | tf_op jit(solution)/shard_map/rotation_rows/all_to_all | solution.py:338
  13.6 8.3 %collective-permute-start = (bf16[3,32,384]{2,1,0:T(8,128)(2,1)S(1)}, bf16[3,32,384]{2,1,0:T(8,128)(2,1)S(1)}, u32[]{:S(2)}, u32[]{:S(2)}) collective-permute-start(bf16[3,32,384]{2,1,0:T(8,128)(2,1)S(1)} %get-tuple-element.20), channel_id=1, source_target_pairs={{0,255},{1,2},{2,1},{3,4},{4,3},{5,6},{6,5},{7,8},{8,7},{9,10},{10... | collective-permute-start | bytes 221192 | tf_op jit(solution)/shard_map/halo/ppermute | solution.py:335
  21.9 0.0 collective-permute-start.1
  21.9 0.5 all-to-all-done.rot
  22.4 2.5 %collective-permute-start.2 = (bf16[32,8,128]{2,1,0:T(8,128)(2,1)S(1)}, bf16[32,8,128]{2,1,0:T(8,128)(2,1)S(1)}, u32[]{:S(2)}, u32[]{:S(2)}) collective-permute-start(bf16[32,8,128]{2,1,0:T(8,128)(2,1)S(1)} %all-to-all-done.rot), channel_id=1, source_target_pairs={{0,160},{32,128},{128,32},{160,0},{1,161},{33,129},{129,33},{161,1... | collective-permute-start | bytes 196616 | tf_op jit(solution)/shard_map/rotation_rows/ppermute | solution.py:339
  24.9 0.0 copy-done
  24.9 0.0 copy-done.3
  24.9 0.0 copy-done.2
  24.9 0.0 copy-done.1
  24.9 1.9 %weighting.2 = (bf16[4,960,384]{2,1,0:T(8,128)(2,1)S(1)}, f32[64,8]{1,0:T(8,128)S(1)}, bf16[4,64,384]{2,1,0:T(8,128)(2,1)S(1)}, bf16[4,64,384]{2,1,0:T(8,128)(2,1)S(1)}, f32[192,128]{1,0:T(8,128)S(1)}) custom-call(bf16[4,960,384]{2,1,0:T(8,128)(2,1)S(1)} %copy-done, f32[1,960]{1,0:T(1,128)S(1)} %bitcast.7, f32[1,960]{1,0:T(1,128)S(1)} %bitcast.8, ...), custom_call_target="tpu_custom_call" | custom-call | flops 1000000000 | bytes 6000000 | tf_op jit(solution)/shard_map/weighting/pallas_call | solution.py:157
  26.8 0.0 collective-permute-done.outer
  26.8 0.0 collective-permute-done.1.inner
  26.8 0.3 weighting.3.edges
  27.1 0.0 collective-permute-done.2.rot
  27.1 1.2 %projections.2 = (f32[2,384,128]{2,1,0:T(8,128)S(1)}, bf16[128,384]{1,0:T(8,128)(2,1)S(1)}) custom-call(bf16[4,960,384]{2,1,0:T(8,128)(2,1)S(1)} %copy-done, bf16[4,960,384]{2,1,0:T(8,128)(2,1)S(1)} %get-tuple-element.16.weighted, bf16[4,64,384]{2,1,0:T(8,128)(2,1)S(1)} %weighting.3.edges, f32[192,128]{1,0:T(8,128)S(1)} %get-tuple-element.22.own_rows, ...), custom_call_target="tpu_custom_call" | custom-call | flops 400000000 | bytes 3000000 | tf_op jit(solution)/shard_map/projections/pallas_call | solution.py:247
  28.3 3.1 %collective-permute-start.3 = (f32[2,384,128]{2,1,0:T(8,128)S(1)}, f32[2,384,128]{2,1,0:T(8,128)S(1)}, u32[]{:S(2)}, u32[]{:S(2)}) collective-permute-start(f32[2,384,128]{2,1,0:T(8,128)S(1)} %get-tuple-element.24), channel_id=1, source_target_pairs={{0,64},{64,0},{1,65},{65,1},{2,66},{66,2},{3,67},{67,3},{4,68},{68... | collective-permute-start | bytes 1179656 | tf_op jit(solution)/shard_map/projections/ppermute | solution.py:347
  31.4 1.1 %projections.3 = f32[2,384,128]{2,1,0:T(8,128)S(1)} custom-call(bf16[4,960,384]{2,1,0:T(8,128)(2,1)S(1)} %copy-done, bf16[4,960,384]{2,1,0:T(8,128)(2,1)S(1)} %get-tuple-element.16.weighted, bf16[4,64,384]{2,1,0:T(8,128)(2,1)S(1)} %weighting.3.edges, bf16[128,384]{1,0:T(8,128)(2,1)S(1)} %get-tuple-element.23.rotation_t), custom_call_target="tpu_custom_call" | custom-call | flops 400000000 | bytes 3000000 | tf_op jit(solution)/shard_map/projections/pallas_call | solution.py:271
  32.5 0.3 collective-permute-done.3
  32.8 12.6 %all_to_all.20 = f32[16,48,128]{2,1,0:T(8,128)S(1)} all-to-all(f32[16,48,128]{2,1,0:T(8,128)S(1)} %bitcast.10), channel_id=1, replica_groups=mesh['x_lo'=2,'core'=2,'x_hi'=2,'z'=8,'y'=4] {'y','x_lo','x_hi'}, dimensions={0} | all-to-all | bytes 786432 | tf_op jit(solution)/shard_map/sum_plane/all_to_all | solution.py:354
  45.5 11.0 %all_to_all.21 = f32[8,48,128]{2,1,0:T(8,128)S(1)} all-to-all(f32[8,48,128]{2,1,0:T(8,128)S(1)} %broadcast_in_dim.4), channel_id=1, replica_groups=mesh['x_lo'=2,'core'=2,'x_hi'=2,'z'=8,'y'=4] {'z'}, dimensions={0} | all-to-all | bytes 393216 | tf_op jit(solution)/shard_map/sum_z/all_to_all | solution.py:323
  56.6 11.7 %all_to_all.22 = f32[16,48,128]{2,1,0:T(8,128)S(1)} all-to-all(f32[16,48,128]{2,1,0:T(8,128)S(1)} %broadcast_in_dim.5), channel_id=1, replica_groups=mesh['x_lo'=2,'core'=2,'x_hi'=2,'z'=8,'y'=4] {'y','x_lo','x_hi'}, dimensions={0} | all-to-all | bytes 786432 | tf_op jit(solution)/shard_map/share_plane/all_to_all | solution.py:323
  68.3 4.2 %collective-permute-start.4 = (f32[2,384,128]{2,1,0:T(8,128)S(1)}, f32[2,384,128]{2,1,0:T(8,128)S(1)}, u32[]{:S(2)}, u32[]{:S(2)}) collective-permute-start(f32[2,384,128]{2,1,0:T(8,128)S(1)} %bitcast.5), channel_id=1, source_target_pairs={{0,64},{64,0},{1,65},{65,1},{2,66},{66,2},{3,67},{67,3},{4,68},{68... | collective-permute-start | bytes 1179656 | tf_op jit(solution)/shard_map/share_core/ppermute | solution.py:361
  72.5 0.8 %share_core.2.begun = f32[4,384,128]{2,1,0:T(8,128)} custom-call(f32[2,384,128]{2,1,0:T(8,128)S(1)} %bitcast.6), custom_call_target="tpu_custom_call" | custom-call | bytes 1000000 | tf_op jit(solution)/shard_map/share_core/pallas_call | solution.py:297
  73.3 0.6 collective-permute-done.4.other
  73.9 0.8 %share_core.3 = f32[4,384,128]{2,1,0:T(8,128)} custom-call(f32[4,384,128]{2,1,0:T(8,128)} %share_core.2.begun, f32[2,384,128]{2,1,0:T(8,128)S(1)} %collective-permute-done.4.other), custom_call_target="tpu_custom_call", output_to_operand_aliasing={{}: (0, {})} | custom-call | bytes 1000000 | tf_op jit(solution)/shard_map/share_core/pallas_call | solution.py:309
  (6 shorter events, 0.1 us)
Async XLA Ops:
  0.0 24.9 %copy-start = (bf16[4,960,384]{2,1,0:T(8,128)(2,1)S(1)}, bf16[4,960,384]{2,1,0:T(8,128)(2,1)}, u32[]{:S(2)}) copy-start(bf16[4,960,384]{2,1,0:T(8,128)(2,1)} %snap.7) | copy-start | bytes 8847364
  0.0 24.9 %copy-start.3 = (s32[960]{0:T(1024)S(1)}, s32[960]{0:T(1024)}, u32[]{:S(2)}) copy-start(s32[960]{0:T(1024)} %param.8) | copy-start | bytes 11524
  0.0 24.9 %copy-start.2 = (f32[960]{0:T(1024)S(1)}, f32[960]{0:T(1024)}, u32[]{:S(2)}) copy-start(f32[960]{0:T(1024)} %param.7) | copy-start | bytes 11524
  0.0 24.9 %copy-start.1 = (f32[960]{0:T(1024)S(1)}, f32[960]{0:T(1024)}, u32[]{:S(2)}) copy-start(f32[960]{0:T(1024)} %param.6) | copy-start | bytes 11524
  1.5 20.9 %all-to-all-start = ((bf16[32,8,128]{2,1,0:T(8,128)(2,1)}), bf16[32,8,128]{2,1,0:T(8,128)(2,1)S(1)}, u32[]{:S(2)}, u32[]{:S(2)}) async-start(bf16[32,8,128]{2,1,0:T(8,128)(2,1)} %get-tuple-element.15), calls=%async_computation | async-start | bytes 131072 | tf_op jit(solution)/shard_map/rotation_rows/all_to_all | solution.py:338
  13.6 13.2 %collective-permute-start = (bf16[3,32,384]{2,1,0:T(8,128)(2,1)S(1)}, bf16[3,32,384]{2,1,0:T(8,128)(2,1)S(1)}, u32[]{:S(2)}, u32[]{:S(2)}) collective-permute-start(bf16[3,32,384]{2,1,0:T(8,128)(2,1)S(1)} %get-tuple-element.20), channel_id=1, source_target_pairs={{0,255},{1,2},{2,1},{3,4},{4,3},{5,6},{6,5},{7,8},{8,7},{9,10},{10... | collective-permute-start | bytes 221192 | tf_op jit(solution)/shard_map/halo/ppermute | solution.py:335
  21.9 4.9 %collective-permute-start.1 = (bf16[3,32,384]{2,1,0:T(8,128)(2,1)S(1)}, bf16[3,32,384]{2,1,0:T(8,128)(2,1)S(1)}, u32[]{:S(2)}, u32[]{:S(2)}) collective-permute-start(bf16[3,32,384]{2,1,0:T(8,128)(2,1)S(1)} %get-tuple-element.21), channel_id=1, source_target_pairs={{0,1},{1,0},{2,3},{3,2},{4,5},{5,4},{6,7},{7,6},{8,9},{9,8},{10,11... | collective-permute-start | bytes 221192 | tf_op jit(solution)/shard_map/halo/ppermute | solution.py:336
  22.4 4.7 %collective-permute-start.2 = (bf16[32,8,128]{2,1,0:T(8,128)(2,1)S(1)}, bf16[32,8,128]{2,1,0:T(8,128)(2,1)S(1)}, u32[]{:S(2)}, u32[]{:S(2)}) collective-permute-start(bf16[32,8,128]{2,1,0:T(8,128)(2,1)S(1)} %all-to-all-done.rot), channel_id=1, source_target_pairs={{0,160},{32,128},{128,32},{160,0},{1,161},{33,129},{129,33},{161,1... | collective-permute-start | bytes 196616 | tf_op jit(solution)/shard_map/rotation_rows/ppermute | solution.py:339
  28.3 4.4 %collective-permute-start.3 = (f32[2,384,128]{2,1,0:T(8,128)S(1)}, f32[2,384,128]{2,1,0:T(8,128)S(1)}, u32[]{:S(2)}, u32[]{:S(2)}) collective-permute-start(f32[2,384,128]{2,1,0:T(8,128)S(1)} %get-tuple-element.24), channel_id=1, source_target_pairs={{0,64},{64,0},{1,65},{65,1},{2,66},{66,2},{3,67},{67,3},{4,68},{68... | collective-permute-start | bytes 1179656 | tf_op jit(solution)/shard_map/projections/ppermute | solution.py:347
  68.3 5.5 %collective-permute-start.4 = (f32[2,384,128]{2,1,0:T(8,128)S(1)}, f32[2,384,128]{2,1,0:T(8,128)S(1)}, u32[]{:S(2)}, u32[]{:S(2)}) collective-permute-start(f32[2,384,128]{2,1,0:T(8,128)S(1)} %bitcast.5), channel_id=1, source_target_pairs={{0,64},{64,0},{1,65},{65,1},{2,66},{66,2},{3,67},{67,3},{4,68},{68... | collective-permute-start | bytes 1179656 | tf_op jit(solution)/shard_map/share_core/ppermute | solution.py:361

commit v15 on v14

--- a/solution.py
+++ b/solution.py
@@ -228,33 +228,48 @@
 
 
 def sent_kernel(snap, weighted, edges, own_rows, rot, send, rotation_t):
-    half = send.shape[0]
-    sent = (1 - lax.axis_index("core")) * half
+    sent = (1 - lax.axis_index("core")) * (COMPONENTS // 2)
     own = own_rows[...]
     other = compact_of(rot)
     first = lax.broadcast_in_dim(lax.axis_index("x_hi"), own.shape, ()) == 0
     rows = jnp.concatenate([jnp.where(first, own, other), jnp.where(first, other, own)], axis=0)
     turned = rows.T.astype(jnp.bfloat16)
     rotation_t[...] = turned
-    for place in range(half):
-        mode = modes_of(turned, snap[sent + place])
-        send[place] = totals_of(mode, weighted.at[sent + place], edges.at[sent + place])
+    mode = modes_of(turned, snap[sent])
+    send[0] = totals_of(mode, weighted.at[sent], edges.at[sent])
 
 
 def project_sent(snapshots, weighted, edges, own_rows, rotation):
-    components, _, width = snapshots.shape
+    _, _, width = snapshots.shape
     modes = rotation.shape[2]
     return pl.pallas_call(
         sent_kernel,
         out_shape=(
-            jax.ShapeDtypeStruct((components // 2, width, modes), jnp.float32),
+            jax.ShapeDtypeStruct((1, width, modes), jnp.float32),
             jax.ShapeDtypeStruct((modes, width), jnp.bfloat16),
         ),
         in_specs=[VMEM] * 5,
         out_specs=(VMEM, VMEM),
         compiler_params=PARAMS,
-        cost_estimate=pl.CostEstimate(flops=400_000_000, bytes_accessed=3_000_000, transcendentals=0),
+        cost_estimate=pl.CostEstimate(flops=200_000_000, bytes_accessed=3_000_000, transcendentals=0),
     )(snapshots, weighted, edges, own_rows, rotation)
+
+
+def second_kernel(snap, weighted, edges, rotation_t, send):
+    at = (1 - lax.axis_index("core")) * (COMPONENTS // 2) + 1
+    send[0] = totals_of(modes_of(rotation_t[...], snap[at]), weighted.at[at], edges.at[at])
+
+
+def project_second(snapshots, weighted, edges, rotation_t):
+    _, _, width = snapshots.shape
+    return pl.pallas_call(
+        second_kernel,
+        out_shape=jax.ShapeDtypeStruct((1, width, rotation_t.shape[0]), jnp.float32),
+        in_specs=[VMEM] * 4,
+        out_specs=VMEM,
+        compiler_params=PARAMS,
+        cost_estimate=pl.CostEstimate(flops=200_000_000, bytes_accessed=2_000_000, transcendentals=0),
+    )(snapshots, weighted, edges, rotation_t)
 
 
 def kept_kernel(snap, weighted, edges, rotation_t, keep):
@@ -344,9 +359,11 @@
         edges = weigh_edges(begin, end, edge_scale, outer, inner)
     with jax.named_scope("projections"):
         send, rotation_t = project_sent(snapshots, weighted, edges, own_rows, other_pieces)
-        received = lax.ppermute(send, "core", swap)
+        received = [lax.ppermute(send, "core", swap)]
+        send = project_second(snapshots, weighted, edges, rotation_t)
+        received.append(lax.ppermute(send, "core", swap))
         keep = project_kept(snapshots, weighted, edges, rotation_t)
-        mine = keep + received
+        mine = keep + jnp.concatenate(received, axis=0)
     modes = mine.shape[2]
     members = lax.axis_size(PLANE_AXES)
     with jax.named_scope("sum_plane"):

time: 74.9 us -> 75.2 us (level)
    ppermute x1 -> x2, starting transfers between devices: 3.07 us -> 3.17 us  [the longest x1 3.07 us: on_device(): received.append(lax.ppermute(send, 'core', swap))]
  transfers between devices with their start and end apart: 6 -> 7, of which waited for: 3 -> 3; matrix products, arithmetic and copies ran while one was open for 0% -> 0% of each run, Pallas kernels for 5% -> 5%
where the time goes in v15:
time: 75.2 us; the launch traced here: 75 us
  blocking collectives  35.4 us (47%)
  starting transfers between devices  30.2 us (40%)
  Pallas kernels  7.66 us (10%)
  waiting for transfers between devices  1.41 us (2%)
    all_to_all x2, blocking collectives, spread(): lax.all_to_all(jnp.broadcast_to(block[None], (count,) + block.shape), axe...  22.6 us
    all_to_all x1, blocking collectives, on_device(): piece = jnp.sum(lax.all_to_all(pieces, PLANE_AXES, 0, 0), axis=0)  12.7 us
    all_to_all x1, starting transfers between devices, on_device(): own_pieces = lax.all_to_all(rows, SPREAD_AXES, 0, 0)  12 us
    ppermute x1, starting transfers between devices, on_device(): outer = lax.ppermute(outer, CELL_AXES, across)  8.31 us
    ppermute x1, starting transfers between devices, on_device(): other = lax.ppermute(mine, 'core', swap)  4.21 us
    ppermute x1, starting transfers between devices, on_device(): received.append(lax.ppermute(send, 'core', swap))  3.07 us
    ppermute x1, starting transfers between devices, on_device(): lax.ppermute(own_pieces, ('x_lo', 'x_hi'), [(i, 3 - i) for i in range(4)])  2.5 us
    pallas_call x1, Pallas kernels, weigh(): pl.pallas_call(weighting_kernel, out_shape=(jax.ShapeDtypeStruct(snapshot...  1.85 us
  transfers between devices with their start and end apart: 7, of which 3 were waited for; matrix products, arithmetic and copies ran while one was open for 0% of the time, Pallas kernels for 5%

profile of v15, /device:TPU:1, one launch (start us, length us, event | category | flops | bytes accessed | tf_op | source)
XLA Modules:
  0.0 75.0 jit_solution(16406744035005010167)
XLA Ops:
  0.0 0.0 copy-start
  0.0 0.0 copy-start.3
  0.0 0.0 copy-start.2
  0.0 0.0 copy-start.1
  0.0 1.5 %start.1 = (bf16[3,32,384]{2,1,0:T(8,128)(2,1)S(1)}, bf16[3,32,384]{2,1,0:T(8,128)(2,1)S(1)}, bf16[32,8,128]{2,1,0:T(8,128)(2,1)}) custom-call(bf16[4,960,384]{2,1,0:T(8,128)(2,1)} %snap.9, bf16[6,128]{1,0:T(8,128)(2,1)} %rot_hbm.1), custom_call_target="tpu_custom_call" | custom-call | bytes 100000000 | tf_op jit(solution)/shard_map/start/pallas_call | solution.py:67
  1.5 12.0 %all-to-all-start = ((bf16[32,8,128]{2,1,0:T(8,128)(2,1)}), bf16[32,8,128]{2,1,0:T(8,128)(2,1)S(1)}, u32[]{:S(2)}, u32[]{:S(2)}) async-start(bf16[32,8,128]{2,1,0:T(8,128)(2,1)} %get-tuple-element.15), calls=%async_computation | async-start | bytes 131072 | tf_op jit(solution)/shard_map/rotation_rows/all_to_all | solution.py:353
  13.6 8.3 %collective-permute-start = (bf16[3,32,384]{2,1,0:T(8,128)(2,1)S(1)}, bf16[3,32,384]{2,1,0:T(8,128)(2,1)S(1)}, u32[]{:S(2)}, u32[]{:S(2)}) collective-permute-start(bf16[3,32,384]{2,1,0:T(8,128)(2,1)S(1)} %get-tuple-element.20), channel_id=1, source_target_pairs={{0,255},{1,2},{2,1},{3,4},{4,3},{5,6},{6,5},{7,8},{8,7},{9,10},{10... | collective-permute-start | bytes 221192 | tf_op jit(solution)/shard_map/halo/ppermute | solution.py:350
  21.9 0.0 collective-permute-start.1
  21.9 0.5 all-to-all-done.rot
  22.4 2.5 %collective-permute-start.2 = (bf16[32,8,128]{2,1,0:T(8,128)(2,1)S(1)}, bf16[32,8,128]{2,1,0:T(8,128)(2,1)S(1)}, u32[]{:S(2)}, u32[]{:S(2)}) collective-permute-start(bf16[32,8,128]{2,1,0:T(8,128)(2,1)S(1)} %all-to-all-done.rot), channel_id=1, source_target_pairs={{0,160},{32,128},{128,32},{160,0},{1,161},{33,129},{129,33},{161,1... | collective-permute-start | bytes 196616 | tf_op jit(solution)/shard_map/rotation_rows/ppermute | solution.py:354
  24.9 0.0 copy-done
  24.9 0.0 copy-done.3
  24.9 0.0 copy-done.2
  24.9 0.0 copy-done.1
  24.9 1.9 %weighting.2 = (bf16[4,960,384]{2,1,0:T(8,128)(2,1)S(1)}, f32[64,8]{1,0:T(8,128)S(1)}, bf16[4,64,384]{2,1,0:T(8,128)(2,1)S(1)}, bf16[4,64,384]{2,1,0:T(8,128)(2,1)S(1)}, f32[192,128]{1,0:T(8,128)S(1)}) custom-call(bf16[4,960,384]{2,1,0:T(8,128)(2,1)S(1)} %copy-done, f32[1,960]{1,0:T(1,128)S(1)} %bitcast.7, f32[1,960]{1,0:T(1,128)S(1)} %bitcast.8, ...), custom_call_target="tpu_custom_call" | custom-call | flops 1000000000 | bytes 6000000 | tf_op jit(solution)/shard_map/weighting/pallas_call | solution.py:157
  26.8 0.0 collective-permute-done.outer
  26.8 0.0 collective-permute-done.1.inner
  26.8 0.3 weighting.3.edges
  27.1 0.0 collective-permute-done.2.rot
  27.1 0.8 %projections.3 = (f32[1,384,128]{2,1,0:T(8,128)S(1)}, bf16[128,384]{1,0:T(8,128)(2,1)S(1)}) custom-call(bf16[4,960,384]{2,1,0:T(8,128)(2,1)S(1)} %copy-done, bf16[4,960,384]{2,1,0:T(8,128)(2,1)S(1)} %get-tuple-element.16.weighted, bf16[4,64,384]{2,1,0:T(8,128)(2,1)S(1)} %weighting.3.edges, f32[192,128]{1,0:T(8,128)S(1)} %get-tuple-element.22.own_rows, ...), custom_call_target="tpu_custom_call" | custom-call | flops 200000000 | bytes 3000000 | tf_op jit(solution)/shard_map/projections/pallas_call | solution.py:245
  27.9 0.7 projections.5
  28.6 3.1 %collective-permute-start.4 = (f32[1,384,128]{2,1,0:T(8,128)S(1)}, f32[1,384,128]{2,1,0:T(8,128)S(1)}, u32[]{:S(2)}, u32[]{:S(2)}) collective-permute-start(f32[1,384,128]{2,1,0:T(8,128)S(1)} %projections.5), channel_id=1, source_target_pairs={{0,64},{64,0},{1,65},{65,1},{2,66},{66,2},{3,67},{67,3},{4,68},{68... | collective-permute-start | bytes 589832 | tf_op jit(solution)/shard_map/projections/ppermute | solution.py:364
  31.7 0.1 collective-permute-start.3
  31.8 1.1 %projections.4 = f32[2,384,128]{2,1,0:T(8,128)S(1)} custom-call(bf16[4,960,384]{2,1,0:T(8,128)(2,1)S(1)} %copy-done, bf16[4,960,384]{2,1,0:T(8,128)(2,1)S(1)} %get-tuple-element.16.weighted, bf16[4,64,384]{2,1,0:T(8,128)(2,1)S(1)} %weighting.3.edges, bf16[128,384]{1,0:T(8,128)(2,1)S(1)} %get-tuple-element.23.rotation_t), custom_call_target="tpu_custom_call" | custom-call | flops 400000000 | bytes 3000000 | tf_op jit(solution)/shard_map/projections/pallas_call | solution.py:286
  32.8 0.0 collective-permute-done.4
  32.8 0.3 collective-permute-done.3
  33.1 12.7 %all_to_all.20 = f32[16,48,128]{2,1,0:T(8,128)S(1)} all-to-all(f32[16,48,128]{2,1,0:T(8,128)S(1)} %bitcast.10), channel_id=1, replica_groups=mesh['x_lo'=2,'core'=2,'x_hi'=2,'z'=8,'y'=4] {'y','x_lo','x_hi'}, dimensions={0} | all-to-all | bytes 786432 | tf_op jit(solution)/shard_map/sum_plane/all_to_all | solution.py:371
  45.9 11.1 %all_to_all.21 = f32[8,48,128]{2,1,0:T(8,128)S(1)} all-to-all(f32[8,48,128]{2,1,0:T(8,128)S(1)} %broadcast_in_dim.4), channel_id=1, replica_groups=mesh['x_lo'=2,'core'=2,'x_hi'=2,'z'=8,'y'=4] {'z'}, dimensions={0} | all-to-all | bytes 393216 | tf_op jit(solution)/shard_map/sum_z/all_to_all | solution.py:338
  57.1 11.6 %all_to_all.22 = f32[16,48,128]{2,1,0:T(8,128)S(1)} all-to-all(f32[16,48,128]{2,1,0:T(8,128)S(1)} %broadcast_in_dim.5), channel_id=1, replica_groups=mesh['x_lo'=2,'core'=2,'x_hi'=2,'z'=8,'y'=4] {'y','x_lo','x_hi'}, dimensions={0} | all-to-all | bytes 786432 | tf_op jit(solution)/shard_map/share_plane/all_to_all | solution.py:338
  68.6 4.2 %collective-permute-start.5 = (f32[2,384,128]{2,1,0:T(8,128)S(1)}, f32[2,384,128]{2,1,0:T(8,128)S(1)}, u32[]{:S(2)}, u32[]{:S(2)}) collective-permute-start(f32[2,384,128]{2,1,0:T(8,128)S(1)} %bitcast.5), channel_id=1, source_target_pairs={{0,64},{64,0},{1,65},{65,1},{2,66},{66,2},{3,67},{67,3},{4,68},{68... | collective-permute-start | bytes 1179656 | tf_op jit(solution)/shard_map/share_core/ppermute | solution.py:378
  72.9 0.8 %share_core.2.begun = f32[4,384,128]{2,1,0:T(8,128)} custom-call(f32[2,384,128]{2,1,0:T(8,128)S(1)} %bitcast.6), custom_call_target="tpu_custom_call" | custom-call | bytes 1000000 | tf_op jit(solution)/shard_map/share_core/pallas_call | solution.py:312
  73.6 0.6 collective-permute-done.5.other
  74.2 0.8 %share_core.3 = f32[4,384,128]{2,1,0:T(8,128)} custom-call(f32[4,384,128]{2,1,0:T(8,128)} %share_core.2.begun, f32[2,384,128]{2,1,0:T(8,128)S(1)} %collective-permute-done.5.other), custom_call_target="tpu_custom_call", output_to_operand_aliasing={{}: (0, {})} | custom-call | bytes 1000000 | tf_op jit(solution)/shard_map/share_core/pallas_call | solution.py:324
  (6 shorter events, 0.1 us)
Async XLA Ops:
  0.0 24.9 %copy-start = (bf16[4,960,384]{2,1,0:T(8,128)(2,1)S(1)}, bf16[4,960,384]{2,1,0:T(8,128)(2,1)}, u32[]{:S(2)}) copy-start(bf16[4,960,384]{2,1,0:T(8,128)(2,1)} %snap.9) | copy-start | bytes 8847364
  0.0 24.9 %copy-start.3 = (s32[960]{0:T(1024)S(1)}, s32[960]{0:T(1024)}, u32[]{:S(2)}) copy-start(s32[960]{0:T(1024)} %param.8) | copy-start | bytes 11524
  0.0 24.9 %copy-start.2 = (f32[960]{0:T(1024)S(1)}, f32[960]{0:T(1024)}, u32[]{:S(2)}) copy-start(f32[960]{0:T(1024)} %param.7) | copy-start | bytes 11524
  0.0 24.9 %copy-start.1 = (f32[960]{0:T(1024)S(1)}, f32[960]{0:T(1024)}, u32[]{:S(2)}) copy-start(f32[960]{0:T(1024)} %param.6) | copy-start | bytes 11524
  1.5 20.9 %all-to-all-start = ((bf16[32,8,128]{2,1,0:T(8,128)(2,1)}), bf16[32,8,128]{2,1,0:T(8,128)(2,1)S(1)}, u32[]{:S(2)}, u32[]{:S(2)}) async-start(bf16[32,8,128]{2,1,0:T(8,128)(2,1)} %get-tuple-element.15), calls=%async_computation | async-start | bytes 131072 | tf_op jit(solution)/shard_map/rotation_rows/all_to_all | solution.py:353
  13.6 13.2 %collective-permute-start = (bf16[3,32,384]{2,1,0:T(8,128)(2,1)S(1)}, bf16[3,32,384]{2,1,0:T(8,128)(2,1)S(1)}, u32[]{:S(2)}, u32[]{:S(2)}) collective-permute-start(bf16[3,32,384]{2,1,0:T(8,128)(2,1)S(1)} %get-tuple-element.20), channel_id=1, source_target_pairs={{0,255},{1,2},{2,1},{3,4},{4,3},{5,6},{6,5},{7,8},{8,7},{9,10},{10... | collective-permute-start | bytes 221192 | tf_op jit(solution)/shard_map/halo/ppermute | solution.py:350
  21.9 4.9 %collective-permute-start.1 = (bf16[3,32,384]{2,1,0:T(8,128)(2,1)S(1)}, bf16[3,32,384]{2,1,0:T(8,128)(2,1)S(1)}, u32[]{:S(2)}, u32[]{:S(2)}) collective-permute-start(bf16[3,32,384]{2,1,0:T(8,128)(2,1)S(1)} %get-tuple-element.21), channel_id=1, source_target_pairs={{0,1},{1,0},{2,3},{3,2},{4,5},{5,4},{6,7},{7,6},{8,9},{9,8},{10,11... | collective-permute-start | bytes 221192 | tf_op jit(solution)/shard_map/halo/ppermute | solution.py:351
  22.4 4.7 %collective-permute-start.2 = (bf16[32,8,128]{2,1,0:T(8,128)(2,1)S(1)}, bf16[32,8,128]{2,1,0:T(8,128)(2,1)S(1)}, u32[]{:S(2)}, u32[]{:S(2)}) collective-permute-start(bf16[32,8,128]{2,1,0:T(8,128)(2,1)S(1)} %all-to-all-done.rot), channel_id=1, source_target_pairs={{0,160},{32,128},{128,32},{160,0},{1,161},{33,129},{129,33},{161,1... | collective-permute-start | bytes 196616 | tf_op jit(solution)/shard_map/rotation_rows/ppermute | solution.py:354
  28.6 4.2 %collective-permute-start.4 = (f32[1,384,128]{2,1,0:T(8,128)S(1)}, f32[1,384,128]{2,1,0:T(8,128)S(1)}, u32[]{:S(2)}, u32[]{:S(2)}) collective-permute-start(f32[1,384,128]{2,1,0:T(8,128)S(1)} %projections.5), channel_id=1, source_target_pairs={{0,64},{64,0},{1,65},{65,1},{2,66},{66,2},{3,67},{67,3},{4,68},{68... | collective-permute-start | bytes 589832 | tf_op jit(solution)/shard_map/projections/ppermute | solution.py:364
  31.7 1.4 %collective-permute-start.3 = (f32[1,384,128]{2,1,0:T(8,128)S(1)}, f32[1,384,128]{2,1,0:T(8,128)S(1)}, u32[]{:S(2)}, u32[]{:S(2)}) collective-permute-start(f32[1,384,128]{2,1,0:T(8,128)S(1)} %get-tuple-element.24), channel_id=1, source_target_pairs={{0,64},{64,0},{1,65},{65,1},{2,66},{66,2},{3,67},{67,3},{4,68},{68... | collective-permute-start | bytes 589832 | tf_op jit(solution)/shard_map/projections/ppermute | solution.py:362
  68.6 5.6 %collective-permute-start.5 = (f32[2,384,128]{2,1,0:T(8,128)S(1)}, f32[2,384,128]{2,1,0:T(8,128)S(1)}, u32[]{:S(2)}, u32[]{:S(2)}) collective-permute-start(f32[2,384,128]{2,1,0:T(8,128)S(1)} %bitcast.5), channel_id=1, source_target_pairs={{0,64},{64,0},{1,65},{65,1},{2,66},{66,2},{3,67},{67,3},{4,68},{68... | collective-permute-start | bytes 1179656 | tf_op jit(solution)/shard_map/share_core/ppermute | solution.py:378

commit v16 on v14

--- a/solution.py
+++ b/solution.py
@@ -17,7 +17,7 @@
 START_BYTES = 100_000_000
 TILE_AXES = ("x_hi", "z", "y")
 SPREAD_AXES = ("z", "y")
-PLANE_AXES = ("y", "x_lo", "x_hi")
+PLANE_AXES = ("x_hi", "x_lo", "y")
 CELL_AXES = ("x_lo", "core", "x_hi", "z", "y")
 VMEM = pl.BlockSpec(memory_space=pltpu.VMEM)
 HBM = pl.BlockSpec(memory_space=pltpu.HBM)

time: 74.9 us -> 75.5 us (level)
    all_to_all x1, blocking collectives: 12.6 us -> 13.7 us  [on_device(): piece = jnp.sum(lax.all_to_all(pieces, PLANE_AXES, 0, 0), axis=0)]
where the time goes in v16:
time: 75.5 us; the launch traced here: 75.2 us
  blocking collectives  35.9 us (48%)
  starting transfers between devices  30.2 us (40%)
  Pallas kernels  7.43 us (10%)
  waiting for transfers between devices  1.42 us (2%)
    all_to_all x2, blocking collectives, spread(): lax.all_to_all(jnp.broadcast_to(block[None], (count,) + block.shape), axe...  22.2 us
    all_to_all x1, blocking collectives, on_device(): piece = jnp.sum(lax.all_to_all(pieces, PLANE_AXES, 0, 0), axis=0)  13.7 us
    all_to_all x1, starting transfers between devices, on_device(): own_pieces = lax.all_to_all(rows, SPREAD_AXES, 0, 0)  12 us
    ppermute x1, starting transfers between devices, on_device(): outer = lax.ppermute(outer, CELL_AXES, across)  8.31 us
    ppermute x1, starting transfers between devices, on_device(): other = lax.ppermute(mine, 'core', swap)  4.3 us
    ppermute x1, starting transfers between devices, on_device(): received = lax.ppermute(send, 'core', swap)  3.07 us
    ppermute x1, starting transfers between devices, on_device(): lax.ppermute(own_pieces, ('x_lo', 'x_hi'), [(i, 3 - i) for i in range(4)])  2.5 us
    pallas_call x1, Pallas kernels, weigh(): pl.pallas_call(weighting_kernel, out_shape=(jax.ShapeDtypeStruct(snapshot...  1.85 us
  transfers between devices with their start and end apart: 6, of which 3 were waited for; matrix products, arithmetic and copies ran while one was open for 0% of the time, Pallas kernels for 5%

profile of v16, /device:TPU:1, one launch (start us, length us, event | category | flops | bytes accessed | tf_op | source)
XLA Modules:
  0.0 75.2 jit_solution(10431009348487615772)
XLA Ops:
  0.0 0.0 copy-start
  0.0 0.0 copy-start.3
  0.0 0.0 copy-start.2
  0.0 0.0 copy-start.1
  0.0 1.5 %start.1 = (bf16[3,32,384]{2,1,0:T(8,128)(2,1)S(1)}, bf16[3,32,384]{2,1,0:T(8,128)(2,1)S(1)}, bf16[32,8,128]{2,1,0:T(8,128)(2,1)}) custom-call(bf16[4,960,384]{2,1,0:T(8,128)(2,1)} %snap.7, bf16[6,128]{1,0:T(8,128)(2,1)} %rot_hbm.1), custom_call_target="tpu_custom_call" | custom-call | bytes 100000000 | tf_op jit(solution)/shard_map/start/pallas_call | solution.py:67
  1.5 12.0 %all-to-all-start = ((bf16[32,8,128]{2,1,0:T(8,128)(2,1)}), bf16[32,8,128]{2,1,0:T(8,128)(2,1)S(1)}, u32[]{:S(2)}, u32[]{:S(2)}) async-start(bf16[32,8,128]{2,1,0:T(8,128)(2,1)} %get-tuple-element.15), calls=%async_computation | async-start | bytes 131072 | tf_op jit(solution)/shard_map/rotation_rows/all_to_all | solution.py:338
  13.6 8.3 %collective-permute-start = (bf16[3,32,384]{2,1,0:T(8,128)(2,1)S(1)}, bf16[3,32,384]{2,1,0:T(8,128)(2,1)S(1)}, u32[]{:S(2)}, u32[]{:S(2)}) collective-permute-start(bf16[3,32,384]{2,1,0:T(8,128)(2,1)S(1)} %get-tuple-element.20), channel_id=1, source_target_pairs={{0,255},{1,2},{2,1},{3,4},{4,3},{5,6},{6,5},{7,8},{8,7},{9,10},{10... | collective-permute-start | bytes 221192 | tf_op jit(solution)/shard_map/halo/ppermute | solution.py:335
  21.9 0.0 collective-permute-start.1
  21.9 0.5 all-to-all-done.rot
  22.4 2.5 %collective-permute-start.2 = (bf16[32,8,128]{2,1,0:T(8,128)(2,1)S(1)}, bf16[32,8,128]{2,1,0:T(8,128)(2,1)S(1)}, u32[]{:S(2)}, u32[]{:S(2)}) collective-permute-start(bf16[32,8,128]{2,1,0:T(8,128)(2,1)S(1)} %all-to-all-done.rot), channel_id=1, source_target_pairs={{0,160},{32,128},{128,32},{160,0},{1,161},{33,129},{129,33},{161,1... | collective-permute-start | bytes 196616 | tf_op jit(solution)/shard_map/rotation_rows/ppermute | solution.py:339
  24.9 0.0 copy-done
  24.9 0.0 copy-done.3
  24.9 0.0 copy-done.2
  24.9 0.0 copy-done.1
  24.9 1.9 %weighting.2 = (bf16[4,960,384]{2,1,0:T(8,128)(2,1)S(1)}, f32[64,8]{1,0:T(8,128)S(1)}, bf16[4,64,384]{2,1,0:T(8,128)(2,1)S(1)}, bf16[4,64,384]{2,1,0:T(8,128)(2,1)S(1)}, f32[192,128]{1,0:T(8,128)S(1)}) custom-call(bf16[4,960,384]{2,1,0:T(8,128)(2,1)S(1)} %copy-done, f32[1,960]{1,0:T(1,128)S(1)} %bitcast.7, f32[1,960]{1,0:T(1,128)S(1)} %bitcast.8, ...), custom_call_target="tpu_custom_call" | custom-call | flops 1000000000 | bytes 6000000 | tf_op jit(solution)/shard_map/weighting/pallas_call | solution.py:157
  26.8 0.0 collective-permute-done.outer
  26.8 0.0 collective-permute-done.1.inner
  26.8 0.3 weighting.3.edges
  27.1 0.0 collective-permute-done.2.rot
  27.1 1.2 %projections.2 = (f32[2,384,128]{2,1,0:T(8,128)S(1)}, bf16[128,384]{1,0:T(8,128)(2,1)S(1)}) custom-call(bf16[4,960,384]{2,1,0:T(8,128)(2,1)S(1)} %copy-done, bf16[4,960,384]{2,1,0:T(8,128)(2,1)S(1)} %get-tuple-element.16.weighted, bf16[4,64,384]{2,1,0:T(8,128)(2,1)S(1)} %weighting.3.edges, f32[192,128]{1,0:T(8,128)S(1)} %get-tuple-element.22.own_rows, ...), custom_call_target="tpu_custom_call" | custom-call | flops 400000000 | bytes 3000000 | tf_op jit(solution)/shard_map/projections/pallas_call | solution.py:247
  28.3 3.1 %collective-permute-start.3 = (f32[2,384,128]{2,1,0:T(8,128)S(1)}, f32[2,384,128]{2,1,0:T(8,128)S(1)}, u32[]{:S(2)}, u32[]{:S(2)}) collective-permute-start(f32[2,384,128]{2,1,0:T(8,128)S(1)} %get-tuple-element.24), channel_id=1, source_target_pairs={{0,64},{64,0},{1,65},{65,1},{2,66},{66,2},{3,67},{67,3},{4,68},{68... | collective-permute-start | bytes 1179656 | tf_op jit(solution)/shard_map/projections/ppermute | solution.py:347
  31.4 1.1 %projections.3 = f32[2,384,128]{2,1,0:T(8,128)S(1)} custom-call(bf16[4,960,384]{2,1,0:T(8,128)(2,1)S(1)} %copy-done, bf16[4,960,384]{2,1,0:T(8,128)(2,1)S(1)} %get-tuple-element.16.weighted, bf16[4,64,384]{2,1,0:T(8,128)(2,1)S(1)} %weighting.3.edges, bf16[128,384]{1,0:T(8,128)(2,1)S(1)} %get-tuple-element.23.rotation_t), custom_call_target="tpu_custom_call" | custom-call | flops 400000000 | bytes 3000000 | tf_op jit(solution)/shard_map/projections/pallas_call | solution.py:271
  32.5 0.3 collective-permute-done.3
  32.8 13.7 %all_to_all.20 = f32[16,48,128]{2,1,0:T(8,128)S(1)} all-to-all(f32[16,48,128]{2,1,0:T(8,128)S(1)} %bitcast.10), channel_id=1, replica_groups=mesh['x_lo'=2,'core'=2,'x_hi'=2,'z'=8,'y'=4] {'x_hi','x_lo','y'}, dimensions={0} | all-to-all | bytes 786432 | tf_op jit(solution)/shard_map/sum_plane/all_to_all | solution.py:354
  46.6 10.9 %all_to_all.21 = f32[8,48,128]{2,1,0:T(8,128)S(1)} all-to-all(f32[8,48,128]{2,1,0:T(8,128)S(1)} %broadcast_in_dim.4), channel_id=1, replica_groups=mesh['x_lo'=2,'core'=2,'x_hi'=2,'z'=8,'y'=4] {'z'}, dimensions={0} | all-to-all | bytes 393216 | tf_op jit(solution)/shard_map/sum_z/all_to_all | solution.py:323
  57.5 11.3 %all_to_all.22 = f32[16,48,128]{2,1,0:T(8,128)S(1)} all-to-all(f32[16,48,128]{2,1,0:T(8,128)S(1)} %broadcast_in_dim.5), channel_id=1, replica_groups=mesh['x_lo'=2,'core'=2,'x_hi'=2,'z'=8,'y'=4] {'x_hi','x_lo','y'}, dimensions={0} | all-to-all | bytes 786432 | tf_op jit(solution)/shard_map/share_plane/all_to_all | solution.py:323
  68.8 4.3 %collective-permute-start.4 = (f32[2,384,128]{2,1,0:T(8,128)S(1)}, f32[2,384,128]{2,1,0:T(8,128)S(1)}, u32[]{:S(2)}, u32[]{:S(2)}) collective-permute-start(f32[2,384,128]{2,1,0:T(8,128)S(1)} %bitcast.5), channel_id=1, source_target_pairs={{0,64},{64,0},{1,65},{65,1},{2,66},{66,2},{3,67},{67,3},{4,68},{68... | collective-permute-start | bytes 1179656 | tf_op jit(solution)/shard_map/share_core/ppermute | solution.py:361
  73.1 0.8 %share_core.2.begun = f32[4,384,128]{2,1,0:T(8,128)} custom-call(f32[2,384,128]{2,1,0:T(8,128)S(1)} %bitcast.6), custom_call_target="tpu_custom_call" | custom-call | bytes 1000000 | tf_op jit(solution)/shard_map/share_core/pallas_call | solution.py:297
  73.9 0.6 collective-permute-done.4.other
  74.5 0.8 %share_core.3 = f32[4,384,128]{2,1,0:T(8,128)} custom-call(f32[4,384,128]{2,1,0:T(8,128)} %share_core.2.begun, f32[2,384,128]{2,1,0:T(8,128)S(1)} %collective-permute-done.4.other), custom_call_target="tpu_custom_call", output_to_operand_aliasing={{}: (0, {})} | custom-call | bytes 1000000 | tf_op jit(solution)/shard_map/share_core/pallas_call | solution.py:309
  (6 shorter events, 0.1 us)
Async XLA Ops:
  0.0 24.9 %copy-start = (bf16[4,960,384]{2,1,0:T(8,128)(2,1)S(1)}, bf16[4,960,384]{2,1,0:T(8,128)(2,1)}, u32[]{:S(2)}) copy-start(bf16[4,960,384]{2,1,0:T(8,128)(2,1)} %snap.7) | copy-start | bytes 8847364
  0.0 24.9 %copy-start.3 = (s32[960]{0:T(1024)S(1)}, s32[960]{0:T(1024)}, u32[]{:S(2)}) copy-start(s32[960]{0:T(1024)} %param.8) | copy-start | bytes 11524
  0.0 24.9 %copy-start.2 = (f32[960]{0:T(1024)S(1)}, f32[960]{0:T(1024)}, u32[]{:S(2)}) copy-start(f32[960]{0:T(1024)} %param.7) | copy-start | bytes 11524
  0.0 24.9 %copy-start.1 = (f32[960]{0:T(1024)S(1)}, f32[960]{0:T(1024)}, u32[]{:S(2)}) copy-start(f32[960]{0:T(1024)} %param.6) | copy-start | bytes 11524
  1.5 20.9 %all-to-all-start = ((bf16[32,8,128]{2,1,0:T(8,128)(2,1)}), bf16[32,8,128]{2,1,0:T(8,128)(2,1)S(1)}, u32[]{:S(2)}, u32[]{:S(2)}) async-start(bf16[32,8,128]{2,1,0:T(8,128)(2,1)} %get-tuple-element.15), calls=%async_computation | async-start | bytes 131072 | tf_op jit(solution)/shard_map/rotation_rows/all_to_all | solution.py:338
  13.6 13.2 %collective-permute-start = (bf16[3,32,384]{2,1,0:T(8,128)(2,1)S(1)}, bf16[3,32,384]{2,1,0:T(8,128)(2,1)S(1)}, u32[]{:S(2)}, u32[]{:S(2)}) collective-permute-start(bf16[3,32,384]{2,1,0:T(8,128)(2,1)S(1)} %get-tuple-element.20), channel_id=1, source_target_pairs={{0,255},{1,2},{2,1},{3,4},{4,3},{5,6},{6,5},{7,8},{8,7},{9,10},{10... | collective-permute-start | bytes 221192 | tf_op jit(solution)/shard_map/halo/ppermute | solution.py:335
  21.9 4.9 %collective-permute-start.1 = (bf16[3,32,384]{2,1,0:T(8,128)(2,1)S(1)}, bf16[3,32,384]{2,1,0:T(8,128)(2,1)S(1)}, u32[]{:S(2)}, u32[]{:S(2)}) collective-permute-start(bf16[3,32,384]{2,1,0:T(8,128)(2,1)S(1)} %get-tuple-element.21), channel_id=1, source_target_pairs={{0,1},{1,0},{2,3},{3,2},{4,5},{5,4},{6,7},{7,6},{8,9},{9,8},{10,11... | collective-permute-start | bytes 221192 | tf_op jit(solution)/shard_map/halo/ppermute | solution.py:336
  22.4 4.7 %collective-permute-start.2 = (bf16[32,8,128]{2,1,0:T(8,128)(2,1)S(1)}, bf16[32,8,128]{2,1,0:T(8,128)(2,1)S(1)}, u32[]{:S(2)}, u32[]{:S(2)}) collective-permute-start(bf16[32,8,128]{2,1,0:T(8,128)(2,1)S(1)} %all-to-all-done.rot), channel_id=1, source_target_pairs={{0,160},{32,128},{128,32},{160,0},{1,161},{33,129},{129,33},{161,1... | collective-permute-start | bytes 196616 | tf_op jit(solution)/shard_map/rotation_rows/ppermute | solution.py:339
  28.3 4.4 %collective-permute-start.3 = (f32[2,384,128]{2,1,0:T(8,128)S(1)}, f32[2,384,128]{2,1,0:T(8,128)S(1)}, u32[]{:S(2)}, u32[]{:S(2)}) collective-permute-start(f32[2,384,128]{2,1,0:T(8,128)S(1)} %get-tuple-element.24), channel_id=1, source_target_pairs={{0,64},{64,0},{1,65},{65,1},{2,66},{66,2},{3,67},{67,3},{4,68},{68... | collective-permute-start | bytes 1179656 | tf_op jit(solution)/shard_map/projections/ppermute | solution.py:347
  68.8 5.7 %collective-permute-start.4 = (f32[2,384,128]{2,1,0:T(8,128)S(1)}, f32[2,384,128]{2,1,0:T(8,128)S(1)}, u32[]{:S(2)}, u32[]{:S(2)}) collective-permute-start(f32[2,384,128]{2,1,0:T(8,128)S(1)} %bitcast.5), channel_id=1, source_target_pairs={{0,64},{64,0},{1,65},{65,1},{2,66},{66,2},{3,67},{67,3},{4,68},{68... | collective-permute-start | bytes 1179656 | tf_op jit(solution)/shard_map/share_core/ppermute | solution.py:361
